TPU v7x, 32 devices: a whole 2x2x4 slice. The times are simulated.
32 devices in a mesh: rep: 4 (over y, x), tp: 8 (over z, core).
Axes of the slice: x: 2, y: 2, z: 4, core: 2. Of those that a mesh axis runs over, the one named last changes fastest.
Arguments:
- inputs: bfloat16 [2, 2048, 8192], P(None, 'rep', 'tp'), may hold values from -6 to 6
- targets: bfloat16 [2, 2048, 2048], P(None, 'rep', 'tp'), may hold values from -6 to 6
- weight: bfloat16 [8192, 2048], P('tp'), may hold values from -0.0625 to 0.0625
- momentum: float32 [4, 8192, 2048], P('rep', 'tp'), may hold values from -0.8 to 0.8
- indices: int32 [2, 4, 64, 16, 2], P(None, None, 'tp'), may hold values from 0 to 127, as said below
Outputs:
- new_weight: bfloat16 [8192, 2048], P('tp')
- new_momentum: float32 [4, 8192, 2048], P('rep', 'tp')
Inputs may be any that keep to these rules, and one draw needn't show every extreme that they name: `indices`: the 2 entries of each block's list are distinct rows of the block's transform.
All inputs are finite; a program needn't handle non-finite values.
Results may differ from a plain program's by a relative error of at most 0.0085.
Values may be sent and summed in bfloat16 or wider, within the bound.
No kernel may reach another device: no remote copies, remote signals or barrier semaphores. Data moves between devices by JAX's collectives and lax.ppermute only.
A program may use at most 128 MiB of HBM per device.

v0:
```python
import functools

import jax
import jax.numpy as jnp
import numpy as np
from jax import lax
from jax.experimental import pallas as pl
from jax.experimental.pallas import tpu as pltpu
from jax.sharding import PartitionSpec as P


BLOCK = 128
STEPS = 2
CORES = 2
BF = jnp.bfloat16
F32 = jnp.float32


def dct_table(size):
    rows = np.arange(size, dtype=np.float64)[:, None]
    cols = np.arange(size, dtype=np.float64)[None, :]
    scale = np.where(rows == 0, np.sqrt(1.0 / size), np.sqrt(2.0 / size))
    return (scale * np.cos(np.pi * (2.0 * cols + 1.0) * rows / (2.0 * size))).astype(np.float32)


def swap(value, axis, size, mask):
    return lax.ppermute(value, axis, [(at, at ^ mask) for at in range(size)])


def dot(left, right):
    return lax.dot_general(left, right, (((1,), (0,)), ((), ())), preferred_element_type=F32)


def room(mib):
    return pltpu.CompilerParams(vmem_limit_bytes=mib << 20)


def cost(flops, moved):
    return pl.CostEstimate(flops=int(flops), bytes_accessed=int(moved), transcendentals=0)


def shaped(shape, dtype):
    return jax.ShapeDtypeStruct(shape, dtype)


def call(kernel, grid, ins, outs, mib, work, place, aliased=None):
    alias = {}
    arrays = [array for array, _, _ in ins]
    specs = [pl.BlockSpec(block, index) for _, block, index in ins]
    if aliased is not None:
        arrays.append(aliased)
        specs.append(pl.BlockSpec(memory_space=pl.ANY))
        alias = {len(arrays): 0}
    return pl.pallas_call(
        kernel,
        grid_spec=pltpu.PrefetchScalarGridSpec(
            num_scalar_prefetch=1,
            grid=(grid,),
            in_specs=specs,
            out_specs=[pl.BlockSpec(block, index) for _, block, index in outs],
        ),
        out_shape=[shape for shape, _, _ in outs],
        input_output_aliases=alias,
        compiler_params=room(mib),
        cost_estimate=cost(*work),
    )(place, *arrays)


def row_mask(rows, lanes, per, count, wanted, axis):
    return lax.broadcasted_iota(jnp.int32, (rows, lanes), axis) // per % count == wanted


def spread_rows(kept, nbr, per):
    kept = kept.astype(F32)
    return jnp.concatenate(
        [jnp.where(row_mask(*kept.shape, per, nbr, a, 0), kept, 0.0) for a in range(nbr)], axis=1
    ).astype(BF)


def spread_cols(basis, nbr, per):
    basis = basis.astype(F32)
    return jnp.concatenate(
        [jnp.where(row_mask(*basis.shape, per, nbr, a, 1), basis, 0.0) for a in range(nbr)], axis=0
    ).astype(BF)


def widen(coef, blocks):
    return jnp.concatenate(
        [jnp.where(row_mask(*coef.shape, 2, blocks, q, 0), coef, 0.0) for q in range(blocks)],
        axis=1,
    )


def narrow(wide, blocks):
    rows = wide.shape[0]
    return functools.reduce(
        jnp.add,
        [
            jnp.where(
                row_mask(rows, BLOCK, 2, blocks, q, 0), wide[:, q * BLOCK : (q + 1) * BLOCK], 0.0
            )
            for q in range(blocks)
        ],
    )


def fold(pair):
    half = pair.shape[0] // 2
    return pair[:half] + pair[half:]


def prep_kernel(place, all_ref, own_ref, cols_ref, rows_ref, dec_ref, own_dec_ref, kept_ref):
    wide = cols_ref.shape[1]

    def one_hot(picks):
        at = lax.broadcasted_iota(jnp.int32, (wide, picks.shape[-1]), 0)
        return (at == picks).astype(F32).astype(BF)

    dec_ref[0] = dot(cols_ref[...], one_hot(all_ref[0])).astype(BF)
    own = one_hot(own_ref[0])
    own_dec_ref[0] = dot(cols_ref[...], own).astype(BF)
    part = own.shape[1] // 3 * 2
    kept_ref[0] = lax.dot_general(
        own[:, :part], rows_ref[...], (((0,), (0,)), ((), ())), preferred_element_type=F32
    ).astype(BF)


def prep(place, picks_all, picks_own):
    tiles, _, width = picks_all.shape
    own = picks_own.shape[2]
    part = own // 3 * 2
    table = dct_table(BLOCK)
    high = np.asarray(table.astype(BF))
    low = np.asarray((table - high.astype(np.float32)).astype(BF))
    rows = jnp.asarray(np.concatenate([high, low], axis=0))
    cols = jnp.asarray(np.ascontiguousarray(np.concatenate([high, low], axis=0).T))
    each = lambda q, p: (q, 0, 0)
    once = lambda q, p: (0, 0)
    return call(
        prep_kernel,
        tiles,
        [
            (picks_all, (1, 1, width), each),
            (picks_own, (1, 1, own), each),
            (cols, cols.shape, once),
            (rows, rows.shape, once),
        ],
        [
            (shaped((tiles, BLOCK, width), BF), (1, BLOCK, width), each),
            (shaped((tiles, BLOCK, own), BF), (1, BLOCK, own), each),
            (shaped((tiles, part, BLOCK), BF), (1, part, BLOCK), each),
        ],
        4,
        (2 * tiles * 256 * 128 * (width + 2 * own), 2 << 20),
        place,
    )


def project_kernel(nbr, per, place, kept_ref, x_ref, out_ref, xt_ref):
    tiles = kept_ref.shape[0]
    xt_ref[...] = x_ref[0].T
    left = jnp.concatenate([spread_rows(kept_ref[q], nbr, per) for q in range(tiles)], axis=0)
    both = dot(left, xt_ref[...])
    pair = kept_ref.shape[1]
    for q in range(tiles):
        value = fold(both[q * pair : (q + 1) * pair])
        high = value.astype(BF)
        out_ref[q] = jnp.concatenate(
            [high.astype(F32), value - high.astype(F32)], axis=0
        ).astype(BF)


def project(place, kept, acts, step, nbr, per):
    tiles, pair, _ = kept.shape
    _, tokens, rows = acts.shape
    return call(
        functools.partial(project_kernel, nbr, per),
        1,
        [
            (kept, kept.shape, lambda j, p: (0, 0, 0)),
            (acts, (1, tokens, rows), lambda j, p: (step, 0, 0)),
        ],
        [
            (shaped((tiles, pair, tokens), BF), (tiles, pair, tokens), lambda j, p: (0, 0, 0)),
            (shaped((rows, tokens), BF), (rows, tokens), lambda j, p: (0, 0)),
        ],
        14,
        (2 * tiles * pair * rows * tokens, 4 * rows * tokens),
        place,
    )


def keep_rows(kept, moment, nbr, per, blocks):
    return narrow(fold(dot(spread_rows(kept, nbr, per), moment.astype(BF))), blocks)


def moment_rows_kernel(nbr, per, place, kept_ref, m_ref, out_ref):
    out_ref[0] = keep_rows(kept_ref[0], m_ref[0], nbr, per, m_ref.shape[2] // BLOCK)


def moment_rows(place, kept, momentum, tile, per):
    tiles, pair, _ = kept.shape
    rows = momentum.shape[1]
    return call(
        functools.partial(moment_rows_kernel, rows // BLOCK, per),
        tiles,
        [
            (kept, (1, pair, BLOCK), lambda j, p: (j, 0, 0)),
            (momentum, (1, rows, tile), lambda j, p: (0, 0, j ^ p[0])),
        ],
        [(shaped((tiles, pair // 2, BLOCK), F32), (1, pair // 2, BLOCK), lambda j, p: (j, 0, 0))],
        8,
        (2 * tiles * pair * rows * tile, 4 * rows * tile * tiles),
        place,
    )[0]


def coef_kernel(scale, place, proj_ref, old_ref, *refs):
    *e_refs, exact_ref, sent_ref = refs
    blocks = e_refs[0].shape[1] // BLOCK
    for q, e_ref in enumerate(e_refs):
        value = 0.9 * old_ref[q] + scale * narrow(fold(dot(proj_ref[q], e_ref[...])), blocks)
        exact_ref[q] = value
        sent_ref[q] = value.astype(BF)


def coefficients(place, proj, errors, old):
    tiles = len(errors)
    tokens, tile = errors[0].shape
    pair = proj.shape[1]
    shape = (tiles, pair // 2, BLOCK)
    whole = lambda j, p: (0, 0, 0)
    return call(
        functools.partial(coef_kernel, 1.0 / tokens),
        1,
        [(proj, (tiles, pair, tokens), whole), (old, shape, whole)]
        + [(piece, piece.shape, lambda j, p: (0, 0)) for piece in errors],
        [(shaped(shape, F32), shape, whole), (shaped(shape, BF), shape, whole)],
        8,
        (2 * tiles * pair * tokens * tile, 2 * tiles * tokens * tile),
        place,
    )


def momentum_kernel(scale, nbr, per, follow, place, xt_ref, e_ref, m_ref, dec_ref, coef_ref, *refs):
    refs = list(refs)
    kept_ref = refs.pop(0) if follow else None
    if len(refs) == 2 and not follow:
        refs.pop(0)
    coef = widen(coef_ref[0], m_ref.shape[2] // BLOCK)
    high = coef.astype(BF).astype(F32)
    back = jnp.concatenate([high, high, coef - high], axis=0).astype(BF)
    new = 0.9 * m_ref[0] + (
        dot(xt_ref[...], e_ref[0]) * scale - dot(spread_cols(dec_ref[0], nbr, per), back)
    )
    refs[0][0] = new
    if follow:
        refs[1][0] = keep_rows(kept_ref[0], new, nbr, per, new.shape[1] // BLOCK)


def momentum_step(place, acts_t, errors, moment, own_dec, coef, per, start, kept_next, total, previous):
    rows, tokens = acts_t.shape
    tiles, _, tile = errors.shape
    nbr = rows // BLOCK
    follow = kept_next is not None
    each = lambda j, p: (start + j, 0, 0)
    here = lambda j, p: (j, 0, 0)
    natural = lambda j, p: (0, 0, (start + j) ^ p[0])
    ins = [
        (acts_t, acts_t.shape, lambda j, p: (0, 0)),
        (errors, (1, tokens, tile), here),
        (moment, (1, rows, tile), natural if moment.shape[0] == 1 else each),
        (own_dec, (1,) + own_dec.shape[1:], each),
        (coef, (1,) + coef.shape[1:], each),
    ]
    outs = []
    if follow:
        ins.append((kept_next, (1,) + kept_next.shape[1:], each))
        outs.append((shaped((tiles, rows, tile), F32), (1, rows, tile), here))
        outs.append((shaped(coef.shape, F32), (1,) + coef.shape[1:], here))
    else:
        outs.append((shaped((1, rows, total), F32), (1, rows, tile), natural))
    return call(
        functools.partial(momentum_kernel, 1.0 / tokens, nbr, per, follow),
        tiles,
        ins,
        outs,
        14,
        (2 * rows * tokens * tile * tiles, 8 * rows * tile * tiles),
        place,
        previous,
    )


def changed(weight, dec_ref, coef_refs, nbr, per):
    blocks = weight.shape[1] // BLOCK
    parts = []
    for coef_ref in coef_refs:
        parts += [widen(coef_ref[0].astype(F32), blocks)] * 2
    change = dot(spread_cols(dec_ref[0], nbr, per), jnp.concatenate(parts, axis=0).astype(BF))
    return (weight.astype(F32) - 0.1 * change).astype(BF)


def first_kernel(start, core, place, w_ref, x_ref, out_ref, w_buf, x_buf, sum_ref, sems):
    count, rows, tile = w_buf.shape
    step = x_buf.shape[2]
    copies = []
    for k in range(rows // step):
        span = slice(k * step, (k + 1) * step)
        copies.append([pltpu.make_async_copy(x_ref.at[0, :, span], x_buf.at[k], sems.at[k, count])])
        for at in range(count):
            column = ((CORES * (start + at) + core) ^ place[0]) * tile
            source = w_ref.at[span, pl.ds(pl.multiple_of(column, tile), tile)]
            target = w_buf.at[at, span, :]
            copies[k].append(pltpu.make_async_copy(source, target, sems.at[k, at]))
    for group in copies:
        for copy in group:
            copy.start()
    for k, group in enumerate(copies):
        group[0].wait()
        for at in range(count):
            group[at + 1].wait()
            part = dot(x_buf[k], w_buf[at, k * step : (k + 1) * step, :])
            if k > 0:
                part = part + sum_ref[at]
            if k < len(copies) - 1:
                sum_ref[at] = part
            else:
                out_ref[at] = part.astype(BF)


def first(place, weight, acts, tile, start, core, count):
    rows = weight.shape[0]
    tokens = acts.shape[1]
    step = 256
    return pl.pallas_call(
        functools.partial(first_kernel, start, core),
        grid_spec=pltpu.PrefetchScalarGridSpec(
            num_scalar_prefetch=1,
            grid=(1,),
            in_specs=[pl.BlockSpec(memory_space=pltpu.HBM)] * 2,
            out_specs=pl.BlockSpec((count, tokens, tile), lambda j, p: (0, 0, 0)),
            scratch_shapes=[
                pltpu.VMEM((count, rows, tile), BF),
                pltpu.VMEM((rows // step, tokens, step), BF),
                pltpu.VMEM((count, tokens, tile), F32),
                pltpu.SemaphoreType.DMA((rows // step, count + 1)),
            ],
        ),
        out_shape=shaped((count, tokens, tile), BF),
        compiler_params=room(52),
        cost_estimate=cost(2 * tokens * rows * tile * count, 2 * rows * (tile * count + tokens)),
        name="first",
    )(place, weight, acts)


def next_kernel(nbr, per, place, w_ref, x_ref, dec_ref, *refs):
    *coef_refs, new_ref, out_ref = refs
    new = changed(w_ref[...], dec_ref, coef_refs, nbr, per)
    new_ref[0] = new
    out_ref[0] = dot(x_ref[0], new).astype(BF)


def forward(place, weight, acts, step, tile, per, start, core, count, basis, coefs):
    rows = weight.shape[0]
    tokens = acts.shape[1]
    at = lambda j: CORES * (start + j) + core
    ins = [
        (weight, (rows, tile), lambda j, p: (0, at(j) ^ p[0])),
        (acts, (1, tokens, rows), lambda j, p: (step, 0, 0)),
        (basis, (1,) + basis.shape[1:], lambda j, p: (at(j), 0, 0)),
    ]
    for coef in coefs:
        ins.append((coef, (1,) + coef.shape[1:], lambda j, p: (at(j), 0, 0)))
    product = (shaped((count, tokens, tile), BF), (1, tokens, tile), lambda j, p: (j, 0, 0))
    new = (shaped((count, rows, tile), BF), (1, rows, tile), lambda j, p: (j, 0, 0))
    return call(
        functools.partial(next_kernel, rows // BLOCK, per),
        count,
        ins,
        [new, product],
        12,
        (2 * tokens * rows * tile * count, 2 * rows * tile * count + 2 * tokens * rows),
        place,
    )


def finish_kernel(nbr, per, reps, place, keep_ref, send_ref, dec_ref, *refs):
    here = pl.program_id(0) % CORES == 0

    @pl.when(here)
    def _():
        refs[-1][...] = changed(keep_ref[0], dec_ref, refs[:reps], nbr, per)

    @pl.when(jnp.logical_not(here))
    def _():
        refs[-1][...] = changed(send_ref[0], dec_ref, refs[:reps], nbr, per)


def finish(place, keep, send, basis, coefs, per, start, total, previous):
    count, rows, tile = keep.shape
    each = lambda j, p: (j // CORES, 0, 0)
    return call(
        functools.partial(finish_kernel, rows // BLOCK, per, len(coefs)),
        count * CORES,
        [
            (keep, (1, rows, tile), each),
            (send, (1, rows, tile), each),
            (basis, (1,) + basis.shape[1:], lambda j, p: (CORES * start + j, 0, 0)),
        ]
        + [(coef, (1,) + coef.shape[1:], lambda j, p: (CORES * start + j, 0, 0)) for coef in coefs],
        [(shaped((rows, total), BF), (rows, tile), lambda j, p: (0, (CORES * start + j) ^ p[0]))],
        12,
        (2 * rows * 256 * tile * count * CORES, 4 * rows * tile * count * CORES),
        place,
        previous,
    )[0]


def by_distance(value, axes, index):
    for place, axis in enumerate(reversed(axes)):
        value = jnp.where((index >> place & 1) == 1, jnp.flip(value, axis), value)
    return value


def pick_tables(indices, step, reps, parts, replica, tp):
    nbr, nbc = indices.shape[2], indices.shape[3]
    per = nbc // parts * 2
    rep_bits, tp_bits = reps.bit_length() - 1, parts.bit_length() - 1
    picks = indices[step].reshape((2,) * rep_bits + (nbr,) + (2,) * tp_bits + (per,))
    picks = by_distance(picks, range(rep_bits), replica)
    picks = by_distance(picks, range(rep_bits + 1, rep_bits + 1 + tp_bits), tp)
    picks = picks.reshape(reps, nbr, parts, per).transpose(2, 0, 1, 3)
    picks = picks.reshape(parts, reps, nbr * per)
    both = jnp.concatenate([picks, picks + BLOCK], axis=2)
    own = jnp.concatenate([both[:, 0], picks[:, 0]], axis=1)
    return both.reshape(parts, 1, -1), own.reshape(parts, 1, -1), per


def local(reps, parts, inputs, targets, weight, momentum, indices):
    return steps(reps, parts, inputs, targets, weight, momentum, indices)


def steps(reps, parts, inputs, targets, weight, momentum, indices):
    rows, cols = weight.shape
    nbr = rows // BLOCK
    tile = cols // parts
    chips = parts // CORES
    count = chips // 2
    replica = lax.axis_index("rep").astype(jnp.int32)
    tp = lax.axis_index("tp").astype(jnp.int32)
    place = tp[None]

    acts_t, tables, projected = [None] * STEPS, [None] * STEPS, [None] * STEPS

    def basis_work(step, picked):
        picks_all, picks_own, per = pick_tables(picked, step, reps, parts, replica, tp)
        tables[step] = prep(place, picks_all, picks_own)
        projected[step], acts_t[step] = project(
            place, tables[step][2], inputs, step, nbr, per
        )
        return per

    moment = momentum
    gathered = None
    weights = [[None, None], [None, None]]
    final_m = final_w = None
    for step in range(STEPS):
        last = step == STEPS - 1
        totals = [None] * chips
        for chunk in (1, 0):
            start = chunk * count
            found = [None, None]
            for core in (1, 0):
                if step == 0:
                    found[core] = first(place, weight, inputs, tile, start, core, count)
                else:
                    weights[chunk][core], found[core] = forward(
                        place,
                        weight,
                        inputs,
                        step,
                        tile,
                        per,
                        start,
                        core,
                        count,
                        tables[step - 1][0],
                        gathered,
                    )
                if core == 1:
                    other = swap(found[1], "tp", parts, 1)
            for at in range(count):
                total = found[0][at].astype(F32) + other[at].astype(F32)
                totals[start + at] = total if start + at == 0 else total.astype(BF)
            if step == 0 and chunk == 1:
                *totals[count:], late = lax.optimization_barrier((*totals[count:], indices))
                for at in range(STEPS):
                    per = basis_work(at, late)
                old = moment_rows(place, tables[0][2], momentum, tile, per)
        total = totals[0] - targets[step].astype(F32)
        for mask in range(1, chips):
            total = total + swap(totals[mask], "tp", parts, mask * CORES).astype(F32)
        errors = lax.optimization_barrier(total.astype(BF))
        pieces = [errors] + [swap(errors, "tp", parts, mask * CORES) for mask in range(1, chips)]
        pairs = []
        for piece in pieces:
            pairs += [piece, swap(piece, "tp", parts, 1)]
        exact, sent = coefficients(place, projected[step], pairs, old)
        gathered = [sent] + [swap(sent, "rep", reps, mask) for mask in range(1, reps)]
        update = functools.partial(momentum_step, place, acts_t[step])
        if not last:
            moment, old = update(
                jnp.stack(pairs),
                moment,
                tables[step][1],
                exact,
                per,
                0,
                tables[step + 1][2],
                cols,
                None,
            )
        else:
            early, _ = coefficients(place, projected[step], pairs[:CORES], old)
            (final_m,) = update(
                jnp.stack(pairs[:CORES]),
                moment,
                tables[step][1],
                early,
                per,
                0,
                None,
                cols,
                None,
            )
            (final_m,) = update(
                jnp.stack(pairs[CORES:]),
                moment,
                tables[step][1],
                exact,
                per,
                CORES,
                None,
                cols,
                final_m,
            )
    for chunk in (0, 1):
        final_w = finish(
            place,
            weights[chunk][0],
            weights[chunk][1],
            tables[STEPS - 1][0],
            gathered,
            per,
            chunk * count,
            cols,
            final_w,
        )
    return (final_w, final_m)


def solution(mesh):
    reps, parts = mesh.shape["rep"], mesh.shape["tp"]
    in_specs = (
        P(None, "rep", "tp"),
        P(None, "rep", "tp"),
        P("tp", None),
        P("rep", "tp", None),
        P(None, None, "tp", None, None),
    )
    out_specs = (P("tp", None), P("rep", "tp", None))
    return jax.shard_map(
        functools.partial(local, reps, parts),
        mesh=mesh,
        in_specs=in_specs,
        out_specs=out_specs,
        check_vma=False,
    )
```

profile of v0, /device:TPU:0, one launch (start us, length us, event | category | flops | bytes accessed | tf_op | source)
XLA Modules:
  0.0 156.7 jit_solution(14890871440683775283)
XLA Ops:
  0.6 2.7 %first.5 = bf16[2,512,256]{2,1,0:T(8,128)(2,1)S(1)} custom-call(s32[1]{0:T(128)} %bitcast.place, bf16[1024,2048]{1,0:T(8,128)(2,1)} %w_ref.15, bf16[2,512,1024]{2,1,0:T(8,128)(2,1)} %x_ref.19), custom_call_target="tpu_custom_call" | custom-call | flops 536870912 | bytes 2097152 | tf_op jit(solution)/shard_map/first/pallas_call | solution.py:336
  3.3 0.6 collective-permute-start
  3.9 2.7 %first.7 = bf16[2,512,256]{2,1,0:T(8,128)(2,1)S(1)} custom-call(s32[1]{0:T(128)} %bitcast.place, bf16[1024,2048]{1,0:T(8,128)(2,1)} %w_ref.15, bf16[2,512,1024]{2,1,0:T(8,128)(2,1)} %x_ref.19), custom_call_target="tpu_custom_call" | custom-call | flops 536870912 | bytes 2097152 | tf_op jit(solution)/shard_map/first/pallas_call | solution.py:336
  6.7 2.7 %first.6 = bf16[2,512,256]{2,1,0:T(8,128)(2,1)S(1)} custom-call(s32[1]{0:T(128)} %bitcast.place, bf16[1024,2048]{1,0:T(8,128)(2,1)} %w_ref.15, bf16[2,512,1024]{2,1,0:T(8,128)(2,1)} %x_ref.19), custom_call_target="tpu_custom_call" | custom-call | flops 536870912 | bytes 2097152 | tf_op jit(solution)/shard_map/first/pallas_call | solution.py:336
  9.4 2.7 %first.4 = bf16[2,512,256]{2,1,0:T(8,128)(2,1)S(1)} custom-call(s32[1]{0:T(128)} %bitcast.place, bf16[1024,2048]{1,0:T(8,128)(2,1)} %w_ref.15, bf16[2,512,1024]{2,1,0:T(8,128)(2,1)} %x_ref.19), custom_call_target="tpu_custom_call" | custom-call | flops 536870912 | bytes 2097152 | tf_op jit(solution)/shard_map/first/pallas_call | solution.py:336
  12.1 0.9 fusion.7
  13.9 4.1 %collective-permute-start.3 = (bf16[512,256]{1,0:T(8,128)(2,1)}, bf16[512,256]{1,0:T(8,128)(2,1)}, u32[]{:S(2)}, u32[]{:S(2)}) collective-permute-start(bf16[512,256]{1,0:T(8,128)(2,1)} %get-tuple-element.34), channel_id=1, source_target_pairs={{0,4},{1,5},{2,6},{3,7},{4,0},{5,1},{6,2},{7,3},{8,12},{9,13},{10,... | collective-permute-start | bytes 786440 | tf_op jit(solution)/shard_map/ppermute | solution.py:27
  18.0 1.3 collective-permute-start.4
  19.4 0.7 pad_add_fusion
  20.1 1.2 fusion.8
  21.8 0.6 slice_bitcast_fusion.1
  22.4 14.4 %collective-permute-done.3 = bf16[512,256]{1,0:T(8,128)(2,1)} collective-permute-done((bf16[512,256]{1,0:T(8,128)(2,1)}, bf16[512,256]{1,0:T(8,128)(2,1)}, u32[]{:S(2)}, u32[]{:S(2)}) %collective-permute-start.3) | collective-permute-done | bytes 262176 | tf_op jit(solution)/shard_map/ppermute | solution.py:27
  36.7 2.4 %collective-permute-done.2 = bf16[512,256]{1,0:T(8,128)(2,1)S(1)} collective-permute-done((bf16[512,256]{1,0:T(8,128)(2,1)S(1)}, bf16[512,256]{1,0:T(8,128)(2,1)S(1)}, u32[]{:S(2)}, u32[]{:S(2)}) %collective-permute-start.2) | collective-permute-done | bytes 262176 | tf_op jit(solution)/shard_map/ppermute | solution.py:27
  39.1 1.4 fusion.5.refs_0_
  40.5 3.6 %collective-permute-start.10 = (bf16[512,256]{1,0:T(8,128)(2,1)S(1)}, bf16[512,256]{1,0:T(8,128)(2,1)S(1)}, u32[]{:S(2)}, u32[]{:S(2)}) collective-permute-start(bf16[512,256]{1,0:T(8,128)(2,1)S(1)} %fusion.5.refs_0_), channel_id=1, source_target_pairs={{0,6},{1,7},{2,4},{3,5},{4,2},{5,3},{6,0},{7,1},{8,14},{9,15},{10,... | collective-permute-start | bytes 786440 | tf_op jit(solution)/shard_map/ppermute | solution.py:27
  44.1 1.7 %collective-permute-start.8 = (bf16[512,256]{1,0:T(8,128)(2,1)S(1)}, bf16[512,256]{1,0:T(8,128)(2,1)}, u32[]{:S(2)}, u32[]{:S(2)}) collective-permute-start(bf16[512,256]{1,0:T(8,128)(2,1)S(1)} %fusion.5.refs_0_), channel_id=1, source_target_pairs={{0,4},{1,5},{2,6},{3,7},{4,0},{5,1},{6,2},{7,3},{8,12},{9,13},{10,... | collective-permute-start | bytes 786440 | tf_op jit(solution)/shard_map/ppermute | solution.py:27
  46.3 0.8 copy-done.3
  47.2 0.8 copy-done.5
  48.0 1.6 %shard_map.110 = (bf16[8,128,256]{2,1,0:T(8,128)(2,1)S(1)}, bf16[8,128,96]{2,1,0:T(8,128)(2,1)S(1)}, bf16[8,64,128]{2,1,0:T(8,128)(2,1)S(1)}) custom-call(s32[1]{0:T(128)} %bitcast.place, s32[8,1,256]{2,1,0:T(1,128)S(1)} %reshape.71.all_ref, s32[8,1,96]{2,1,0:T(1,128)S(1)} %bitcast.85, bf16[128,256]{1,0:T(8,128)(2,1)S(1)} %copy-done.3, ...), custom_call_target="tpu_custom_call" | custom-call | flops 234881024 | bytes 2097152 | tf_op jit(solution)/shard_map/pallas_call | solution.py:54
  49.6 0.6 copy.18
  50.2 0.8 reshape.70.all_ref
  51.0 0.7 pad_add_fusion.2
  51.8 0.8 copy-done.4
  52.6 0.8 copy-done.6
  53.5 1.6 %shard_map.104 = (bf16[8,128,256]{2,1,0:T(8,128)(2,1)S(1)}, bf16[8,128,96]{2,1,0:T(8,128)(2,1)S(1)}, bf16[8,64,128]{2,1,0:T(8,128)(2,1)S(1)}) custom-call(s32[1]{0:T(128)} %bitcast.place, s32[8,1,256]{2,1,0:T(1,128)S(1)} %reshape.70.all_ref, s32[8,1,96]{2,1,0:T(1,128)S(1)} %bitcast.86, bf16[128,256]{1,0:T(8,128)(2,1)S(1)} %copy-done.4, ...), custom_call_target="tpu_custom_call" | custom-call | flops 234881024 | bytes 2097152 | tf_op jit(solution)/shard_map/pallas_call | solution.py:54
  55.1 0.8 shard_map.105
  55.9 0.8 shard_map.111
  56.8 3.4 %copy-done.2 = f32[1,1024,2048]{2,1,0:T(8,128)S(1)} copy-done((f32[1,1024,2048]{2,1,0:T(8,128)S(1)}, f32[1,1024,2048]{2,1,0:T(8,128)}, u32[]{:S(2)}) %copy-start.2) | copy-done | bytes 8388632
  60.2 2.4 %shard_map.106.old_ref = f32[8,32,128]{2,1,0:T(8,128)S(1)} custom-call(s32[1]{0:T(128)} %bitcast.place, bf16[8,64,128]{2,1,0:T(8,128)(2,1)S(1)} %get-tuple-element.32.kept_ref, f32[1,1024,2048]{2,1,0:T(8,128)S(1)} %copy-done.2), custom_call_target="tpu_custom_call" | custom-call | flops 268435456 | bytes 8388608 | tf_op jit(solution)/shard_map/pallas_call | solution.py:54
  62.6 0.6 collective-permute-start.11
  63.2 3.0 %collective-permute-done.8.refs_4_ = bf16[512,256]{1,0:T(8,128)(2,1)} collective-permute-done((bf16[512,256]{1,0:T(8,128)(2,1)S(1)}, bf16[512,256]{1,0:T(8,128)(2,1)}, u32[]{:S(2)}, u32[]{:S(2)}) %collective-permute-start.8) | collective-permute-done | bytes 262176 | tf_op jit(solution)/shard_map/ppermute | solution.py:27
  66.8 1.2 collective-permute-done.9.refs_5_
  68.4 1.5 shard_map.107
  69.9 2.5 %collective-permute-start.14 = (bf16[8,32,128]{2,1,0:T(8,128)(2,1)S(1)}, bf16[8,32,128]{2,1,0:T(8,128)(2,1)S(1)}, u32[]{:S(2)}, u32[]{:S(2)}) collective-permute-start(bf16[8,32,128]{2,1,0:T(8,128)(2,1)S(1)} %get-tuple-element.36.refs_0_), channel_id=1, source_target_pairs={{0,24},{8,16},{16,8},{24,0},{1,25},{9,17},{17,9},{25,1},{2,26},{10... | collective-permute-start | bytes 196616 | tf_op jit(solution)/shard_map/ppermute | solution.py:27
  72.4 0.5 collective-permute-start.13
  72.9 0.5 collective-permute-start.12
  73.4 1.0 bitcast_dynamic-update-slice_fusion.11
  74.4 0.7 collective-permute-done.14.refs_3_
  75.1 1.6 collective-permute-done.13.refs_2_
  76.7 0.5 collective-permute-done.12.refs_1_
  77.2 1.9 %shard_map.114 = (bf16[2,1024,256]{2,1,0:T(8,128)(2,1)S(1)}, bf16[2,512,256]{2,1,0:T(8,128)(2,1)S(1)}) custom-call(s32[1]{0:T(128)} %bitcast.place, bf16[1024,2048]{1,0:T(8,128)(2,1)S(1)} %copy-done, bf16[2,512,1024]{2,1,0:T(8,128)(2,1)S(1)} %copy-done.1, bf16[8,128,256]{2,1,0:T(8,128)(2,1)S(1)} %get-tuple-element.31.dec_ref, ...), custom_call_target="tpu_custom_call" | custom-call | flops 536870912 | bytes 2097152 | tf_op jit(solution)/shard_map/pallas_call | solution.py:54
  79.2 1.9 %shard_map.109 = (bf16[2,1024,256]{2,1,0:T(8,128)(2,1)S(1)}, bf16[2,512,256]{2,1,0:T(8,128)(2,1)S(1)}) custom-call(s32[1]{0:T(128)} %bitcast.place, bf16[1024,2048]{1,0:T(8,128)(2,1)S(1)} %copy-done, bf16[2,512,1024]{2,1,0:T(8,128)(2,1)S(1)} %copy-done.1, bf16[8,128,256]{2,1,0:T(8,128)(2,1)S(1)} %get-tuple-element.31.dec_ref, ...), custom_call_target="tpu_custom_call" | custom-call | flops 536870912 | bytes 2097152 | tf_op jit(solution)/shard_map/pallas_call | solution.py:54
  81.1 0.6 collective-permute-start.17
  81.6 1.0 bitcast_dynamic-update-slice_fusion.9
  82.6 1.9 %shard_map.113 = (bf16[2,1024,256]{2,1,0:T(8,128)(2,1)S(1)}, bf16[2,512,256]{2,1,0:T(8,128)(2,1)S(1)}) custom-call(s32[1]{0:T(128)} %bitcast.place, bf16[1024,2048]{1,0:T(8,128)(2,1)S(1)} %copy-done, bf16[2,512,1024]{2,1,0:T(8,128)(2,1)S(1)} %copy-done.1, bf16[8,128,256]{2,1,0:T(8,128)(2,1)S(1)} %get-tuple-element.31.dec_ref, ...), custom_call_target="tpu_custom_call" | custom-call | flops 536870912 | bytes 2097152 | tf_op jit(solution)/shard_map/pallas_call | solution.py:54
  84.5 1.9 %shard_map.108 = (bf16[2,1024,256]{2,1,0:T(8,128)(2,1)S(1)}, bf16[2,512,256]{2,1,0:T(8,128)(2,1)S(1)}) custom-call(s32[1]{0:T(128)} %bitcast.place, bf16[1024,2048]{1,0:T(8,128)(2,1)S(1)} %copy-done, bf16[2,512,1024]{2,1,0:T(8,128)(2,1)S(1)} %copy-done.1, bf16[8,128,256]{2,1,0:T(8,128)(2,1)S(1)} %get-tuple-element.31.dec_ref, ...), custom_call_target="tpu_custom_call" | custom-call | flops 536870912 | bytes 2097152 | tf_op jit(solution)/shard_map/pallas_call | solution.py:54
  86.5 0.6 collective-permute-start.16
  87.2 3.5 %collective-permute-start.18 = (bf16[512,256]{1,0:T(8,128)(2,1)S(1)}, bf16[512,256]{1,0:T(8,128)(2,1)S(1)}, u32[]{:S(2)}, u32[]{:S(2)}) collective-permute-start(bf16[512,256]{1,0:T(8,128)(2,1)S(1)} %get-tuple-element.58), channel_id=1, source_target_pairs={{0,4},{1,5},{2,6},{3,7},{4,0},{5,1},{6,2},{7,3},{8,12},{9,13},{10,... | collective-permute-start | bytes 786440 | tf_op jit(solution)/shard_map/ppermute | solution.py:27
  91.2 8.5 %collective-permute-done.16 = bf16[512,256]{1,0:T(8,128)(2,1)S(1)} collective-permute-done((bf16[512,256]{1,0:T(8,128)(2,1)S(1)}, bf16[512,256]{1,0:T(8,128)(2,1)S(1)}, u32[]{:S(2)}, u32[]{:S(2)}) %collective-permute-start.16) | collective-permute-done | bytes 262176 | tf_op jit(solution)/shard_map/ppermute | solution.py:27
  99.7 9.5 %collective-permute-done.18 = bf16[512,256]{1,0:T(8,128)(2,1)S(1)} collective-permute-done((bf16[512,256]{1,0:T(8,128)(2,1)S(1)}, bf16[512,256]{1,0:T(8,128)(2,1)S(1)}, u32[]{:S(2)}, u32[]{:S(2)}) %collective-permute-start.18) | collective-permute-done | bytes 262176 | tf_op jit(solution)/shard_map/ppermute | solution.py:27
  109.4 2.4 %collective-permute-start.25 = (bf16[512,256]{1,0:T(8,128)(2,1)S(1)}, bf16[512,256]{1,0:T(8,128)(2,1)S(1)}, u32[]{:S(2)}, u32[]{:S(2)}) collective-permute-start(bf16[512,256]{1,0:T(8,128)(2,1)S(1)} %fusion.2.refs_0_), channel_id=1, source_target_pairs={{0,6},{1,7},{2,4},{3,5},{4,2},{5,3},{6,0},{7,1},{8,14},{9,15},{10,... | collective-permute-start | bytes 786440 | tf_op jit(solution)/shard_map/ppermute | solution.py:27
  111.9 9.9 %collective-permute-start.23 = (bf16[512,256]{1,0:T(8,128)(2,1)S(1)}, bf16[512,256]{1,0:T(8,128)(2,1)S(1)}, u32[]{:S(2)}, u32[]{:S(2)}) collective-permute-start(bf16[512,256]{1,0:T(8,128)(2,1)S(1)} %fusion.2.refs_0_), channel_id=1, source_target_pairs={{0,4},{1,5},{2,6},{3,7},{4,0},{5,1},{6,2},{7,3},{8,12},{9,13},{10,... | collective-permute-start | bytes 786440 | tf_op jit(solution)/shard_map/ppermute | solution.py:27
  121.9 7.0 %shard_map.112 = (f32[8,1024,256]{2,1,0:T(8,128)S(1)}, f32[8,32,128]{2,1,0:T(8,128)S(1)}) custom-call(s32[1]{0:T(128)} %bitcast.place, bf16[1024,512]{1,0:T(8,128)(2,1)S(1)} %get-tuple-element.42.xt_ref, bf16[8,512,256]{2,1,0:T(8,128)(2,1)S(1)} %bitcast_dynamic-update-slice_fusion.6.e_ref, f32[1,1024,2048]{2,1,0:T(8,128)S(1)} %bitcast.82, ...), custom_call_target="tpu_custom_call" | custom-call | flops 2147483648 | bytes 16777216 | tf_op jit(solution)/shard_map/pallas_call | solution.py:54
  129.0 0.6 collective-permute-start.26
  129.5 8.8 %collective-permute-done.23.refs_4_ = bf16[512,256]{1,0:T(8,128)(2,1)S(1)} collective-permute-done((bf16[512,256]{1,0:T(8,128)(2,1)S(1)}, bf16[512,256]{1,0:T(8,128)(2,1)S(1)}, u32[]{:S(2)}, u32[]{:S(2)}) %collective-permute-start.23) | collective-permute-done | bytes 262176 | tf_op jit(solution)/shard_map/ppermute | solution.py:27
  138.4 0.6 collective-permute-start.22
  139.0 0.8 shard_map.118
  139.8 2.1 %shard_map.119.refs_0_ = f32[1,1024,2048]{2,1,0:T(8,128)} custom-call(s32[1]{0:T(128)} %bitcast.place, bf16[1024,512]{1,0:T(8,128)(2,1)S(1)} %get-tuple-element.53.xt_ref, bf16[2,512,256]{2,1,0:T(8,128)(2,1)S(1)} %pad_maximum_fusion.e_ref, f32[8,1024,256]{2,1,0:T(8,128)S(1)} %get-tuple-element.54.m_ref, bf16[8,128,96]{2,1,0:T(8,128)(2,1)S(1)} %get-tuple-element.55.dec_ref, ...), custom_call_target="tpu_custom_call" | custom-call | flops 536870912 | bytes 4194304 | tf_op jit(solution)/shard_map/pallas_call | solution.py:54
  142.5 1.6 collective-permute-start.29
  144.1 0.8 collective-permute-start.28
  144.8 1.2 collective-permute-start.27
  146.2 5.3 %shard_map.120 = f32[1,1024,2048]{2,1,0:T(8,128)} custom-call(s32[1]{0:T(128)} %bitcast.place, bf16[1024,512]{1,0:T(8,128)(2,1)S(1)} %get-tuple-element.53.xt_ref, bf16[6,512,256]{2,1,0:T(8,128)(2,1)S(1)} %bitcast_dynamic-update-slice_fusion.e_ref, f32[8,1024,256]{2,1,0:T(8,128)S(1)} %get-tuple-element.54.m_ref, ...), custom_call_target="tpu_custom_call", output_to_operand_aliasing={{}: (6, {})} | custom-call | flops 1610612736 | bytes 12582912 | tf_op jit(solution)/shard_map/pallas_call | solution.py:54
  151.5 2.6 %shard_map.116.refs_4_ = bf16[1024,2048]{1,0:T(8,128)(2,1)} custom-call(s32[1]{0:T(128)} %bitcast.place, bf16[2,1024,256]{2,1,0:T(8,128)(2,1)S(1)} %get-tuple-element.51.keep_ref, bf16[2,1024,256]{2,1,0:T(8,128)(2,1)S(1)} %get-tuple-element.52.send_ref, bf16[8,128,256]{2,1,0:T(8,128)(2,1)S(1)} %get-tuple-element.39.dec_ref, ...), custom_call_target="tpu_custom_call" | custom-call | flops 536870912 | bytes 4194304 | tf_op jit(solution)/shard_map/pallas_call | solution.py:54
  154.1 2.6 %shard_map.117 = bf16[1024,2048]{1,0:T(8,128)(2,1)} custom-call(s32[1]{0:T(128)} %bitcast.place, bf16[2,1024,256]{2,1,0:T(8,128)(2,1)S(1)} %get-tuple-element.37.keep_ref, bf16[2,1024,256]{2,1,0:T(8,128)(2,1)S(1)} %get-tuple-element.38.send_ref, bf16[8,128,256]{2,1,0:T(8,128)(2,1)S(1)} %get-tuple-element.39.dec_ref, ...), custom_call_target="tpu_custom_call", output_to_operand_aliasing={{}: (8, {})} | custom-call | flops 536870912 | bytes 4194304 | tf_op jit(solution)/shard_map/pallas_call | solution.py:54
  (93 shorter events, 4.7 us)
Async XLA Ops:
  3.3 8.8 %collective-permute-start = (bf16[2,512,256]{2,1,0:T(8,128)(2,1)S(1)}, bf16[2,512,256]{2,1,0:T(8,128)(2,1)S(1)}, u32[]{:S(2)}, u32[]{:S(2)}) collective-permute-start(bf16[2,512,256]{2,1,0:T(8,128)(2,1)S(1)} %first.5), channel_id=1, source_target_pairs={{0,1},{1,0},{2,3},{3,2},{4,5},{5,4},{6,7},{7,6},{8,9},{9,8},{10,11... | collective-permute-start | bytes 1572872 | tf_op jit(solution)/shard_map/ppermute | solution.py:27
  6.6 13.6 %collective-permute-start.1 = (bf16[2,512,256]{2,1,0:T(8,128)(2,1)S(1)}, bf16[2,512,256]{2,1,0:T(8,128)(2,1)}, u32[]{:S(2)}, u32[]{:S(2)}) collective-permute-start(bf16[2,512,256]{2,1,0:T(8,128)(2,1)S(1)} %first.7), channel_id=1, source_target_pairs={{0,1},{1,0},{2,3},{3,2},{4,5},{5,4},{6,7},{7,6},{8,9},{9,8},{10,11... | collective-permute-start | bytes 1572872 | tf_op jit(solution)/shard_map/ppermute | solution.py:27
  9.3 3.7 %copy-start.9 = (s32[2,4,8,16,2]{3,4,2,1,0:T(2,128)S(1)}, s32[2,4,8,16,2]{3,4,2,1,0:T(2,128)}, u32[]{:S(2)}) copy-start(s32[2,4,8,16,2]{3,4,2,1,0:T(2,128)} %param.13) | copy-start | bytes 24580
  13.9 22.8 %collective-permute-start.3 = (bf16[512,256]{1,0:T(8,128)(2,1)}, bf16[512,256]{1,0:T(8,128)(2,1)}, u32[]{:S(2)}, u32[]{:S(2)}) collective-permute-start(bf16[512,256]{1,0:T(8,128)(2,1)} %get-tuple-element.34), channel_id=1, source_target_pairs={{0,4},{1,5},{2,6},{3,7},{4,0},{5,1},{6,2},{7,3},{8,12},{9,13},{10,... | collective-permute-start | bytes 786440 | tf_op jit(solution)/shard_map/ppermute | solution.py:27
  18.0 18.8 %collective-permute-start.4 = (bf16[512,256]{1,0:T(8,128)(2,1)}, bf16[512,256]{1,0:T(8,128)(2,1)}, u32[]{:S(2)}, u32[]{:S(2)}) collective-permute-start(bf16[512,256]{1,0:T(8,128)(2,1)} %get-tuple-element.35), channel_id=1, source_target_pairs={{0,6},{1,7},{2,4},{3,5},{4,2},{5,3},{6,0},{7,1},{8,14},{9,15},{10,... | collective-permute-start | bytes 786440 | tf_op jit(solution)/shard_map/ppermute | solution.py:27
  20.1 34.9 %copy-start.1 = (bf16[2,512,1024]{2,1,0:T(8,128)(2,1)S(1)}, bf16[2,512,1024]{2,1,0:T(8,128)(2,1)}, u32[]{:S(2)}) copy-start(bf16[2,512,1024]{2,1,0:T(8,128)(2,1)} %x_ref.19) | copy-start | bytes 6291460
  21.3 17.8 %collective-permute-start.2 = (bf16[512,256]{1,0:T(8,128)(2,1)S(1)}, bf16[512,256]{1,0:T(8,128)(2,1)S(1)}, u32[]{:S(2)}, u32[]{:S(2)}) collective-permute-start(bf16[512,256]{1,0:T(8,128)(2,1)S(1)} %fusion.8), channel_id=1, source_target_pairs={{0,2},{1,3},{2,0},{3,1},{4,6},{5,7},{6,4},{7,5},{8,10},{9,11},{10,... | collective-permute-start | bytes 786440 | tf_op jit(solution)/shard_map/ppermute | solution.py:27
  21.8 27.8 %copy-start.8 = (s32[8,4,64]{2,0,1:T(8,128)S(1)}, s32[8,4,64]{2,0,1:T(8,128)}, u32[]{:S(2)}) copy-start(s32[8,4,64]{2,0,1:T(8,128)} %pad_add_fusion) | copy-start | bytes 24580
  40.5 22.1 %collective-permute-start.10 = (bf16[512,256]{1,0:T(8,128)(2,1)S(1)}, bf16[512,256]{1,0:T(8,128)(2,1)S(1)}, u32[]{:S(2)}, u32[]{:S(2)}) collective-permute-start(bf16[512,256]{1,0:T(8,128)(2,1)S(1)} %fusion.5.refs_0_), channel_id=1, source_target_pairs={{0,6},{1,7},{2,4},{3,5},{4,2},{5,3},{6,0},{7,1},{8,14},{9,15},{10,... | collective-permute-start | bytes 786440 | tf_op jit(solution)/shard_map/ppermute | solution.py:27
  44.1 22.1 %collective-permute-start.8 = (bf16[512,256]{1,0:T(8,128)(2,1)S(1)}, bf16[512,256]{1,0:T(8,128)(2,1)}, u32[]{:S(2)}, u32[]{:S(2)}) collective-permute-start(bf16[512,256]{1,0:T(8,128)(2,1)S(1)} %fusion.5.refs_0_), channel_id=1, source_target_pairs={{0,4},{1,5},{2,6},{3,7},{4,0},{5,1},{6,2},{7,3},{8,12},{9,13},{10,... | collective-permute-start | bytes 786440 | tf_op jit(solution)/shard_map/ppermute | solution.py:27
  45.8 20.4 %collective-permute-start.6 = (bf16[512,256]{1,0:T(8,128)(2,1)S(1)}, bf16[512,256]{1,0:T(8,128)(2,1)}, u32[]{:S(2)}, u32[]{:S(2)}) collective-permute-start(bf16[512,256]{1,0:T(8,128)(2,1)S(1)} %fusion.5.refs_0_), channel_id=1, source_target_pairs={{0,2},{1,3},{2,0},{3,1},{4,6},{5,7},{6,4},{7,5},{8,10},{9,11},{10,... | collective-permute-start | bytes 786440 | tf_op jit(solution)/shard_map/ppermute | solution.py:27
  46.3 0.8 copy-start.3
  47.2 0.8 copy-start.5
  51.8 0.8 copy-start.4
  52.6 0.8 copy-start.6
  56.7 10.0 %collective-permute-start.5 = (bf16[512,256]{1,0:T(8,128)(2,1)S(1)}, bf16[512,256]{1,0:T(8,128)(2,1)S(1)}, u32[]{:S(2)}, u32[]{:S(2)}) collective-permute-start(bf16[512,256]{1,0:T(8,128)(2,1)S(1)} %fusion.5.refs_0_), channel_id=1, source_target_pairs={{0,1},{1,0},{2,3},{3,2},{4,5},{5,4},{6,7},{7,6},{8,9},{9,8},{10,11... | collective-permute-start | bytes 786440 | tf_op jit(solution)/shard_map/ppermute | solution.py:27
  56.8 3.4 %copy-start.2 = (f32[1,1024,2048]{2,1,0:T(8,128)S(1)}, f32[1,1024,2048]{2,1,0:T(8,128)}, u32[]{:S(2)}) copy-start(f32[1,1024,2048]{2,1,0:T(8,128)} %m_ref.3) | copy-start | bytes 25165828
  62.6 14.6 %copy-start = (bf16[1024,2048]{1,0:T(8,128)(2,1)S(1)}, bf16[1024,2048]{1,0:T(8,128)(2,1)}, u32[]{:S(2)}) copy-start(bf16[1024,2048]{1,0:T(8,128)(2,1)} %w_ref.15) | copy-start | bytes 12582916
  62.6 4.2 %collective-permute-start.11 = (bf16[512,256]{1,0:T(8,128)(2,1)S(1)}, bf16[512,256]{1,0:T(8,128)(2,1)S(1)}, u32[]{:S(2)}, u32[]{:S(2)}) collective-permute-start(bf16[512,256]{1,0:T(8,128)(2,1)S(1)} %collective-permute-done.10.refs_6_), channel_id=1, source_target_pairs={{0,1},{1,0},{2,3},{3,2},{4,5},{5,4},{6,7},{7,6},{8,9},{9,8},{10,11... | collective-permute-start | bytes 786440 | tf_op jit(solution)/shard_map/ppermute | solution.py:27
  66.2 1.7 %collective-permute-start.9 = (bf16[512,256]{1,0:T(8,128)(2,1)}, bf16[512,256]{1,0:T(8,128)(2,1)S(1)}, u32[]{:S(2)}, u32[]{:S(2)}) collective-permute-start(bf16[512,256]{1,0:T(8,128)(2,1)} %collective-permute-done.8.refs_4_), channel_id=1, source_target_pairs={{0,1},{1,0},{2,3},{3,2},{4,5},{5,4},{6,7},{7,6},{8,9},{9,8},{10,11... | collective-permute-start | bytes 786440 | tf_op jit(solution)/shard_map/ppermute | solution.py:27
  66.3 2.1 %collective-permute-start.7 = (bf16[512,256]{1,0:T(8,128)(2,1)}, bf16[512,256]{1,0:T(8,128)(2,1)S(1)}, u32[]{:S(2)}, u32[]{:S(2)}) collective-permute-start(bf16[512,256]{1,0:T(8,128)(2,1)} %collective-permute-done.6.refs_2_), channel_id=1, source_target_pairs={{0,1},{1,0},{2,3},{3,2},{4,5},{5,4},{6,7},{7,6},{8,9},{9,8},{10,11... | collective-permute-start | bytes 786440 | tf_op jit(solution)/shard_map/ppermute | solution.py:27
  69.9 5.3 %collective-permute-start.14 = (bf16[8,32,128]{2,1,0:T(8,128)(2,1)S(1)}, bf16[8,32,128]{2,1,0:T(8,128)(2,1)S(1)}, u32[]{:S(2)}, u32[]{:S(2)}) collective-permute-start(bf16[8,32,128]{2,1,0:T(8,128)(2,1)S(1)} %get-tuple-element.36.refs_0_), channel_id=1, source_target_pairs={{0,24},{8,16},{16,8},{24,0},{1,25},{9,17},{17,9},{25,1},{2,26},{10... | collective-permute-start | bytes 196616 | tf_op jit(solution)/shard_map/ppermute | solution.py:27
  72.4 4.3 %collective-permute-start.13 = (bf16[8,32,128]{2,1,0:T(8,128)(2,1)S(1)}, bf16[8,32,128]{2,1,0:T(8,128)(2,1)S(1)}, u32[]{:S(2)}, u32[]{:S(2)}) collective-permute-start(bf16[8,32,128]{2,1,0:T(8,128)(2,1)S(1)} %get-tuple-element.36.refs_0_), channel_id=1, source_target_pairs={{0,16},{8,24},{16,0},{24,8},{1,17},{9,25},{17,1},{25,9},{2,18},{10... | collective-permute-start | bytes 196616 | tf_op jit(solution)/shard_map/ppermute | solution.py:27
  72.9 4.3 %collective-permute-start.12 = (bf16[8,32,128]{2,1,0:T(8,128)(2,1)S(1)}, bf16[8,32,128]{2,1,0:T(8,128)(2,1)S(1)}, u32[]{:S(2)}, u32[]{:S(2)}) collective-permute-start(bf16[8,32,128]{2,1,0:T(8,128)(2,1)S(1)} %get-tuple-element.36.refs_0_), channel_id=1, source_target_pairs={{0,8},{8,0},{16,24},{24,16},{1,9},{9,1},{17,25},{25,17},{2,10},{10... | collective-permute-start | bytes 196616 | tf_op jit(solution)/shard_map/ppermute | solution.py:27
  79.1 7.3 %collective-permute-start.15 = (bf16[2,512,256]{2,1,0:T(8,128)(2,1)S(1)}, bf16[2,512,256]{2,1,0:T(8,128)(2,1)S(1)}, u32[]{:S(2)}, u32[]{:S(2)}) collective-permute-start(bf16[2,512,256]{2,1,0:T(8,128)(2,1)S(1)} %get-tuple-element.47), channel_id=1, source_target_pairs={{0,1},{1,0},{2,3},{3,2},{4,5},{5,4},{6,7},{7,6},{8,9},{9,8},{10,11... | collective-permute-start | bytes 1572872 | tf_op jit(solution)/shard_map/ppermute | solution.py:27
  81.1 6.0 %collective-permute-start.17 = (bf16[2,512,256]{2,1,0:T(8,128)(2,1)S(1)}, bf16[2,512,256]{2,1,0:T(8,128)(2,1)S(1)}, u32[]{:S(2)}, u32[]{:S(2)}) collective-permute-start(bf16[2,512,256]{2,1,0:T(8,128)(2,1)S(1)} %get-tuple-element.49), channel_id=1, source_target_pairs={{0,1},{1,0},{2,3},{3,2},{4,5},{5,4},{6,7},{7,6},{8,9},{9,8},{10,11... | collective-permute-start | bytes 1572872 | tf_op jit(solution)/shard_map/ppermute | solution.py:27
  82.6 39.3 %slice-start = ((s8[8388608]{0:T(1024)(128)(4,1)}), s8[4194304]{0:T(1024)(128)(4,1)S(1)}, s32[]{:S(2)}) async-start(s8[8388608]{0:T(1024)(128)(4,1)} %bitcast.81), calls=%async_computation | async-start | bytes 8388608
  84.5 37.4 %slice-start.1 = ((s8[8388608]{0:T(1024)(128)(4,1)}), s8[4194304]{0:T(1024)(128)(4,1)S(1)}, s32[]{:S(2)}) async-start(s8[8388608]{0:T(1024)(128)(4,1)} %bitcast.81), calls=%async_computation.1 | async-start | bytes 8388608
  86.4 22.8 %copy-start.7 = (bf16[2,512,256]{2,1,0:T(8,128)(2,1)S(1)}, bf16[2,512,256]{2,1,0:T(8,128)(2,1)}, u32[]{:S(2)}) copy-start(bf16[2,512,256]{2,1,0:T(8,128)(2,1)} %param.10) | copy-start | bytes 1572868
  86.5 13.2 %collective-permute-start.16 = (bf16[512,256]{1,0:T(8,128)(2,1)S(1)}, bf16[512,256]{1,0:T(8,128)(2,1)S(1)}, u32[]{:S(2)}, u32[]{:S(2)}) collective-permute-start(bf16[512,256]{1,0:T(8,128)(2,1)S(1)} %fusion.9), channel_id=1, source_target_pairs={{0,2},{1,3},{2,0},{3,1},{4,6},{5,7},{6,4},{7,5},{8,10},{9,11},{10,... | collective-permute-start | bytes 786440 | tf_op jit(solution)/shard_map/ppermute | solution.py:27
  87.2 22.0 %collective-permute-start.18 = (bf16[512,256]{1,0:T(8,128)(2,1)S(1)}, bf16[512,256]{1,0:T(8,128)(2,1)S(1)}, u32[]{:S(2)}, u32[]{:S(2)}) collective-permute-start(bf16[512,256]{1,0:T(8,128)(2,1)S(1)} %get-tuple-element.58), channel_id=1, source_target_pairs={{0,4},{1,5},{2,6},{3,7},{4,0},{5,1},{6,2},{7,3},{8,12},{9,13},{10,... | collective-permute-start | bytes 786440 | tf_op jit(solution)/shard_map/ppermute | solution.py:27
  90.8 18.4 %collective-permute-start.19 = (bf16[512,256]{1,0:T(8,128)(2,1)S(1)}, bf16[512,256]{1,0:T(8,128)(2,1)S(1)}, u32[]{:S(2)}, u32[]{:S(2)}) collective-permute-start(bf16[512,256]{1,0:T(8,128)(2,1)S(1)} %get-tuple-element.59), channel_id=1, source_target_pairs={{0,6},{1,7},{2,4},{3,5},{4,2},{5,3},{6,0},{7,1},{8,14},{9,15},{10,... | collective-permute-start | bytes 786440 | tf_op jit(solution)/shard_map/ppermute | solution.py:27
  109.4 19.6 %collective-permute-start.25 = (bf16[512,256]{1,0:T(8,128)(2,1)S(1)}, bf16[512,256]{1,0:T(8,128)(2,1)S(1)}, u32[]{:S(2)}, u32[]{:S(2)}) collective-permute-start(bf16[512,256]{1,0:T(8,128)(2,1)S(1)} %fusion.2.refs_0_), channel_id=1, source_target_pairs={{0,6},{1,7},{2,4},{3,5},{4,2},{5,3},{6,0},{7,1},{8,14},{9,15},{10,... | collective-permute-start | bytes 786440 | tf_op jit(solution)/shard_map/ppermute | solution.py:27
  111.9 26.5 %collective-permute-start.23 = (bf16[512,256]{1,0:T(8,128)(2,1)S(1)}, bf16[512,256]{1,0:T(8,128)(2,1)S(1)}, u32[]{:S(2)}, u32[]{:S(2)}) collective-permute-start(bf16[512,256]{1,0:T(8,128)(2,1)S(1)} %fusion.2.refs_0_), channel_id=1, source_target_pairs={{0,4},{1,5},{2,6},{3,7},{4,0},{5,1},{6,2},{7,3},{8,12},{9,13},{10,... | collective-permute-start | bytes 786440 | tf_op jit(solution)/shard_map/ppermute | solution.py:27
  121.8 16.6 %collective-permute-start.20 = (bf16[512,256]{1,0:T(8,128)(2,1)S(1)}, bf16[512,256]{1,0:T(8,128)(2,1)S(1)}, u32[]{:S(2)}, u32[]{:S(2)}) collective-permute-start(bf16[512,256]{1,0:T(8,128)(2,1)S(1)} %fusion.2.refs_0_), channel_id=1, source_target_pairs={{0,1},{1,0},{2,3},{3,2},{4,5},{5,4},{6,7},{7,6},{8,9},{9,8},{10,11... | collective-permute-start | bytes 786440 | tf_op jit(solution)/shard_map/ppermute | solution.py:27
  121.8 16.6 %collective-permute-start.21 = (bf16[512,256]{1,0:T(8,128)(2,1)S(1)}, bf16[512,256]{1,0:T(8,128)(2,1)S(1)}, u32[]{:S(2)}, u32[]{:S(2)}) collective-permute-start(bf16[512,256]{1,0:T(8,128)(2,1)S(1)} %fusion.2.refs_0_), channel_id=1, source_target_pairs={{0,2},{1,3},{2,0},{3,1},{4,6},{5,7},{6,4},{7,5},{8,10},{9,11},{10,... | collective-permute-start | bytes 786440 | tf_op jit(solution)/shard_map/ppermute | solution.py:27
  129.0 13.0 %collective-permute-start.26 = (bf16[512,256]{1,0:T(8,128)(2,1)S(1)}, bf16[512,256]{1,0:T(8,128)(2,1)S(1)}, u32[]{:S(2)}, u32[]{:S(2)}) collective-permute-start(bf16[512,256]{1,0:T(8,128)(2,1)S(1)} %collective-permute-done.25.refs_6_), channel_id=1, source_target_pairs={{0,1},{1,0},{2,3},{3,2},{4,5},{5,4},{6,7},{7,6},{8,9},{9,8},{10,11... | collective-permute-start | bytes 786440 | tf_op jit(solution)/shard_map/ppermute | solution.py:27
  138.4 3.6 %collective-permute-start.24 = (bf16[512,256]{1,0:T(8,128)(2,1)S(1)}, bf16[512,256]{1,0:T(8,128)(2,1)S(1)}, u32[]{:S(2)}, u32[]{:S(2)}) collective-permute-start(bf16[512,256]{1,0:T(8,128)(2,1)S(1)} %collective-permute-done.23.refs_4_), channel_id=1, source_target_pairs={{0,1},{1,0},{2,3},{3,2},{4,5},{5,4},{6,7},{7,6},{8,9},{9,8},{10,11... | collective-permute-start | bytes 786440 | tf_op jit(solution)/shard_map/ppermute | solution.py:27
  138.4 3.6 %collective-permute-start.22 = (bf16[512,256]{1,0:T(8,128)(2,1)S(1)}, bf16[512,256]{1,0:T(8,128)(2,1)S(1)}, u32[]{:S(2)}, u32[]{:S(2)}) collective-permute-start(bf16[512,256]{1,0:T(8,128)(2,1)S(1)} %collective-permute-done.21.refs_2_), channel_id=1, source_target_pairs={{0,1},{1,0},{2,3},{3,2},{4,5},{5,4},{6,7},{7,6},{8,9},{9,8},{10,11... | collective-permute-start | bytes 786440 | tf_op jit(solution)/shard_map/ppermute | solution.py:27
  142.5 9.0 %collective-permute-start.29 = (bf16[8,32,128]{2,1,0:T(8,128)(2,1)S(1)}, bf16[8,32,128]{2,1,0:T(8,128)(2,1)S(1)}, u32[]{:S(2)}, u32[]{:S(2)}) collective-permute-start(bf16[8,32,128]{2,1,0:T(8,128)(2,1)S(1)} %get-tuple-element.50.refs_0_), channel_id=1, source_target_pairs={{0,24},{8,16},{16,8},{24,0},{1,25},{9,17},{17,9},{25,1},{2,26},{10... | collective-permute-start | bytes 196616 | tf_op jit(solution)/shard_map/ppermute | solution.py:27
  144.1 7.4 %collective-permute-start.28 = (bf16[8,32,128]{2,1,0:T(8,128)(2,1)S(1)}, bf16[8,32,128]{2,1,0:T(8,128)(2,1)S(1)}, u32[]{:S(2)}, u32[]{:S(2)}) collective-permute-start(bf16[8,32,128]{2,1,0:T(8,128)(2,1)S(1)} %get-tuple-element.50.refs_0_), channel_id=1, source_target_pairs={{0,16},{8,24},{16,0},{24,8},{1,17},{9,25},{17,1},{25,9},{2,18},{10... | collective-permute-start | bytes 196616 | tf_op jit(solution)/shard_map/ppermute | solution.py:27
  144.8 6.7 %collective-permute-start.27 = (bf16[8,32,128]{2,1,0:T(8,128)(2,1)S(1)}, bf16[8,32,128]{2,1,0:T(8,128)(2,1)S(1)}, u32[]{:S(2)}, u32[]{:S(2)}) collective-permute-start(bf16[8,32,128]{2,1,0:T(8,128)(2,1)S(1)} %get-tuple-element.50.refs_0_), channel_id=1, source_target_pairs={{0,8},{8,0},{16,24},{24,16},{1,9},{9,1},{17,25},{25,17},{2,10},{10... | collective-permute-start | bytes 196616 | tf_op jit(solution)/shard_map/ppermute | solution.py:27
where the time goes:
time: 157 us
  waiting for transfers between devices  51.1 us (33%)
  Pallas kernels  47.9 us (31%)
  starting transfers between devices  39.1 us (25%)
  local copies, waits for them, and re-layouts  11.6 us (7%)
  other arithmetic  5.82 us (4%)
    ppermute x30, waiting for transfers between devices, swap(): return lax.ppermute(value, axis, [(at, at ^ mask) for at in range(size)])  51.1 us
    ppermute x30, starting transfers between devices, swap(): return lax.ppermute(value, axis, [(at, at ^ mask) for at in range(size)])  39.1 us
    pallas_call x17, Pallas kernels, call(): pl.pallas_call(kernel, grid_spec=pltpu.PrefetchScalarGridSpec(num_scalar_...  37.2 us
    pallas_call x4, Pallas kernels, first(): pl.pallas_call(functools.partial(first_kernel, start, core), grid_spec=pl...  10.7 us
    unnamed x36, local copies, waits for them, and re-layouts  8.9 us
  transfers between devices with their start and end apart: 30, of which 11 were waited for; matrix products, arithmetic and copies ran while one was open for 6% of the time, Pallas kernels for 23%

commit v1 on v0

--- a/solution.py
+++ b/solution.py
@@ -25,6 +25,11 @@
 
 def swap(value, axis, size, mask):
     return lax.ppermute(value, axis, [(at, at ^ mask) for at in range(size)])
+
+
+def mask_at(position, chips):
+    half = chips // 2
+    return position % half * 2 + position // half
 
 
 def dot(left, right):
@@ -194,6 +199,10 @@
     return narrow(fold(dot(spread_rows(kept, nbr, per), moment.astype(BF))), blocks)
 
 
+def natural(position, tiles, place):
+    return (mask_at(position // CORES, tiles // CORES) * CORES + position % CORES) ^ place[0]
+
+
 def moment_rows_kernel(nbr, per, place, kept_ref, m_ref, out_ref):
     out_ref[0] = keep_rows(kept_ref[0], m_ref[0], nbr, per, m_ref.shape[2] // BLOCK)
 
@@ -206,11 +215,34 @@
         tiles,
         [
             (kept, (1, pair, BLOCK), lambda j, p: (j, 0, 0)),
-            (momentum, (1, rows, tile), lambda j, p: (0, 0, j ^ p[0])),
+            (momentum, (1, rows, tile), lambda j, p: (0, 0, natural(j, tiles, p))),
         ],
         [(shaped((tiles, pair // 2, BLOCK), F32), (1, pair // 2, BLOCK), lambda j, p: (j, 0, 0))],
         8,
         (2 * tiles * pair * rows * tile, 4 * rows * tile * tiles),
+        place,
+    )[0]
+
+
+def error_kernel(place, total_ref, goal_ref, *refs):
+    *found, out_ref = refs
+    total = total_ref[...] - goal_ref[0].astype(F32)
+    for ref in found:
+        total = total + ref[...].astype(F32)
+    out_ref[...] = total.astype(BF)
+
+
+def error_of(place, total, found, targets, step):
+    shape = total.shape
+    whole = lambda j, p: (0, 0)
+    return call(
+        error_kernel,
+        1,
+        [(total, shape, whole), (targets, (1,) + shape, lambda j, p: (step, 0, 0))]
+        + [(piece, shape, whole) for piece in found],
+        [(shaped(shape, BF), shape, whole)],
+        6,
+        (4 * total.size, 12 * total.size),
         place,
     )[0]
 
@@ -224,16 +256,17 @@
         sent_ref[q] = value.astype(BF)
 
 
-def coefficients(place, proj, errors, old):
+def coefficients(place, proj, errors, old, position):
     tiles = len(errors)
     tokens, tile = errors[0].shape
     pair = proj.shape[1]
     shape = (tiles, pair // 2, BLOCK)
+    at = lambda j, p: (position, 0, 0)
     whole = lambda j, p: (0, 0, 0)
     return call(
         functools.partial(coef_kernel, 1.0 / tokens),
         1,
-        [(proj, (tiles, pair, tokens), whole), (old, shape, whole)]
+        [(proj, (tiles, pair, tokens), at), (old, shape, at)]
         + [(piece, piece.shape, lambda j, p: (0, 0)) for piece in errors],
         [(shaped(shape, F32), shape, whole), (shaped(shape, BF), shape, whole)],
         8,
@@ -258,20 +291,22 @@
         refs[1][0] = keep_rows(kept_ref[0], new, nbr, per, new.shape[1] // BLOCK)
 
 
-def momentum_step(place, acts_t, errors, moment, own_dec, coef, per, start, kept_next, total, previous):
+def momentum_step(
+    place, acts_t, errors, moment, own_dec, coef, per, start, kept_next, total, previous
+):
     rows, tokens = acts_t.shape
     tiles, _, tile = errors.shape
     nbr = rows // BLOCK
     follow = kept_next is not None
     each = lambda j, p: (start + j, 0, 0)
     here = lambda j, p: (j, 0, 0)
-    natural = lambda j, p: (0, 0, (start + j) ^ p[0])
+    columns = lambda j, p: (0, 0, natural(start + j, total // tile, p))
     ins = [
         (acts_t, acts_t.shape, lambda j, p: (0, 0)),
         (errors, (1, tokens, tile), here),
-        (moment, (1, rows, tile), natural if moment.shape[0] == 1 else each),
+        (moment, (1, rows, tile), columns if moment.shape[0] == 1 else each),
         (own_dec, (1,) + own_dec.shape[1:], each),
-        (coef, (1,) + coef.shape[1:], each),
+        (coef, (1,) + coef.shape[1:], here),
     ]
     outs = []
     if follow:
@@ -279,7 +314,7 @@
         outs.append((shaped((tiles, rows, tile), F32), (1, rows, tile), here))
         outs.append((shaped(coef.shape, F32), (1,) + coef.shape[1:], here))
     else:
-        outs.append((shaped((1, rows, total), F32), (1, rows, tile), natural))
+        outs.append((shaped((1, rows, total), F32), (1, rows, tile), columns))
     return call(
         functools.partial(momentum_kernel, 1.0 / tokens, nbr, per, follow),
         tiles,
@@ -301,26 +336,29 @@
     return (weight.astype(F32) - 0.1 * change).astype(BF)
 
 
-def first_kernel(start, core, place, w_ref, x_ref, out_ref, w_buf, x_buf, sum_ref, sems):
+def first_kernel(chips, start, core, place, w_ref, x_ref, out_ref, w_buf, x_buf, sum_ref, sems):
     count, rows, tile = w_buf.shape
     step = x_buf.shape[2]
     copies = []
     for k in range(rows // step):
         span = slice(k * step, (k + 1) * step)
-        copies.append([pltpu.make_async_copy(x_ref.at[0, :, span], x_buf.at[k], sems.at[k, count])])
+        copies.append([])
         for at in range(count):
-            column = ((CORES * (start + at) + core) ^ place[0]) * tile
+            column = natural(CORES * (start + at) + core, CORES * chips, place) * tile
             source = w_ref.at[span, pl.ds(pl.multiple_of(column, tile), tile)]
             target = w_buf.at[at, span, :]
             copies[k].append(pltpu.make_async_copy(source, target, sems.at[k, at]))
+        source = x_ref.at[0, :, span]
+        copies[k].append(pltpu.make_async_copy(source, x_buf.at[k], sems.at[k, count]))
     for group in copies:
         for copy in group:
             copy.start()
     for k, group in enumerate(copies):
-        group[0].wait()
+        span = slice(k * step, (k + 1) * step)
+        for copy in group:
+            copy.wait()
         for at in range(count):
-            group[at + 1].wait()
-            part = dot(x_buf[k], w_buf[at, k * step : (k + 1) * step, :])
+            part = dot(x_buf[k], w_buf[at, span, :])
             if k > 0:
                 part = part + sum_ref[at]
             if k < len(copies) - 1:
@@ -333,12 +371,13 @@
     rows = weight.shape[0]
     tokens = acts.shape[1]
     step = 256
+    hbm = pl.BlockSpec(memory_space=pltpu.HBM)
     return pl.pallas_call(
-        functools.partial(first_kernel, start, core),
+        functools.partial(first_kernel, weight.shape[1] // tile // CORES, start, core),
         grid_spec=pltpu.PrefetchScalarGridSpec(
             num_scalar_prefetch=1,
             grid=(1,),
-            in_specs=[pl.BlockSpec(memory_space=pltpu.HBM)] * 2,
+            in_specs=[hbm, hbm],
             out_specs=pl.BlockSpec((count, tokens, tile), lambda j, p: (0, 0, 0)),
             scratch_shapes=[
                 pltpu.VMEM((count, rows, tile), BF),
@@ -366,12 +405,12 @@
     tokens = acts.shape[1]
     at = lambda j: CORES * (start + j) + core
     ins = [
-        (weight, (rows, tile), lambda j, p: (0, at(j) ^ p[0])),
+        (weight, (rows, tile), lambda j, p: (0, natural(at(j), weight.shape[1] // tile, p))),
         (acts, (1, tokens, rows), lambda j, p: (step, 0, 0)),
         (basis, (1,) + basis.shape[1:], lambda j, p: (at(j), 0, 0)),
     ]
     for coef in coefs:
-        ins.append((coef, (1,) + coef.shape[1:], lambda j, p: (at(j), 0, 0)))
+        ins.append((coef, (1,) + coef.shape[1:], lambda j, p: (CORES * j + core, 0, 0)))
     product = (shaped((count, tokens, tile), BF), (1, tokens, tile), lambda j, p: (j, 0, 0))
     new = (shaped((count, rows, tile), BF), (1, rows, tile), lambda j, p: (j, 0, 0))
     return call(
@@ -408,8 +447,14 @@
             (send, (1, rows, tile), each),
             (basis, (1,) + basis.shape[1:], lambda j, p: (CORES * start + j, 0, 0)),
         ]
-        + [(coef, (1,) + coef.shape[1:], lambda j, p: (CORES * start + j, 0, 0)) for coef in coefs],
-        [(shaped((rows, total), BF), (rows, tile), lambda j, p: (0, (CORES * start + j) ^ p[0]))],
+        + [(coef, (1,) + coef.shape[1:], lambda j, p: (j, 0, 0)) for coef in coefs],
+        [
+            (
+                shaped((rows, total), BF),
+                (rows, tile),
+                lambda j, p: (0, natural(CORES * start + j, total // tile, p)),
+            )
+        ],
         12,
         (2 * rows * 256 * tile * count * CORES, 4 * rows * tile * count * CORES),
         place,
@@ -430,7 +475,8 @@
     picks = indices[step].reshape((2,) * rep_bits + (nbr,) + (2,) * tp_bits + (per,))
     picks = by_distance(picks, range(rep_bits), replica)
     picks = by_distance(picks, range(rep_bits + 1, rep_bits + 1 + tp_bits), tp)
-    picks = picks.reshape(reps, nbr, parts, per).transpose(2, 0, 1, 3)
+    picks = picks.reshape(reps, nbr, parts // CORES // 2, 2, CORES, per)
+    picks = picks.transpose(3, 2, 4, 0, 1, 5)
     picks = picks.reshape(parts, reps, nbr * per)
     both = jnp.concatenate([picks, picks + BLOCK], axis=2)
     own = jnp.concatenate([both[:, 0], picks[:, 0]], axis=1)
@@ -452,23 +498,24 @@
     place = tp[None]
 
     acts_t, tables, projected = [None] * STEPS, [None] * STEPS, [None] * STEPS
-
-    def basis_work(step, picked):
-        picks_all, picks_own, per = pick_tables(picked, step, reps, parts, replica, tp)
-        tables[step] = prep(place, picks_all, picks_own)
-        projected[step], acts_t[step] = project(
-            place, tables[step][2], inputs, step, nbr, per
-        )
-        return per
+    chunks = (0, 1)
+    mask_of = [mask_at(position, chips) for position in range(chips)]
+
+    def basis_work(picked):
+        for step in range(STEPS):
+            picks_all, picks_own, per = pick_tables(picked, step, reps, parts, replica, tp)
+            tables[step] = prep(place, picks_all, picks_own)
+            projected[step], acts_t[step] = project(place, tables[step][2], inputs, step, nbr, per)
+        return moment_rows(place, tables[0][2], momentum, tile, per), per
 
     moment = momentum
-    gathered = None
+    gathered = [None, None]
     weights = [[None, None], [None, None]]
     final_m = final_w = None
     for step in range(STEPS):
         last = step == STEPS - 1
-        totals = [None] * chips
-        for chunk in (1, 0):
+        found_all = []
+        for chunk in chunks:
             start = chunk * count
             found = [None, None]
             for core in (1, 0):
@@ -486,35 +533,41 @@
                         core,
                         count,
                         tables[step - 1][0],
-                        gathered,
+                        gathered[chunk],
                     )
                 if core == 1:
                     other = swap(found[1], "tp", parts, 1)
-            for at in range(count):
-                total = found[0][at].astype(F32) + other[at].astype(F32)
-                totals[start + at] = total if start + at == 0 else total.astype(BF)
-            if step == 0 and chunk == 1:
-                *totals[count:], late = lax.optimization_barrier((*totals[count:], indices))
-                for at in range(STEPS):
-                    per = basis_work(at, late)
-                old = moment_rows(place, tables[0][2], momentum, tile, per)
-        total = totals[0] - targets[step].astype(F32)
-        for mask in range(1, chips):
-            total = total + swap(totals[mask], "tp", parts, mask * CORES).astype(F32)
-        errors = lax.optimization_barrier(total.astype(BF))
-        pieces = [errors] + [swap(errors, "tp", parts, mask * CORES) for mask in range(1, chips)]
-        pairs = []
-        for piece in pieces:
-            pairs += [piece, swap(piece, "tp", parts, 1)]
-        exact, sent = coefficients(place, projected[step], pairs, old)
-        gathered = [sent] + [swap(sent, "rep", reps, mask) for mask in range(1, reps)]
+            sums = [found[0][at].astype(F32) + other[at].astype(F32) for at in range(count)]
+            if chunk == 0:
+                total, sums = sums[0], [None] + [value.astype(BF) for value in sums[1:]]
+                if step == 0:
+                    *sums[1:], late = lax.optimization_barrier((*sums[1:], indices))
+                    old, per = basis_work(late)
+            for at, value in enumerate(sums):
+                mask = mask_of[start + at]
+                if mask:
+                    found_all.append(swap(value.astype(BF), "tp", parts, mask * CORES))
+        errors = error_of(place, total, found_all, targets, step)
+        pairs, exact, sent = [], [], []
+        for position, mask in enumerate(mask_of):
+            piece = errors
+            if mask:
+                piece = swap(errors, "tp", parts, mask * CORES)
+            pair = [piece, swap(piece, "tp", parts, 1)]
+            value, small = coefficients(place, projected[step], pair, old, position)
+            pairs += pair
+            exact.append(value)
+            sent.append(small)
+        for chunk in chunks:
+            both = jnp.concatenate(sent[chunk * count : (chunk + 1) * count])
+            gathered[chunk] = [both] + [swap(both, "rep", reps, mask) for mask in range(1, reps)]
         update = functools.partial(momentum_step, place, acts_t[step])
         if not last:
             moment, old = update(
                 jnp.stack(pairs),
                 moment,
                 tables[step][1],
-                exact,
+                jnp.concatenate(exact),
                 per,
                 0,
                 tables[step + 1][2],
@@ -522,36 +575,25 @@
                 None,
             )
         else:
-            early, _ = coefficients(place, projected[step], pairs[:CORES], old)
-            (final_m,) = update(
-                jnp.stack(pairs[:CORES]),
-                moment,
-                tables[step][1],
-                early,
-                per,
-                0,
-                None,
-                cols,
-                None,
-            )
-            (final_m,) = update(
-                jnp.stack(pairs[CORES:]),
-                moment,
-                tables[step][1],
-                exact,
-                per,
-                CORES,
-                None,
-                cols,
-                final_m,
-            )
-    for chunk in (0, 1):
+            for chunk in chunks:
+                (final_m,) = update(
+                    jnp.stack(pairs[chunk * count * CORES : (chunk + 1) * count * CORES]),
+                    moment,
+                    tables[step][1],
+                    jnp.concatenate(exact[chunk * count : (chunk + 1) * count]),
+                    per,
+                    chunk * count * CORES,
+                    None,
+                    cols,
+                    final_m,
+                )
+    for chunk in chunks:
         final_w = finish(
             place,
             weights[chunk][0],
             weights[chunk][1],
             tables[STEPS - 1][0],
-            gathered,
+            gathered[chunk],
             per,
             chunk * count,
             cols,

time: 157 us -> 157 us (level)
  waiting for transfers between devices: 51.1 us -> 62.1 us
  local copies, waits for them, and re-layouts: 11.6 us -> 5.56 us
  other arithmetic: 5.82 us -> 3.92 us
  Pallas kernels: 47.9 us -> 46 us
    ppermute x30 -> x36, waiting for transfers between devices: 51.1 us -> 62.1 us  [swap(): return lax.ppermute(value, axis, [(at, at ^ mask) for at in range(size)])]
    unnamed x36 -> x29, local copies, waits for them, and re-layouts: 8.9 us -> 4.41 us
    pallas_call x4, Pallas kernels: 10.7 us -> 9.01 us  [first(): pl.pallas_call(functools.partial(first_kernel, weight.shape[1] // tile //...]
    convert_element_type x6 -> x3, other arithmetic: 3.89 us -> 2.19 us  [the longest x2 2.08 us: steps(): found_all.append(swap(value.astype(BF), 'tp', parts, mask * CORES))]
    ppermute x30 -> x36, starting transfers between devices: 39.1 us -> 38 us  [swap(): return lax.ppermute(value, axis, [(at, at ^ mask) for at in range(size)])]
    pallas_call x17 -> x24, Pallas kernels: 37.2 us -> 37 us  [call(): pl.pallas_call(kernel, grid_spec=pltpu.PrefetchScalarGridSpec(num_scalar_...]
  transfers between devices with their start and end apart: 30 -> 36, of which waited for: 11 -> 12; matrix products, arithmetic and copies ran while one was open for 6% -> 3% of each run, Pallas kernels for 23% -> 26%
where the time goes in v1:
time: 157 us
  waiting for transfers between devices  62.1 us (40%)
  Pallas kernels  46 us (29%)
  starting transfers between devices  38 us (24%)
  local copies, waits for them, and re-layouts  5.56 us (4%)
  other arithmetic  3.92 us (2%)
    ppermute x36, waiting for transfers between devices, swap(): return lax.ppermute(value, axis, [(at, at ^ mask) for at in range(size)])  62.1 us
    ppermute x36, starting transfers between devices, swap(): return lax.ppermute(value, axis, [(at, at ^ mask) for at in range(size)])  38 us
    pallas_call x24, Pallas kernels, call(): pl.pallas_call(kernel, grid_spec=pltpu.PrefetchScalarGridSpec(num_scalar_...  37 us
    pallas_call x4, Pallas kernels, first(): pl.pallas_call(functools.partial(first_kernel, weight.shape[1] // tile //...  9.01 us
    unnamed x29, local copies, waits for them, and re-layouts  4.41 us
  transfers between devices with their start and end apart: 36, of which 12 were waited for; matrix products, arithmetic and copies ran while one was open for 3% of the time, Pallas kernels for 26%

profile of v1, /device:TPU:0, one launch (start us, length us, event | category | flops | bytes accessed | tf_op | source)
XLA Modules:
  0.0 156.9 jit_solution(11249153882858620804)
XLA Ops:
  0.6 2.0 %first.5 = bf16[2,512,256]{2,1,0:T(8,128)(2,1)S(1)} custom-call(s32[1]{0:T(128)} %bitcast.place, bf16[1024,2048]{1,0:T(8,128)(2,1)} %w_ref.15, bf16[2,512,1024]{2,1,0:T(8,128)(2,1)} %x_ref.19), custom_call_target="tpu_custom_call" | custom-call | flops 536870912 | bytes 2097152 | tf_op jit(solution)/shard_map/first/pallas_call | solution.py:375
  2.7 0.6 collective-permute-start
  3.2 2.8 %first.7 = bf16[2,512,256]{2,1,0:T(8,128)(2,1)} custom-call(s32[1]{0:T(128)} %bitcast.place, bf16[1024,2048]{1,0:T(8,128)(2,1)} %w_ref.15, bf16[2,512,1024]{2,1,0:T(8,128)(2,1)} %x_ref.19), custom_call_target="tpu_custom_call" | custom-call | flops 536870912 | bytes 2097152 | tf_op jit(solution)/shard_map/first/pallas_call | solution.py:375
  6.2 2.0 %first.6 = bf16[2,512,256]{2,1,0:T(8,128)(2,1)S(1)} custom-call(s32[1]{0:T(128)} %bitcast.place, bf16[1024,2048]{1,0:T(8,128)(2,1)} %w_ref.15, bf16[2,512,1024]{2,1,0:T(8,128)(2,1)} %x_ref.19), custom_call_target="tpu_custom_call" | custom-call | flops 536870912 | bytes 2097152 | tf_op jit(solution)/shard_map/first/pallas_call | solution.py:375
  8.3 2.1 %first.4 = bf16[2,512,256]{2,1,0:T(8,128)(2,1)S(1)} custom-call(s32[1]{0:T(128)} %bitcast.place, bf16[1024,2048]{1,0:T(8,128)(2,1)} %w_ref.15, bf16[2,512,1024]{2,1,0:T(8,128)(2,1)} %x_ref.19), custom_call_target="tpu_custom_call" | custom-call | flops 536870912 | bytes 2097152 | tf_op jit(solution)/shard_map/first/pallas_call | solution.py:375
  10.3 0.8 add_bitcast_fusion.1
  11.5 0.3 copy.15
  12.2 0.3 copy.20
  12.6 4.1 %collective-permute-start.1 = (bf16[512,256]{1,0:T(8,128)(2,1)}, bf16[512,256]{1,0:T(8,128)(2,1)S(1)}, u32[]{:S(2)}, u32[]{:S(2)}) collective-permute-start(bf16[512,256]{1,0:T(8,128)(2,1)} %get-tuple-element.44), channel_id=1, source_target_pairs={{0,4},{1,5},{2,6},{3,7},{4,0},{5,1},{6,2},{7,3},{8,12},{9,13},{10,... | collective-permute-start | bytes 786440 | tf_op jit(solution)/shard_map/ppermute | solution.py:27
  16.8 1.9 %fusion.2 = (bf16[512,256]{1,0:T(8,128)(2,1)}, bf16[512,256]{1,0:T(8,128)(2,1)}) fusion(bf16[2,512,256]{2,1,0:T(8,128)(2,1)} %collective-permute-done.2, bf16[2,512,256]{2,1,0:T(8,128)(2,1)S(1)} %first.6), kind=kLoop, calls=%fused_computation.12 | loop fusion | flops 1048576 | bytes 1572864 | tf_op jit(solution)/shard_map/convert_element_type | solution.py:549
  18.7 1.3 collective-permute-start.4
  20.1 0.2 collective-permute-start.3
  20.6 0.8 copy-done.5
  21.4 1.6 %shard_map.112 = (bf16[8,128,256]{2,1,0:T(8,128)(2,1)S(1)}, bf16[8,128,96]{2,1,0:T(8,128)(2,1)S(1)}, bf16[8,64,128]{2,1,0:T(8,128)(2,1)S(1)}) custom-call(s32[1]{0:T(128)} %bitcast.place, s32[8,1,256]{2,1,0:T(1,128)S(1)} %reshape.67.all_ref, s32[8,1,96]{2,1,0:T(1,128)S(1)} %bitcast.77, bf16[128,256]{1,0:T(8,128)(2,1)S(1)} %copy-done.4, ...), custom_call_target="tpu_custom_call" | custom-call | flops 234881024 | bytes 2097152 | tf_op jit(solution)/shard_map/pallas_call | solution.py:59
  23.1 1.6 %shard_map.104 = (bf16[8,128,256]{2,1,0:T(8,128)(2,1)S(1)}, bf16[8,128,96]{2,1,0:T(8,128)(2,1)S(1)}, bf16[8,64,128]{2,1,0:T(8,128)(2,1)S(1)}) custom-call(s32[1]{0:T(128)} %bitcast.place, s32[8,1,256]{2,1,0:T(1,128)S(1)} %reshape.66.all_ref, s32[8,1,96]{2,1,0:T(1,128)S(1)} %bitcast.78, bf16[128,256]{1,0:T(8,128)(2,1)S(1)} %copy-done.4, ...), custom_call_target="tpu_custom_call" | custom-call | flops 234881024 | bytes 2097152 | tf_op jit(solution)/shard_map/pallas_call | solution.py:59
  24.7 0.8 shard_map.105
  25.5 0.8 shard_map.113
  26.4 9.0 %collective-permute-done.1.refs_0_ = bf16[512,256]{1,0:T(8,128)(2,1)S(1)} collective-permute-done((bf16[512,256]{1,0:T(8,128)(2,1)}, bf16[512,256]{1,0:T(8,128)(2,1)S(1)}, u32[]{:S(2)}, u32[]{:S(2)}) %collective-permute-start.1) | collective-permute-done | bytes 262176 | tf_op jit(solution)/shard_map/ppermute | solution.py:27
  35.3 2.7 %collective-permute-done.3.refs_1_ = bf16[512,256]{1,0:T(8,128)(2,1)S(1)} collective-permute-done((bf16[512,256]{1,0:T(8,128)(2,1)}, bf16[512,256]{1,0:T(8,128)(2,1)S(1)}, u32[]{:S(2)}, u32[]{:S(2)}) %collective-permute-start.3) | collective-permute-done | bytes 262176 | tf_op jit(solution)/shard_map/ppermute | solution.py:27
  38.2 5.0 %collective-permute-start.13 = (bf16[512,256]{1,0:T(8,128)(2,1)S(1)}, bf16[512,256]{1,0:T(8,128)(2,1)S(1)}, u32[]{:S(2)}, u32[]{:S(2)}) collective-permute-start(bf16[512,256]{1,0:T(8,128)(2,1)S(1)} %shard_map.107.refs_0_), channel_id=1, source_target_pairs={{0,4},{1,5},{2,6},{3,7},{4,0},{5,1},{6,2},{7,3},{8,12},{9,13},{10,... | collective-permute-start | bytes 786440 | tf_op jit(solution)/shard_map/ppermute | solution.py:27
  43.2 0.5 collective-permute-start.7
  43.9 3.4 %copy-done.2 = f32[1,1024,2048]{2,1,0:T(8,128)S(1)} copy-done((f32[1,1024,2048]{2,1,0:T(8,128)S(1)}, f32[1,1024,2048]{2,1,0:T(8,128)}, u32[]{:S(2)}) %copy-start.2) | copy-done | bytes 8388632
  47.3 2.4 %shard_map.106.old_ref = f32[8,32,128]{2,1,0:T(8,128)S(1)} custom-call(s32[1]{0:T(128)} %bitcast.place, bf16[8,64,128]{2,1,0:T(8,128)(2,1)S(1)} %get-tuple-element.42.kept_ref, f32[1,1024,2048]{2,1,0:T(8,128)S(1)} %copy-done.2), custom_call_target="tpu_custom_call" | custom-call | flops 268435456 | bytes 8388608 | tf_op jit(solution)/shard_map/pallas_call | solution.py:59
  49.7 11.6 %collective-permute-done.13.refs_0_ = bf16[512,256]{1,0:T(8,128)(2,1)S(1)} collective-permute-done((bf16[512,256]{1,0:T(8,128)(2,1)S(1)}, bf16[512,256]{1,0:T(8,128)(2,1)S(1)}, u32[]{:S(2)}, u32[]{:S(2)}) %collective-permute-start.13) | collective-permute-done | bytes 262176 | tf_op jit(solution)/shard_map/ppermute | solution.py:27
  61.3 0.5 collective-permute-start.8
  61.8 1.2 collective-permute-done.5.refs_0_
  63.3 0.2 shard_map.109
  63.6 1.0 collective-permute-done.6.refs_1_
  64.5 0.2 shard_map.108
  64.8 2.5 %collective-permute-start.11 = (bf16[4,32,128]{2,1,0:T(8,128)(2,1)S(1)}, bf16[4,32,128]{2,1,0:T(8,128)(2,1)S(1)}, u32[]{:S(2)}, u32[]{:S(2)}) collective-permute-start(bf16[4,32,128]{2,1,0:T(8,128)(2,1)S(1)} %constant_dynamic-update-slice_fusion.refs_0_), channel_id=1, source_target_pairs={{0,24},{8,16},{16,8},{24,0},{1,25},{9,17},{17,9},{25,1},{2,26},{10... | collective-permute-start | bytes 98312 | tf_op jit(solution)/shard_map/ppermute | solution.py:27
  67.3 0.5 collective-permute-start.10
  67.8 0.5 collective-permute-start.9
  68.4 0.2 shard_map.115
  68.6 2.5 %collective-permute-start.17 = (bf16[4,32,128]{2,1,0:T(8,128)(2,1)S(1)}, bf16[4,32,128]{2,1,0:T(8,128)(2,1)S(1)}, u32[]{:S(2)}, u32[]{:S(2)}) collective-permute-start(bf16[4,32,128]{2,1,0:T(8,128)(2,1)S(1)} %constant_dynamic-update-slice_fusion.2.refs_0_), channel_id=1, source_target_pairs={{0,24},{8,16},{16,8},{24,0},{1,25},{9,17},{17,9},{25,1},{2,26},{10... | collective-permute-start | bytes 98312 | tf_op jit(solution)/shard_map/ppermute | solution.py:27
  71.1 0.5 collective-permute-start.16
  71.6 0.5 collective-permute-start.15
  72.2 2.0 %shard_map.111 = (bf16[2,1024,256]{2,1,0:T(8,128)(2,1)S(1)}, bf16[2,512,256]{2,1,0:T(8,128)(2,1)S(1)}) custom-call(s32[1]{0:T(128)} %bitcast.place, bf16[1024,2048]{1,0:T(8,128)(2,1)S(1)} %copy-done, bf16[2,512,1024]{2,1,0:T(8,128)(2,1)S(1)} %copy-done.1, bf16[8,128,256]{2,1,0:T(8,128)(2,1)S(1)} %get-tuple-element.41.dec_ref, ...), custom_call_target="tpu_custom_call" | custom-call | flops 536870912 | bytes 2097152 | tf_op jit(solution)/shard_map/pallas_call | solution.py:59
  74.3 0.8 collective-permute-done.16.refs_2_
  75.0 0.5 collective-permute-done.15.refs_1_
  75.5 1.9 %shard_map.118 = (bf16[2,1024,256]{2,1,0:T(8,128)(2,1)S(1)}, bf16[2,512,256]{2,1,0:T(8,128)(2,1)S(1)}) custom-call(s32[1]{0:T(128)} %bitcast.place, bf16[1024,2048]{1,0:T(8,128)(2,1)S(1)} %copy-done, bf16[2,512,1024]{2,1,0:T(8,128)(2,1)S(1)} %copy-done.1, bf16[8,128,256]{2,1,0:T(8,128)(2,1)S(1)} %get-tuple-element.41.dec_ref, ...), custom_call_target="tpu_custom_call" | custom-call | flops 536870912 | bytes 2097152 | tf_op jit(solution)/shard_map/pallas_call | solution.py:59
  77.6 2.0 %shard_map.110 = (bf16[2,1024,256]{2,1,0:T(8,128)(2,1)S(1)}, bf16[2,512,256]{2,1,0:T(8,128)(2,1)S(1)}) custom-call(s32[1]{0:T(128)} %bitcast.place, bf16[1024,2048]{1,0:T(8,128)(2,1)S(1)} %copy-done, bf16[2,512,1024]{2,1,0:T(8,128)(2,1)S(1)} %copy-done.1, bf16[8,128,256]{2,1,0:T(8,128)(2,1)S(1)} %get-tuple-element.41.dec_ref, ...), custom_call_target="tpu_custom_call" | custom-call | flops 536870912 | bytes 2097152 | tf_op jit(solution)/shard_map/pallas_call | solution.py:59
  79.6 2.0 %shard_map.117 = (bf16[2,1024,256]{2,1,0:T(8,128)(2,1)S(1)}, bf16[2,512,256]{2,1,0:T(8,128)(2,1)S(1)}) custom-call(s32[1]{0:T(128)} %bitcast.place, bf16[1024,2048]{1,0:T(8,128)(2,1)S(1)} %copy-done, bf16[2,512,1024]{2,1,0:T(8,128)(2,1)S(1)} %copy-done.1, bf16[8,128,256]{2,1,0:T(8,128)(2,1)S(1)} %get-tuple-element.41.dec_ref, ...), custom_call_target="tpu_custom_call" | custom-call | flops 536870912 | bytes 2097152 | tf_op jit(solution)/shard_map/pallas_call | solution.py:59
  81.7 0.9 collective-permute-start.22
  82.6 3.7 %collective-permute-start.21 = (bf16[512,256]{1,0:T(8,128)(2,1)S(1)}, bf16[512,256]{1,0:T(8,128)(2,1)S(1)}, u32[]{:S(2)}, u32[]{:S(2)}) collective-permute-start(bf16[512,256]{1,0:T(8,128)(2,1)S(1)} %get-tuple-element.79), channel_id=1, source_target_pairs={{0,2},{1,3},{2,0},{3,1},{4,6},{5,7},{6,4},{7,5},{8,10},{9,11},{10,... | collective-permute-start | bytes 786440 | tf_op jit(solution)/shard_map/ppermute | solution.py:27
  86.4 1.5 collective-permute-start.19
  87.9 4.9 %collective-permute-done.22.refs_2_ = bf16[512,256]{1,0:T(8,128)(2,1)S(1)} collective-permute-done((bf16[512,256]{1,0:T(8,128)(2,1)S(1)}, bf16[512,256]{1,0:T(8,128)(2,1)S(1)}, u32[]{:S(2)}, u32[]{:S(2)}) %collective-permute-start.22) | collective-permute-done | bytes 262176 | tf_op jit(solution)/shard_map/ppermute | solution.py:27
  92.8 5.1 %collective-permute-done.21.refs_1_ = bf16[512,256]{1,0:T(8,128)(2,1)S(1)} collective-permute-done((bf16[512,256]{1,0:T(8,128)(2,1)S(1)}, bf16[512,256]{1,0:T(8,128)(2,1)S(1)}, u32[]{:S(2)}, u32[]{:S(2)}) %collective-permute-start.21) | collective-permute-done | bytes 262176 | tf_op jit(solution)/shard_map/ppermute | solution.py:27
  97.9 11.2 %collective-permute-done.19.refs_0_ = bf16[512,256]{1,0:T(8,128)(2,1)S(1)} collective-permute-done((bf16[512,256]{1,0:T(8,128)(2,1)S(1)}, bf16[512,256]{1,0:T(8,128)(2,1)S(1)}, u32[]{:S(2)}, u32[]{:S(2)}) %collective-permute-start.19) | collective-permute-done | bytes 262176 | tf_op jit(solution)/shard_map/ppermute | solution.py:27
  109.3 0.9 collective-permute-start.25
  110.2 3.6 %collective-permute-start.31 = (bf16[512,256]{1,0:T(8,128)(2,1)S(1)}, bf16[512,256]{1,0:T(8,128)(2,1)S(1)}, u32[]{:S(2)}, u32[]{:S(2)}) collective-permute-start(bf16[512,256]{1,0:T(8,128)(2,1)S(1)} %shard_map.119.refs_0_), channel_id=1, source_target_pairs={{0,4},{1,5},{2,6},{3,7},{4,0},{5,1},{6,2},{7,3},{8,12},{9,13},{10,... | collective-permute-start | bytes 786440 | tf_op jit(solution)/shard_map/ppermute | solution.py:27
  113.8 6.5 %collective-permute-done.25.refs_0_ = bf16[512,256]{1,0:T(8,128)(2,1)S(1)} collective-permute-done((bf16[512,256]{1,0:T(8,128)(2,1)S(1)}, bf16[512,256]{1,0:T(8,128)(2,1)S(1)}, u32[]{:S(2)}, u32[]{:S(2)}) %collective-permute-start.25) | collective-permute-done | bytes 262176 | tf_op jit(solution)/shard_map/ppermute | solution.py:27
  120.4 7.6 %collective-permute-done.23.refs_0_ = bf16[512,256]{1,0:T(8,128)(2,1)S(1)} collective-permute-done((bf16[512,256]{1,0:T(8,128)(2,1)S(1)}, bf16[512,256]{1,0:T(8,128)(2,1)S(1)}, u32[]{:S(2)}, u32[]{:S(2)}) %collective-permute-start.23) | collective-permute-done | bytes 262176 | tf_op jit(solution)/shard_map/ppermute | solution.py:27
  128.0 7.1 %shard_map.116 = (f32[8,1024,256]{2,1,0:T(8,128)S(1)}, f32[8,32,128]{2,1,0:T(8,128)S(1)}) custom-call(s32[1]{0:T(128)} %bitcast.place, bf16[1024,512]{1,0:T(8,128)(2,1)S(1)} %get-tuple-element.52.xt_ref, bf16[8,512,256]{2,1,0:T(8,128)(2,1)S(1)} %bitcast_dynamic-update-slice_fusion.e_ref, f32[1,1024,2048]{2,1,0:T(8,128)S(1)} %bitcast.68, ...), custom_call_target="tpu_custom_call" | custom-call | flops 2147483648 | bytes 16777216 | tf_op jit(solution)/shard_map/pallas_call | solution.py:59
  135.1 0.5 collective-permute-start.32
  136.4 1.5 collective-permute-start.29
  137.9 0.5 collective-permute-start.28
  138.7 2.5 %collective-permute-start.35 = (bf16[4,32,128]{2,1,0:T(8,128)(2,1)S(1)}, bf16[4,32,128]{2,1,0:T(8,128)(2,1)S(1)}, u32[]{:S(2)}, u32[]{:S(2)}) collective-permute-start(bf16[4,32,128]{2,1,0:T(8,128)(2,1)S(1)} %constant_dynamic-update-slice_fusion.6.refs_0_), channel_id=1, source_target_pairs={{0,24},{8,16},{16,8},{24,0},{1,25},{9,17},{17,9},{25,1},{2,26},{10... | collective-permute-start | bytes 98312 | tf_op jit(solution)/shard_map/ppermute | solution.py:27
  141.2 0.5 collective-permute-start.34
  141.7 0.5 collective-permute-start.33
  142.5 3.8 %shard_map.126.refs_0_ = f32[1,1024,2048]{2,1,0:T(8,128)} custom-call(s32[1]{0:T(128)} %bitcast.place, bf16[1024,512]{1,0:T(8,128)(2,1)S(1)} %get-tuple-element.71.xt_ref, bf16[4,512,256]{2,1,0:T(8,128)(2,1)S(1)} %pad_maximum_fusion.1.e_ref, f32[8,1024,256]{2,1,0:T(8,128)S(1)} %get-tuple-element.72.m_ref, bf16[8,128,96]{2,1,0:T(8,128)(2,1)S(1)} %get-tuple-element.73.dec_ref, ...), custom_call_target="tpu_custom_call" | custom-call | flops 1073741824 | bytes 8388608 | tf_op jit(solution)/shard_map/pallas_call | solution.py:59
  146.3 3.7 %shard_map.127 = f32[1,1024,2048]{2,1,0:T(8,128)} custom-call(s32[1]{0:T(128)} %bitcast.place, bf16[1024,512]{1,0:T(8,128)(2,1)S(1)} %get-tuple-element.71.xt_ref, bf16[4,512,256]{2,1,0:T(8,128)(2,1)S(1)} %pad_maximum_fusion.e_ref, f32[8,1024,256]{2,1,0:T(8,128)S(1)} %get-tuple-element.72.m_ref, ...), custom_call_target="tpu_custom_call", output_to_operand_aliasing={{}: (6, {})} | custom-call | flops 1073741824 | bytes 8388608 | tf_op jit(solution)/shard_map/pallas_call | solution.py:59
  150.0 1.5 collective-permute-start.27
  151.6 2.6 %shard_map.124.refs_4_ = bf16[1024,2048]{1,0:T(8,128)(2,1)} custom-call(s32[1]{0:T(128)} %bitcast.place, bf16[2,1024,256]{2,1,0:T(8,128)(2,1)S(1)} %get-tuple-element.67.keep_ref, bf16[2,1024,256]{2,1,0:T(8,128)(2,1)S(1)} %get-tuple-element.68.send_ref, bf16[8,128,256]{2,1,0:T(8,128)(2,1)S(1)} %get-tuple-element.49.dec_ref, ...), custom_call_target="tpu_custom_call" | custom-call | flops 536870912 | bytes 4194304 | tf_op jit(solution)/shard_map/pallas_call | solution.py:59
  154.2 2.7 %shard_map.125 = bf16[1024,2048]{1,0:T(8,128)(2,1)} custom-call(s32[1]{0:T(128)} %bitcast.place, bf16[2,1024,256]{2,1,0:T(8,128)(2,1)S(1)} %get-tuple-element.47.keep_ref, bf16[2,1024,256]{2,1,0:T(8,128)(2,1)S(1)} %get-tuple-element.48.send_ref, bf16[8,128,256]{2,1,0:T(8,128)(2,1)S(1)} %get-tuple-element.49.dec_ref, ...), custom_call_target="tpu_custom_call", output_to_operand_aliasing={{}: (8, {})} | custom-call | flops 536870912 | bytes 4194304 | tf_op jit(solution)/shard_map/pallas_call | solution.py:59
  (110 shorter events, 3.8 us)
Async XLA Ops:
  2.7 7.6 %collective-permute-start = (bf16[2,512,256]{2,1,0:T(8,128)(2,1)S(1)}, bf16[2,512,256]{2,1,0:T(8,128)(2,1)S(1)}, u32[]{:S(2)}, u32[]{:S(2)}) collective-permute-start(bf16[2,512,256]{2,1,0:T(8,128)(2,1)S(1)} %first.5), channel_id=1, source_target_pairs={{0,1},{1,0},{2,3},{3,2},{4,5},{5,4},{6,7},{7,6},{8,9},{9,8},{10,11... | collective-permute-start | bytes 1572872 | tf_op jit(solution)/shard_map/ppermute | solution.py:27
  6.1 10.7 %collective-permute-start.2 = (bf16[2,512,256]{2,1,0:T(8,128)(2,1)}, bf16[2,512,256]{2,1,0:T(8,128)(2,1)}, u32[]{:S(2)}, u32[]{:S(2)}) collective-permute-start(bf16[2,512,256]{2,1,0:T(8,128)(2,1)} %first.7), channel_id=1, source_target_pairs={{0,1},{1,0},{2,3},{3,2},{4,5},{5,4},{6,7},{7,6},{8,9},{9,8},{10,11... | collective-permute-start | bytes 1572872 | tf_op jit(solution)/shard_map/ppermute | solution.py:27
  8.2 2.9 %copy-start.6 = (s32[2,4,8,16,2]{3,4,2,1,0:T(2,128)S(1)}, s32[2,4,8,16,2]{3,4,2,1,0:T(2,128)}, u32[]{:S(2)}) copy-start(s32[2,4,8,16,2]{3,4,2,1,0:T(2,128)} %param.13) | copy-start | bytes 24580
  11.2 9.4 %copy-start.4 = (bf16[128,256]{1,0:T(8,128)(2,1)S(1)}, bf16[128,256]{1,0:T(8,128)(2,1)}, u32[]{:S(2)}) copy-start(bf16[128,256]{1,0:T(8,128)(2,1)} %constant.21.clone.cols_ref) | copy-start | bytes 196612
  12.1 12.6 %copy-start.1 = (bf16[2,512,1024]{2,1,0:T(8,128)(2,1)S(1)}, bf16[2,512,1024]{2,1,0:T(8,128)(2,1)}, u32[]{:S(2)}) copy-start(bf16[2,512,1024]{2,1,0:T(8,128)(2,1)} %x_ref.19) | copy-start | bytes 6291460
  12.6 22.7 %collective-permute-start.1 = (bf16[512,256]{1,0:T(8,128)(2,1)}, bf16[512,256]{1,0:T(8,128)(2,1)S(1)}, u32[]{:S(2)}, u32[]{:S(2)}) collective-permute-start(bf16[512,256]{1,0:T(8,128)(2,1)} %get-tuple-element.44), channel_id=1, source_target_pairs={{0,4},{1,5},{2,6},{3,7},{4,0},{5,1},{6,2},{7,3},{8,12},{9,13},{10,... | collective-permute-start | bytes 786440 | tf_op jit(solution)/shard_map/ppermute | solution.py:27
  18.7 16.6 %collective-permute-start.4 = (bf16[512,256]{1,0:T(8,128)(2,1)}, bf16[512,256]{1,0:T(8,128)(2,1)S(1)}, u32[]{:S(2)}, u32[]{:S(2)}) collective-permute-start(bf16[512,256]{1,0:T(8,128)(2,1)} %get-tuple-element.82), channel_id=1, source_target_pairs={{0,6},{1,7},{2,4},{3,5},{4,2},{5,3},{6,0},{7,1},{8,14},{9,15},{10,... | collective-permute-start | bytes 786440 | tf_op jit(solution)/shard_map/ppermute | solution.py:27
  20.1 18.0 %collective-permute-start.3 = (bf16[512,256]{1,0:T(8,128)(2,1)}, bf16[512,256]{1,0:T(8,128)(2,1)S(1)}, u32[]{:S(2)}, u32[]{:S(2)}) collective-permute-start(bf16[512,256]{1,0:T(8,128)(2,1)} %get-tuple-element.83), channel_id=1, source_target_pairs={{0,2},{1,3},{2,0},{3,1},{4,6},{5,7},{6,4},{7,5},{8,10},{9,11},{10,... | collective-permute-start | bytes 786440 | tf_op jit(solution)/shard_map/ppermute | solution.py:27
  20.6 0.8 copy-start.5
  24.7 13.3 %copy-start.3 = (bf16[2,512,256]{2,1,0:T(8,128)(2,1)S(1)}, bf16[2,512,256]{2,1,0:T(8,128)(2,1)}, u32[]{:S(2)}) copy-start(bf16[2,512,256]{2,1,0:T(8,128)(2,1)} %goal_ref.3) | copy-start | bytes 1572868
  38.2 23.1 %collective-permute-start.13 = (bf16[512,256]{1,0:T(8,128)(2,1)S(1)}, bf16[512,256]{1,0:T(8,128)(2,1)S(1)}, u32[]{:S(2)}, u32[]{:S(2)}) collective-permute-start(bf16[512,256]{1,0:T(8,128)(2,1)S(1)} %shard_map.107.refs_0_), channel_id=1, source_target_pairs={{0,4},{1,5},{2,6},{3,7},{4,0},{5,1},{6,2},{7,3},{8,12},{9,13},{10,... | collective-permute-start | bytes 786440 | tf_op jit(solution)/shard_map/ppermute | solution.py:27
  43.2 19.9 %collective-permute-start.12 = (bf16[512,256]{1,0:T(8,128)(2,1)S(1)}, bf16[512,256]{1,0:T(8,128)(2,1)S(1)}, u32[]{:S(2)}, u32[]{:S(2)}) collective-permute-start(bf16[512,256]{1,0:T(8,128)(2,1)S(1)} %shard_map.107.refs_0_), channel_id=1, source_target_pairs={{0,1},{1,0},{2,3},{3,2},{4,5},{5,4},{6,7},{7,6},{8,9},{9,8},{10,11... | collective-permute-start | bytes 786440 | tf_op jit(solution)/shard_map/ppermute | solution.py:27
  43.2 18.1 %collective-permute-start.7 = (bf16[512,256]{1,0:T(8,128)(2,1)S(1)}, bf16[512,256]{1,0:T(8,128)(2,1)S(1)}, u32[]{:S(2)}, u32[]{:S(2)}) collective-permute-start(bf16[512,256]{1,0:T(8,128)(2,1)S(1)} %shard_map.107.refs_0_), channel_id=1, source_target_pairs={{0,6},{1,7},{2,4},{3,5},{4,2},{5,3},{6,0},{7,1},{8,14},{9,15},{10,... | collective-permute-start | bytes 786440 | tf_op jit(solution)/shard_map/ppermute | solution.py:27
  43.7 19.3 %collective-permute-start.5 = (bf16[512,256]{1,0:T(8,128)(2,1)S(1)}, bf16[512,256]{1,0:T(8,128)(2,1)S(1)}, u32[]{:S(2)}, u32[]{:S(2)}) collective-permute-start(bf16[512,256]{1,0:T(8,128)(2,1)S(1)} %shard_map.107.refs_0_), channel_id=1, source_target_pairs={{0,2},{1,3},{2,0},{3,1},{4,6},{5,7},{6,4},{7,5},{8,10},{9,11},{10,... | collective-permute-start | bytes 786440 | tf_op jit(solution)/shard_map/ppermute | solution.py:27
  43.9 3.4 %copy-start.2 = (f32[1,1024,2048]{2,1,0:T(8,128)S(1)}, f32[1,1024,2048]{2,1,0:T(8,128)}, u32[]{:S(2)}) copy-start(f32[1,1024,2048]{2,1,0:T(8,128)} %m_ref.3) | copy-start | bytes 25165828
  61.3 7.1 %collective-permute-start.14 = (bf16[512,256]{1,0:T(8,128)(2,1)S(1)}, bf16[512,256]{1,0:T(8,128)(2,1)S(1)}, u32[]{:S(2)}, u32[]{:S(2)}) collective-permute-start(bf16[512,256]{1,0:T(8,128)(2,1)S(1)} %collective-permute-done.13.refs_0_), channel_id=1, source_target_pairs={{0,1},{1,0},{2,3},{3,2},{4,5},{5,4},{6,7},{7,6},{8,9},{9,8},{10,11... | collective-permute-start | bytes 786440 | tf_op jit(solution)/shard_map/ppermute | solution.py:27
  61.3 2.0 %collective-permute-start.8 = (bf16[512,256]{1,0:T(8,128)(2,1)S(1)}, bf16[512,256]{1,0:T(8,128)(2,1)S(1)}, u32[]{:S(2)}, u32[]{:S(2)}) collective-permute-start(bf16[512,256]{1,0:T(8,128)(2,1)S(1)} %collective-permute-done.7.refs_0_), channel_id=1, source_target_pairs={{0,1},{1,0},{2,3},{3,2},{4,5},{5,4},{6,7},{7,6},{8,9},{9,8},{10,11... | collective-permute-start | bytes 786440 | tf_op jit(solution)/shard_map/ppermute | solution.py:27
  63.0 1.5 collective-permute-start.6
  63.3 8.9 %copy-start = (bf16[1024,2048]{1,0:T(8,128)(2,1)S(1)}, bf16[1024,2048]{1,0:T(8,128)(2,1)}, u32[]{:S(2)}) copy-start(bf16[1024,2048]{1,0:T(8,128)(2,1)} %w_ref.15) | copy-start | bytes 12582916
  64.8 6.8 %collective-permute-start.11 = (bf16[4,32,128]{2,1,0:T(8,128)(2,1)S(1)}, bf16[4,32,128]{2,1,0:T(8,128)(2,1)S(1)}, u32[]{:S(2)}, u32[]{:S(2)}) collective-permute-start(bf16[4,32,128]{2,1,0:T(8,128)(2,1)S(1)} %constant_dynamic-update-slice_fusion.refs_0_), channel_id=1, source_target_pairs={{0,24},{8,16},{16,8},{24,0},{1,25},{9,17},{17,9},{25,1},{2,26},{10... | collective-permute-start | bytes 98312 | tf_op jit(solution)/shard_map/ppermute | solution.py:27
  67.3 4.8 %collective-permute-start.10 = (bf16[4,32,128]{2,1,0:T(8,128)(2,1)S(1)}, bf16[4,32,128]{2,1,0:T(8,128)(2,1)S(1)}, u32[]{:S(2)}, u32[]{:S(2)}) collective-permute-start(bf16[4,32,128]{2,1,0:T(8,128)(2,1)S(1)} %constant_dynamic-update-slice_fusion.refs_0_), channel_id=1, source_target_pairs={{0,16},{8,24},{16,0},{24,8},{1,17},{9,25},{17,1},{25,9},{2,18},{10... | collective-permute-start | bytes 98312 | tf_op jit(solution)/shard_map/ppermute | solution.py:27
  67.8 4.3 %collective-permute-start.9 = (bf16[4,32,128]{2,1,0:T(8,128)(2,1)S(1)}, bf16[4,32,128]{2,1,0:T(8,128)(2,1)S(1)}, u32[]{:S(2)}, u32[]{:S(2)}) collective-permute-start(bf16[4,32,128]{2,1,0:T(8,128)(2,1)S(1)} %constant_dynamic-update-slice_fusion.refs_0_), channel_id=1, source_target_pairs={{0,8},{8,0},{16,24},{24,16},{1,9},{9,1},{17,25},{25,17},{2,10},{10... | collective-permute-start | bytes 98312 | tf_op jit(solution)/shard_map/ppermute | solution.py:27
  68.6 5.7 %collective-permute-start.17 = (bf16[4,32,128]{2,1,0:T(8,128)(2,1)S(1)}, bf16[4,32,128]{2,1,0:T(8,128)(2,1)S(1)}, u32[]{:S(2)}, u32[]{:S(2)}) collective-permute-start(bf16[4,32,128]{2,1,0:T(8,128)(2,1)S(1)} %constant_dynamic-update-slice_fusion.2.refs_0_), channel_id=1, source_target_pairs={{0,24},{8,16},{16,8},{24,0},{1,25},{9,17},{17,9},{25,1},{2,26},{10... | collective-permute-start | bytes 98312 | tf_op jit(solution)/shard_map/ppermute | solution.py:27
  71.1 3.9 %collective-permute-start.16 = (bf16[4,32,128]{2,1,0:T(8,128)(2,1)S(1)}, bf16[4,32,128]{2,1,0:T(8,128)(2,1)S(1)}, u32[]{:S(2)}, u32[]{:S(2)}) collective-permute-start(bf16[4,32,128]{2,1,0:T(8,128)(2,1)S(1)} %constant_dynamic-update-slice_fusion.2.refs_0_), channel_id=1, source_target_pairs={{0,16},{8,24},{16,0},{24,8},{1,17},{9,25},{17,1},{25,9},{2,18},{10... | collective-permute-start | bytes 98312 | tf_op jit(solution)/shard_map/ppermute | solution.py:27
  71.6 3.9 %collective-permute-start.15 = (bf16[4,32,128]{2,1,0:T(8,128)(2,1)S(1)}, bf16[4,32,128]{2,1,0:T(8,128)(2,1)S(1)}, u32[]{:S(2)}, u32[]{:S(2)}) collective-permute-start(bf16[4,32,128]{2,1,0:T(8,128)(2,1)S(1)} %constant_dynamic-update-slice_fusion.2.refs_0_), channel_id=1, source_target_pairs={{0,8},{8,0},{16,24},{24,16},{1,9},{9,1},{17,25},{25,17},{2,10},{10... | collective-permute-start | bytes 98312 | tf_op jit(solution)/shard_map/ppermute | solution.py:27
  74.1 7.4 %collective-permute-start.20 = (bf16[2,512,256]{2,1,0:T(8,128)(2,1)S(1)}, bf16[2,512,256]{2,1,0:T(8,128)(2,1)S(1)}, u32[]{:S(2)}, u32[]{:S(2)}) collective-permute-start(bf16[2,512,256]{2,1,0:T(8,128)(2,1)S(1)} %get-tuple-element.64), channel_id=1, source_target_pairs={{0,1},{1,0},{2,3},{3,2},{4,5},{5,4},{6,7},{7,6},{8,9},{9,8},{10,11... | collective-permute-start | bytes 1572872 | tf_op jit(solution)/shard_map/ppermute | solution.py:27
  77.5 8.9 %collective-permute-start.18 = (bf16[2,512,256]{2,1,0:T(8,128)(2,1)S(1)}, bf16[2,512,256]{2,1,0:T(8,128)(2,1)S(1)}, u32[]{:S(2)}, u32[]{:S(2)}) collective-permute-start(bf16[2,512,256]{2,1,0:T(8,128)(2,1)S(1)} %get-tuple-element.62), channel_id=1, source_target_pairs={{0,1},{1,0},{2,3},{3,2},{4,5},{5,4},{6,7},{7,6},{8,9},{9,8},{10,11... | collective-permute-start | bytes 1572872 | tf_op jit(solution)/shard_map/ppermute | solution.py:27
  77.6 50.4 %slice-start = ((s8[8388608]{0:T(1024)(128)(4,1)}), s8[4194304]{0:T(1024)(128)(4,1)S(1)}, s32[]{:S(2)}) async-start(s8[8388608]{0:T(1024)(128)(4,1)} %bitcast.67), calls=%async_computation | async-start | bytes 8388608
  79.6 48.5 %slice-start.1 = ((s8[8388608]{0:T(1024)(128)(4,1)}), s8[4194304]{0:T(1024)(128)(4,1)S(1)}, s32[]{:S(2)}) async-start(s8[8388608]{0:T(1024)(128)(4,1)} %bitcast.67), calls=%async_computation.1 | async-start | bytes 8388608
  81.7 11.1 %collective-permute-start.22 = (bf16[512,256]{1,0:T(8,128)(2,1)S(1)}, bf16[512,256]{1,0:T(8,128)(2,1)S(1)}, u32[]{:S(2)}, u32[]{:S(2)}) collective-permute-start(bf16[512,256]{1,0:T(8,128)(2,1)S(1)} %get-tuple-element.78), channel_id=1, source_target_pairs={{0,6},{1,7},{2,4},{3,5},{4,2},{5,3},{6,0},{7,1},{8,14},{9,15},{10,... | collective-permute-start | bytes 786440 | tf_op jit(solution)/shard_map/ppermute | solution.py:27
  82.6 15.2 %collective-permute-start.21 = (bf16[512,256]{1,0:T(8,128)(2,1)S(1)}, bf16[512,256]{1,0:T(8,128)(2,1)S(1)}, u32[]{:S(2)}, u32[]{:S(2)}) collective-permute-start(bf16[512,256]{1,0:T(8,128)(2,1)S(1)} %get-tuple-element.79), channel_id=1, source_target_pairs={{0,2},{1,3},{2,0},{3,1},{4,6},{5,7},{6,4},{7,5},{8,10},{9,11},{10,... | collective-permute-start | bytes 786440 | tf_op jit(solution)/shard_map/ppermute | solution.py:27
  86.4 22.7 %collective-permute-start.19 = (bf16[512,256]{1,0:T(8,128)(2,1)S(1)}, bf16[512,256]{1,0:T(8,128)(2,1)S(1)}, u32[]{:S(2)}, u32[]{:S(2)}) collective-permute-start(bf16[512,256]{1,0:T(8,128)(2,1)S(1)} %get-tuple-element.80), channel_id=1, source_target_pairs={{0,4},{1,5},{2,6},{3,7},{4,0},{5,1},{6,2},{7,3},{8,12},{9,13},{10,... | collective-permute-start | bytes 786440 | tf_op jit(solution)/shard_map/ppermute | solution.py:27
  109.3 11.1 %collective-permute-start.25 = (bf16[512,256]{1,0:T(8,128)(2,1)S(1)}, bf16[512,256]{1,0:T(8,128)(2,1)S(1)}, u32[]{:S(2)}, u32[]{:S(2)}) collective-permute-start(bf16[512,256]{1,0:T(8,128)(2,1)S(1)} %shard_map.119.refs_0_), channel_id=1, source_target_pairs={{0,6},{1,7},{2,4},{3,5},{4,2},{5,3},{6,0},{7,1},{8,14},{9,15},{10,... | collective-permute-start | bytes 786440 | tf_op jit(solution)/shard_map/ppermute | solution.py:27
  110.2 17.8 %collective-permute-start.23 = (bf16[512,256]{1,0:T(8,128)(2,1)S(1)}, bf16[512,256]{1,0:T(8,128)(2,1)S(1)}, u32[]{:S(2)}, u32[]{:S(2)}) collective-permute-start(bf16[512,256]{1,0:T(8,128)(2,1)S(1)} %shard_map.119.refs_0_), channel_id=1, source_target_pairs={{0,2},{1,3},{2,0},{3,1},{4,6},{5,7},{6,4},{7,5},{8,10},{9,11},{10,... | collective-permute-start | bytes 786440 | tf_op jit(solution)/shard_map/ppermute | solution.py:27
  110.2 24.9 %collective-permute-start.31 = (bf16[512,256]{1,0:T(8,128)(2,1)S(1)}, bf16[512,256]{1,0:T(8,128)(2,1)S(1)}, u32[]{:S(2)}, u32[]{:S(2)}) collective-permute-start(bf16[512,256]{1,0:T(8,128)(2,1)S(1)} %shard_map.119.refs_0_), channel_id=1, source_target_pairs={{0,4},{1,5},{2,6},{3,7},{4,0},{5,1},{6,2},{7,3},{8,12},{9,13},{10,... | collective-permute-start | bytes 786440 | tf_op jit(solution)/shard_map/ppermute | solution.py:27
  113.8 21.9 %collective-permute-start.30 = (bf16[512,256]{1,0:T(8,128)(2,1)S(1)}, bf16[512,256]{1,0:T(8,128)(2,1)S(1)}, u32[]{:S(2)}, u32[]{:S(2)}) collective-permute-start(bf16[512,256]{1,0:T(8,128)(2,1)S(1)} %shard_map.119.refs_0_), channel_id=1, source_target_pairs={{0,1},{1,0},{2,3},{3,2},{4,5},{5,4},{6,7},{7,6},{8,9},{9,8},{10,11... | collective-permute-start | bytes 786440 | tf_op jit(solution)/shard_map/ppermute | solution.py:27
  120.4 15.5 %collective-permute-start.26 = (bf16[512,256]{1,0:T(8,128)(2,1)S(1)}, bf16[512,256]{1,0:T(8,128)(2,1)S(1)}, u32[]{:S(2)}, u32[]{:S(2)}) collective-permute-start(bf16[512,256]{1,0:T(8,128)(2,1)S(1)} %collective-permute-done.25.refs_0_), channel_id=1, source_target_pairs={{0,1},{1,0},{2,3},{3,2},{4,5},{5,4},{6,7},{7,6},{8,9},{9,8},{10,11... | collective-permute-start | bytes 786440 | tf_op jit(solution)/shard_map/ppermute | solution.py:27
  128.0 8.1 %collective-permute-start.24 = (bf16[512,256]{1,0:T(8,128)(2,1)S(1)}, bf16[512,256]{1,0:T(8,128)(2,1)S(1)}, u32[]{:S(2)}, u32[]{:S(2)}) collective-permute-start(bf16[512,256]{1,0:T(8,128)(2,1)S(1)} %collective-permute-done.23.refs_0_), channel_id=1, source_target_pairs={{0,1},{1,0},{2,3},{3,2},{4,5},{5,4},{6,7},{7,6},{8,9},{9,8},{10,11... | collective-permute-start | bytes 786440 | tf_op jit(solution)/shard_map/ppermute | solution.py:27
  135.1 3.3 %collective-permute-start.32 = (bf16[512,256]{1,0:T(8,128)(2,1)S(1)}, bf16[512,256]{1,0:T(8,128)(2,1)S(1)}, u32[]{:S(2)}, u32[]{:S(2)}) collective-permute-start(bf16[512,256]{1,0:T(8,128)(2,1)S(1)} %collective-permute-done.31.refs_0_), channel_id=1, source_target_pairs={{0,1},{1,0},{2,3},{3,2},{4,5},{5,4},{6,7},{7,6},{8,9},{9,8},{10,11... | collective-permute-start | bytes 786440 | tf_op jit(solution)/shard_map/ppermute | solution.py:27
  136.4 17.8 %collective-permute-start.29 = (bf16[4,32,128]{2,1,0:T(8,128)(2,1)S(1)}, bf16[4,32,128]{2,1,0:T(8,128)(2,1)S(1)}, u32[]{:S(2)}, u32[]{:S(2)}) collective-permute-start(bf16[4,32,128]{2,1,0:T(8,128)(2,1)S(1)} %constant_dynamic-update-slice_fusion.4.refs_0_), channel_id=1, source_target_pairs={{0,24},{8,16},{16,8},{24,0},{1,25},{9,17},{17,9},{25,1},{2,26},{10... | collective-permute-start | bytes 98312 | tf_op jit(solution)/shard_map/ppermute | solution.py:27
  137.9 16.3 %collective-permute-start.28 = (bf16[4,32,128]{2,1,0:T(8,128)(2,1)S(1)}, bf16[4,32,128]{2,1,0:T(8,128)(2,1)S(1)}, u32[]{:S(2)}, u32[]{:S(2)}) collective-permute-start(bf16[4,32,128]{2,1,0:T(8,128)(2,1)S(1)} %constant_dynamic-update-slice_fusion.4.refs_0_), channel_id=1, source_target_pairs={{0,16},{8,24},{16,0},{24,8},{1,17},{9,25},{17,1},{25,9},{2,18},{10... | collective-permute-start | bytes 98312 | tf_op jit(solution)/shard_map/ppermute | solution.py:27
  138.7 11.4 %collective-permute-start.35 = (bf16[4,32,128]{2,1,0:T(8,128)(2,1)S(1)}, bf16[4,32,128]{2,1,0:T(8,128)(2,1)S(1)}, u32[]{:S(2)}, u32[]{:S(2)}) collective-permute-start(bf16[4,32,128]{2,1,0:T(8,128)(2,1)S(1)} %constant_dynamic-update-slice_fusion.6.refs_0_), channel_id=1, source_target_pairs={{0,24},{8,16},{16,8},{24,0},{1,25},{9,17},{17,9},{25,1},{2,26},{10... | collective-permute-start | bytes 98312 | tf_op jit(solution)/shard_map/ppermute | solution.py:27
  141.2 10.4 %collective-permute-start.34 = (bf16[4,32,128]{2,1,0:T(8,128)(2,1)S(1)}, bf16[4,32,128]{2,1,0:T(8,128)(2,1)S(1)}, u32[]{:S(2)}, u32[]{:S(2)}) collective-permute-start(bf16[4,32,128]{2,1,0:T(8,128)(2,1)S(1)} %constant_dynamic-update-slice_fusion.6.refs_0_), channel_id=1, source_target_pairs={{0,16},{8,24},{16,0},{24,8},{1,17},{9,25},{17,1},{25,9},{2,18},{10... | collective-permute-start | bytes 98312 | tf_op jit(solution)/shard_map/ppermute | solution.py:27
  141.7 9.9 %collective-permute-start.33 = (bf16[4,32,128]{2,1,0:T(8,128)(2,1)S(1)}, bf16[4,32,128]{2,1,0:T(8,128)(2,1)S(1)}, u32[]{:S(2)}, u32[]{:S(2)}) collective-permute-start(bf16[4,32,128]{2,1,0:T(8,128)(2,1)S(1)} %constant_dynamic-update-slice_fusion.6.refs_0_), channel_id=1, source_target_pairs={{0,8},{8,0},{16,24},{24,16},{1,9},{9,1},{17,25},{25,17},{2,10},{10... | collective-permute-start | bytes 98312 | tf_op jit(solution)/shard_map/ppermute | solution.py:27
  150.0 4.1 %collective-permute-start.27 = (bf16[4,32,128]{2,1,0:T(8,128)(2,1)S(1)}, bf16[4,32,128]{2,1,0:T(8,128)(2,1)S(1)}, u32[]{:S(2)}, u32[]{:S(2)}) collective-permute-start(bf16[4,32,128]{2,1,0:T(8,128)(2,1)S(1)} %constant_dynamic-update-slice_fusion.4.refs_0_), channel_id=1, source_target_pairs={{0,8},{8,0},{16,24},{24,16},{1,9},{9,1},{17,25},{25,17},{2,10},{10... | collective-permute-start | bytes 98312 | tf_op jit(solution)/shard_map/ppermute | solution.py:27

commit v2 on v1

--- a/solution.py
+++ b/solution.py
@@ -400,7 +400,7 @@
     out_ref[0] = dot(x_ref[0], new).astype(BF)
 
 
-def forward(place, weight, acts, step, tile, per, start, core, count, basis, coefs):
+def forward(place, weight, acts, step, tile, per, start, core, count, basis, coefs, skip):
     rows = weight.shape[0]
     tokens = acts.shape[1]
     at = lambda j: CORES * (start + j) + core
@@ -410,7 +410,7 @@
         (basis, (1,) + basis.shape[1:], lambda j, p: (at(j), 0, 0)),
     ]
     for coef in coefs:
-        ins.append((coef, (1,) + coef.shape[1:], lambda j, p: (CORES * j + core, 0, 0)))
+        ins.append((coef, (1,) + coef.shape[1:], lambda j, p: (CORES * (skip + j) + core, 0, 0)))
     product = (shaped((count, tokens, tile), BF), (1, tokens, tile), lambda j, p: (j, 0, 0))
     new = (shaped((count, rows, tile), BF), (1, rows, tile), lambda j, p: (j, 0, 0))
     return call(
@@ -436,7 +436,7 @@
         refs[-1][...] = changed(send_ref[0], dec_ref, refs[:reps], nbr, per)
 
 
-def finish(place, keep, send, basis, coefs, per, start, total, previous):
+def finish(place, keep, send, basis, coefs, per, start, total, previous, skip):
     count, rows, tile = keep.shape
     each = lambda j, p: (j // CORES, 0, 0)
     return call(
@@ -447,7 +447,7 @@
             (send, (1, rows, tile), each),
             (basis, (1,) + basis.shape[1:], lambda j, p: (CORES * start + j, 0, 0)),
         ]
-        + [(coef, (1,) + coef.shape[1:], lambda j, p: (j, 0, 0)) for coef in coefs],
+        + [(coef, (1,) + coef.shape[1:], lambda j, p: (CORES * skip + j, 0, 0)) for coef in coefs],
         [
             (
                 shaped((rows, total), BF),
@@ -500,6 +500,7 @@
     acts_t, tables, projected = [None] * STEPS, [None] * STEPS, [None] * STEPS
     chunks = (0, 1)
     mask_of = [mask_at(position, chips) for position in range(chips)]
+    groups = ((1, count - 1, 0, 1), (count, count, 1, 0), (0, 1, 0, 0))
 
     def basis_work(picked):
         for step in range(STEPS):
@@ -510,19 +511,18 @@
 
     moment = momentum
     gathered = [None, None]
-    weights = [[None, None], [None, None]]
+    weights = [[None, None] for _ in groups]
     final_m = final_w = None
     for step in range(STEPS):
         last = step == STEPS - 1
         found_all = []
-        for chunk in chunks:
-            start = chunk * count
+        for group, (start, size, chunk, skip) in enumerate(groups):
             found = [None, None]
             for core in (1, 0):
                 if step == 0:
-                    found[core] = first(place, weight, inputs, tile, start, core, count)
+                    found[core] = first(place, weight, inputs, tile, start, core, size)
                 else:
-                    weights[chunk][core], found[core] = forward(
+                    weights[group][core], found[core] = forward(
                         place,
                         weight,
                         inputs,
@@ -531,22 +531,24 @@
                         per,
                         start,
                         core,
-                        count,
+                        size,
                         tables[step - 1][0],
                         gathered[chunk],
+                        skip,
                     )
                 if core == 1:
                     other = swap(found[1], "tp", parts, 1)
-            sums = [found[0][at].astype(F32) + other[at].astype(F32) for at in range(count)]
-            if chunk == 0:
-                total, sums = sums[0], [None] + [value.astype(BF) for value in sums[1:]]
-                if step == 0:
-                    *sums[1:], late = lax.optimization_barrier((*sums[1:], indices))
-                    old, per = basis_work(late)
+            sums = [found[0][at].astype(F32) + other[at].astype(F32) for at in range(size)]
+            if start == 0:
+                total = sums[0]
+                continue
+            sums = [value.astype(BF) for value in sums]
+            if step == 0 and group == 1:
+                *sums, late = lax.optimization_barrier((*sums, indices))
+                old, per = basis_work(late)
             for at, value in enumerate(sums):
                 mask = mask_of[start + at]
-                if mask:
-                    found_all.append(swap(value.astype(BF), "tp", parts, mask * CORES))
+                found_all.append(swap(value, "tp", parts, mask * CORES))
         errors = error_of(place, total, found_all, targets, step)
         pairs, exact, sent = [], [], []
         for position, mask in enumerate(mask_of):
@@ -575,29 +577,31 @@
                 None,
             )
         else:
-            for chunk in chunks:
+            for start, size in ((0, 1), (1, count - 1), (count, count)):
                 (final_m,) = update(
-                    jnp.stack(pairs[chunk * count * CORES : (chunk + 1) * count * CORES]),
+                    jnp.stack(pairs[start * CORES : (start + size) * CORES]),
                     moment,
                     tables[step][1],
-                    jnp.concatenate(exact[chunk * count : (chunk + 1) * count]),
+                    jnp.concatenate(exact[start : start + size]),
                     per,
-                    chunk * count * CORES,
+                    start * CORES,
                     None,
                     cols,
                     final_m,
                 )
-    for chunk in chunks:
+    for group in (2, 0, 1):
+        start, _, chunk, skip = groups[group]
         final_w = finish(
             place,
-            weights[chunk][0],
-            weights[chunk][1],
+            weights[group][0],
+            weights[group][1],
             tables[STEPS - 1][0],
             gathered[chunk],
             per,
-            chunk * count,
+            start,
             cols,
             final_w,
+            skip,
         )
     return (final_w, final_m)
 

time: 157 us -> 157 us (level); the launches traced: 157 us -> 155 us
  waiting for transfers between devices: 62.1 us -> 52.8 us
  starting transfers between devices: 38 us -> 42.1 us
  Pallas kernels: 46 us -> 49.6 us
    ppermute x36 -> x38, waiting for transfers between devices: 62.1 us -> 52.8 us  [swap(): return lax.ppermute(value, axis, [(at, at ^ mask) for at in range(size)])]
    ppermute x36 -> x38, starting transfers between devices: 38 us -> 42.1 us  [swap(): return lax.ppermute(value, axis, [(at, at ^ mask) for at in range(size)])]
    pallas_call x4 -> x6, Pallas kernels: 9.01 us -> 12.1 us  [first(): pl.pallas_call(functools.partial(first_kernel, weight.shape[1] // tile //...]
    pallas_call x24 -> x28, Pallas kernels: 37 us -> 37.5 us  [call(): pl.pallas_call(kernel, grid_spec=pltpu.PrefetchScalarGridSpec(num_scalar_...]
  transfers between devices with their start and end apart: 36 -> 38, of which waited for: 12 -> 11; matrix products, arithmetic and copies ran while one was open for 3% -> 3% of each run, Pallas kernels for 26% -> 29%
where the time goes in v2:
time: 157 us; the launch traced here: 155 us
  waiting for transfers between devices  52.8 us (34%)
  Pallas kernels  49.6 us (32%)
  starting transfers between devices  42.1 us (27%)
  local copies, waits for them, and re-layouts  5.56 us (4%)
  other arithmetic  3.82 us (2%)
    ppermute x38, waiting for transfers between devices, swap(): return lax.ppermute(value, axis, [(at, at ^ mask) for at in range(size)])  52.8 us
    ppermute x38, starting transfers between devices, swap(): return lax.ppermute(value, axis, [(at, at ^ mask) for at in range(size)])  42.1 us
    pallas_call x28, Pallas kernels, call(): pl.pallas_call(kernel, grid_spec=pltpu.PrefetchScalarGridSpec(num_scalar_...  37.5 us
    pallas_call x6, Pallas kernels, first(): pl.pallas_call(functools.partial(first_kernel, weight.shape[1] // tile //...  12.1 us
    unnamed x29, local copies, waits for them, and re-layouts  4.41 us
  transfers between devices with their start and end apart: 38, of which 11 were waited for; matrix products, arithmetic and copies ran while one was open for 3% of the time, Pallas kernels for 29%

profile of v2, /device:TPU:0, one launch (start us, length us, event | category | flops | bytes accessed | tf_op | source)
XLA Modules:
  0.0 155.3 jit_solution(15092521488143245577)
XLA Ops:
  0.6 2.0 %first.11 = bf16[1,512,256]{2,1,0:T(8,128)(2,1)S(1)} custom-call(s32[1]{0:T(128)} %bitcast.place, bf16[1024,2048]{1,0:T(8,128)(2,1)} %w_ref.23, bf16[2,512,1024]{2,1,0:T(8,128)(2,1)} %x_ref.27), custom_call_target="tpu_custom_call" | custom-call | flops 268435456 | bytes 1572864 | tf_op jit(solution)/shard_map/first/pallas_call | solution.py:375
  2.6 0.6 collective-permute-start.2
  3.2 2.0 %first.9 = bf16[1,512,256]{2,1,0:T(8,128)(2,1)S(1)} custom-call(s32[1]{0:T(128)} %bitcast.place, bf16[1024,2048]{1,0:T(8,128)(2,1)} %w_ref.23, bf16[2,512,1024]{2,1,0:T(8,128)(2,1)} %x_ref.27), custom_call_target="tpu_custom_call" | custom-call | flops 268435456 | bytes 1572864 | tf_op jit(solution)/shard_map/first/pallas_call | solution.py:375
  5.3 2.0 %first.7 = bf16[2,512,256]{2,1,0:T(8,128)(2,1)S(1)} custom-call(s32[1]{0:T(128)} %bitcast.place, bf16[1024,2048]{1,0:T(8,128)(2,1)} %w_ref.23, bf16[2,512,1024]{2,1,0:T(8,128)(2,1)} %x_ref.27), custom_call_target="tpu_custom_call" | custom-call | flops 536870912 | bytes 2097152 | tf_op jit(solution)/shard_map/first/pallas_call | solution.py:375
  7.3 0.6 collective-permute-start
  7.9 2.0 %first.6 = bf16[2,512,256]{2,1,0:T(8,128)(2,1)S(1)} custom-call(s32[1]{0:T(128)} %bitcast.place, bf16[1024,2048]{1,0:T(8,128)(2,1)} %w_ref.23, bf16[2,512,1024]{2,1,0:T(8,128)(2,1)} %x_ref.27), custom_call_target="tpu_custom_call" | custom-call | flops 536870912 | bytes 2097152 | tf_op jit(solution)/shard_map/first/pallas_call | solution.py:375
  10.0 2.0 %first.10 = bf16[1,512,256]{2,1,0:T(8,128)(2,1)S(1)} custom-call(s32[1]{0:T(128)} %bitcast.place, bf16[1024,2048]{1,0:T(8,128)(2,1)} %w_ref.23, bf16[2,512,1024]{2,1,0:T(8,128)(2,1)} %x_ref.27), custom_call_target="tpu_custom_call" | custom-call | flops 268435456 | bytes 1572864 | tf_op jit(solution)/shard_map/first/pallas_call | solution.py:375
  12.0 2.0 %first.8 = bf16[1,512,256]{2,1,0:T(8,128)(2,1)S(1)} custom-call(s32[1]{0:T(128)} %bitcast.place, bf16[1024,2048]{1,0:T(8,128)(2,1)} %w_ref.23, bf16[2,512,1024]{2,1,0:T(8,128)(2,1)} %x_ref.27), custom_call_target="tpu_custom_call" | custom-call | flops 268435456 | bytes 1572864 | tf_op jit(solution)/shard_map/first/pallas_call | solution.py:375
  14.0 0.8 fusion.2
  14.8 3.6 %collective-permute-start.3 = (bf16[512,256]{1,0:T(8,128)(2,1)}, bf16[512,256]{1,0:T(8,128)(2,1)S(1)}, u32[]{:S(2)}, u32[]{:S(2)}) collective-permute-start(bf16[512,256]{1,0:T(8,128)(2,1)} %fusion.2), channel_id=1, source_target_pairs={{0,4},{1,5},{2,6},{3,7},{4,0},{5,1},{6,2},{7,3},{8,12},{9,13},{10,... | collective-permute-start | bytes 786440 | tf_op jit(solution)/shard_map/ppermute | solution.py:27
  18.4 1.0 add_bitcast_fusion.1.total_ref
  19.4 0.9 fusion.1
  21.9 1.6 %collective-permute-start.4 = (bf16[512,256]{1,0:T(8,128)(2,1)}, bf16[512,256]{1,0:T(8,128)(2,1)S(1)}, u32[]{:S(2)}, u32[]{:S(2)}) collective-permute-start(bf16[512,256]{1,0:T(8,128)(2,1)} %get-tuple-element.49), channel_id=1, source_target_pairs={{0,2},{1,3},{2,0},{3,1},{4,6},{5,7},{6,4},{7,5},{8,10},{9,11},{10,... | collective-permute-start | bytes 786440 | tf_op jit(solution)/shard_map/ppermute | solution.py:27
  23.7 0.8 copy-done.5
  24.6 1.6 %shard_map.112 = (bf16[8,128,256]{2,1,0:T(8,128)(2,1)S(1)}, bf16[8,128,96]{2,1,0:T(8,128)(2,1)S(1)}, bf16[8,64,128]{2,1,0:T(8,128)(2,1)S(1)}) custom-call(s32[1]{0:T(128)} %bitcast.place, s32[8,1,256]{2,1,0:T(1,128)S(1)} %reshape.67.all_ref, s32[8,1,96]{2,1,0:T(1,128)S(1)} %bitcast.77, bf16[128,256]{1,0:T(8,128)(2,1)S(1)} %copy-done.4, ...), custom_call_target="tpu_custom_call" | custom-call | flops 234881024 | bytes 2097152 | tf_op jit(solution)/shard_map/pallas_call | solution.py:59
  26.2 1.6 %shard_map.104 = (bf16[8,128,256]{2,1,0:T(8,128)(2,1)S(1)}, bf16[8,128,96]{2,1,0:T(8,128)(2,1)S(1)}, bf16[8,64,128]{2,1,0:T(8,128)(2,1)S(1)}) custom-call(s32[1]{0:T(128)} %bitcast.place, s32[8,1,256]{2,1,0:T(1,128)S(1)} %reshape.66.all_ref, s32[8,1,96]{2,1,0:T(1,128)S(1)} %bitcast.78, bf16[128,256]{1,0:T(8,128)(2,1)S(1)} %copy-done.4, ...), custom_call_target="tpu_custom_call" | custom-call | flops 234881024 | bytes 2097152 | tf_op jit(solution)/shard_map/pallas_call | solution.py:59
  27.8 0.8 shard_map.105
  28.7 0.8 shard_map.113
  29.5 1.9 %collective-permute-done.3.refs_0_ = bf16[512,256]{1,0:T(8,128)(2,1)S(1)} collective-permute-done((bf16[512,256]{1,0:T(8,128)(2,1)}, bf16[512,256]{1,0:T(8,128)(2,1)S(1)}, u32[]{:S(2)}, u32[]{:S(2)}) %collective-permute-start.3) | collective-permute-done | bytes 262176 | tf_op jit(solution)/shard_map/ppermute | solution.py:27
  31.4 9.1 %collective-permute-done.4.refs_1_ = bf16[512,256]{1,0:T(8,128)(2,1)S(1)} collective-permute-done((bf16[512,256]{1,0:T(8,128)(2,1)}, bf16[512,256]{1,0:T(8,128)(2,1)S(1)}, u32[]{:S(2)}, u32[]{:S(2)}) %collective-permute-start.4) | collective-permute-done | bytes 262176 | tf_op jit(solution)/shard_map/ppermute | solution.py:27
  40.7 4.6 %collective-permute-start.14 = (bf16[512,256]{1,0:T(8,128)(2,1)S(1)}, bf16[512,256]{1,0:T(8,128)(2,1)S(1)}, u32[]{:S(2)}, u32[]{:S(2)}) collective-permute-start(bf16[512,256]{1,0:T(8,128)(2,1)S(1)} %shard_map.107.refs_0_), channel_id=1, source_target_pairs={{0,4},{1,5},{2,6},{3,7},{4,0},{5,1},{6,2},{7,3},{8,12},{9,13},{10,... | collective-permute-start | bytes 786440 | tf_op jit(solution)/shard_map/ppermute | solution.py:27
  45.3 0.5 collective-permute-start.8
  46.0 3.4 %copy-done.2 = f32[1,1024,2048]{2,1,0:T(8,128)S(1)} copy-done((f32[1,1024,2048]{2,1,0:T(8,128)S(1)}, f32[1,1024,2048]{2,1,0:T(8,128)}, u32[]{:S(2)}) %copy-start.2) | copy-done | bytes 8388632
  49.4 2.4 %shard_map.106.old_ref = f32[8,32,128]{2,1,0:T(8,128)S(1)} custom-call(s32[1]{0:T(128)} %bitcast.place, bf16[8,64,128]{2,1,0:T(8,128)(2,1)S(1)} %get-tuple-element.47.kept_ref, f32[1,1024,2048]{2,1,0:T(8,128)S(1)} %copy-done.2), custom_call_target="tpu_custom_call" | custom-call | flops 268435456 | bytes 8388608 | tf_op jit(solution)/shard_map/pallas_call | solution.py:59
  51.8 11.6 %collective-permute-done.14.refs_0_ = bf16[512,256]{1,0:T(8,128)(2,1)S(1)} collective-permute-done((bf16[512,256]{1,0:T(8,128)(2,1)S(1)}, bf16[512,256]{1,0:T(8,128)(2,1)S(1)}, u32[]{:S(2)}, u32[]{:S(2)}) %collective-permute-start.14) | collective-permute-done | bytes 262176 | tf_op jit(solution)/shard_map/ppermute | solution.py:27
  63.5 0.5 collective-permute-start.9
  64.0 1.2 collective-permute-done.6.refs_0_
  65.7 2.5 %collective-permute-start.18 = (bf16[4,32,128]{2,1,0:T(8,128)(2,1)S(1)}, bf16[4,32,128]{2,1,0:T(8,128)(2,1)S(1)}, u32[]{:S(2)}, u32[]{:S(2)}) collective-permute-start(bf16[4,32,128]{2,1,0:T(8,128)(2,1)S(1)} %constant_dynamic-update-slice_fusion.2.refs_0_), channel_id=1, source_target_pairs={{0,24},{8,16},{16,8},{24,0},{1,25},{9,17},{17,9},{25,1},{2,26},{10... | collective-permute-start | bytes 98312 | tf_op jit(solution)/shard_map/ppermute | solution.py:27
  68.2 0.5 collective-permute-start.17
  68.7 0.5 collective-permute-start.16
  69.7 2.5 %collective-permute-start.12 = (bf16[4,32,128]{2,1,0:T(8,128)(2,1)S(1)}, bf16[4,32,128]{2,1,0:T(8,128)(2,1)S(1)}, u32[]{:S(2)}, u32[]{:S(2)}) collective-permute-start(bf16[4,32,128]{2,1,0:T(8,128)(2,1)S(1)} %constant_dynamic-update-slice_fusion.refs_0_), channel_id=1, source_target_pairs={{0,24},{8,16},{16,8},{24,0},{1,25},{9,17},{17,9},{25,1},{2,26},{10... | collective-permute-start | bytes 98312 | tf_op jit(solution)/shard_map/ppermute | solution.py:27
  72.3 0.5 collective-permute-start.11
  72.9 0.6 collective-permute-start.10
  73.5 0.8 shard_map.120
  74.7 1.5 collective-permute-done.11.refs_2_
  76.2 0.7 collective-permute-done.10.refs_1_
  76.8 1.9 %shard_map.111 = (bf16[2,1024,256]{2,1,0:T(8,128)(2,1)S(1)}, bf16[2,512,256]{2,1,0:T(8,128)(2,1)S(1)}) custom-call(s32[1]{0:T(128)} %bitcast.place, bf16[1024,2048]{1,0:T(8,128)(2,1)S(1)} %copy-done, bf16[2,512,1024]{2,1,0:T(8,128)(2,1)S(1)} %copy-done.1, bf16[8,128,256]{2,1,0:T(8,128)(2,1)S(1)} %get-tuple-element.46.dec_ref, ...), custom_call_target="tpu_custom_call" | custom-call | flops 536870912 | bytes 2097152 | tf_op jit(solution)/shard_map/pallas_call | solution.py:59
  78.9 0.8 shard_map.118
  79.7 0.5 collective-permute-start.19
  80.3 0.8 shard_map.119
  81.1 2.0 %shard_map.110 = (bf16[2,1024,256]{2,1,0:T(8,128)(2,1)S(1)}, bf16[2,512,256]{2,1,0:T(8,128)(2,1)S(1)}) custom-call(s32[1]{0:T(128)} %bitcast.place, bf16[1024,2048]{1,0:T(8,128)(2,1)S(1)} %copy-done, bf16[2,512,1024]{2,1,0:T(8,128)(2,1)S(1)} %copy-done.1, bf16[8,128,256]{2,1,0:T(8,128)(2,1)S(1)} %get-tuple-element.46.dec_ref, ...), custom_call_target="tpu_custom_call" | custom-call | flops 536870912 | bytes 2097152 | tf_op jit(solution)/shard_map/pallas_call | solution.py:59
  83.2 3.8 %collective-permute-start.21 = (bf16[512,256]{1,0:T(8,128)(2,1)S(1)}, bf16[512,256]{1,0:T(8,128)(2,1)S(1)}, u32[]{:S(2)}, u32[]{:S(2)}) collective-permute-start(bf16[512,256]{1,0:T(8,128)(2,1)S(1)} %fusion.3), channel_id=1, source_target_pairs={{0,4},{1,5},{2,6},{3,7},{4,0},{5,1},{6,2},{7,3},{8,12},{9,13},{10,... | collective-permute-start | bytes 786440 | tf_op jit(solution)/shard_map/ppermute | solution.py:27
  87.1 3.3 %collective-permute-start.24 = (bf16[512,256]{1,0:T(8,128)(2,1)S(1)}, bf16[512,256]{1,0:T(8,128)(2,1)S(1)}, u32[]{:S(2)}, u32[]{:S(2)}) collective-permute-start(bf16[512,256]{1,0:T(8,128)(2,1)S(1)} %get-tuple-element.88), channel_id=1, source_target_pairs={{0,6},{1,7},{2,4},{3,5},{4,2},{5,3},{6,0},{7,1},{8,14},{9,15},{10,... | collective-permute-start | bytes 786440 | tf_op jit(solution)/shard_map/ppermute | solution.py:27
  90.5 0.8 shard_map.117
  91.4 14.0 %collective-permute-done.21.refs_0_ = bf16[512,256]{1,0:T(8,128)(2,1)S(1)} collective-permute-done((bf16[512,256]{1,0:T(8,128)(2,1)S(1)}, bf16[512,256]{1,0:T(8,128)(2,1)S(1)}, u32[]{:S(2)}, u32[]{:S(2)}) %collective-permute-start.21) | collective-permute-done | bytes 262176 | tf_op jit(solution)/shard_map/ppermute | solution.py:27
  105.4 0.9 collective-permute-done.23.refs_1_
  106.4 6.5 %collective-permute-start.33 = (bf16[512,256]{1,0:T(8,128)(2,1)S(1)}, bf16[512,256]{1,0:T(8,128)(2,1)S(1)}, u32[]{:S(2)}, u32[]{:S(2)}) collective-permute-start(bf16[512,256]{1,0:T(8,128)(2,1)S(1)} %shard_map.121.refs_0_), channel_id=1, source_target_pairs={{0,4},{1,5},{2,6},{3,7},{4,0},{5,1},{6,2},{7,3},{8,12},{9,13},{10,... | collective-permute-start | bytes 786440 | tf_op jit(solution)/shard_map/ppermute | solution.py:27
  113.0 0.5 collective-permute-start.27
  113.7 7.1 %shard_map.116 = (f32[8,1024,256]{2,1,0:T(8,128)S(1)}, f32[8,32,128]{2,1,0:T(8,128)S(1)}) custom-call(s32[1]{0:T(128)} %bitcast.place, bf16[1024,512]{1,0:T(8,128)(2,1)S(1)} %get-tuple-element.58.xt_ref, bf16[8,512,256]{2,1,0:T(8,128)(2,1)S(1)} %bitcast_dynamic-update-slice_fusion.e_ref, f32[1,1024,2048]{2,1,0:T(8,128)S(1)} %bitcast.68, ...), custom_call_target="tpu_custom_call" | custom-call | flops 2147483648 | bytes 16777216 | tf_op jit(solution)/shard_map/pallas_call | solution.py:59
  120.8 9.9 %collective-permute-done.33.refs_0_ = bf16[512,256]{1,0:T(8,128)(2,1)S(1)} collective-permute-done((bf16[512,256]{1,0:T(8,128)(2,1)S(1)}, bf16[512,256]{1,0:T(8,128)(2,1)S(1)}, u32[]{:S(2)}, u32[]{:S(2)}) %collective-permute-start.33) | collective-permute-done | bytes 262176 | tf_op jit(solution)/shard_map/ppermute | solution.py:27
  130.7 0.5 collective-permute-start.28
  131.2 1.7 %collective-permute-done.25.refs_0_ = bf16[512,256]{1,0:T(8,128)(2,1)S(1)} collective-permute-done((bf16[512,256]{1,0:T(8,128)(2,1)S(1)}, bf16[512,256]{1,0:T(8,128)(2,1)S(1)}, u32[]{:S(2)}, u32[]{:S(2)}) %collective-permute-start.25) | collective-permute-done | bytes 262176 | tf_op jit(solution)/shard_map/ppermute | solution.py:27
  133.2 2.2 %shard_map.129.refs_0_ = f32[1,1024,2048]{2,1,0:T(8,128)} custom-call(s32[1]{0:T(128)} %bitcast.place, bf16[1024,512]{1,0:T(8,128)(2,1)S(1)} %get-tuple-element.81.xt_ref, bf16[2,512,256]{2,1,0:T(8,128)(2,1)S(1)} %pad_maximum_fusion.2.e_ref, f32[8,1024,256]{2,1,0:T(8,128)S(1)} %get-tuple-element.82.m_ref, bf16[8,128,96]{2,1,0:T(8,128)(2,1)S(1)} %get-tuple-element.83.dec_ref, ...), custom_call_target="tpu_custom_call" | custom-call | flops 536870912 | bytes 4194304 | tf_op jit(solution)/shard_map/pallas_call | solution.py:59
  136.0 1.6 %collective-permute-start.31 = (bf16[4,32,128]{2,1,0:T(8,128)(2,1)S(1)}, bf16[4,32,128]{2,1,0:T(8,128)(2,1)S(1)}, u32[]{:S(2)}, u32[]{:S(2)}) collective-permute-start(bf16[4,32,128]{2,1,0:T(8,128)(2,1)S(1)} %constant_dynamic-update-slice_fusion.4.refs_0_), channel_id=1, source_target_pairs={{0,24},{8,16},{16,8},{24,0},{1,25},{9,17},{17,9},{25,1},{2,26},{10... | collective-permute-start | bytes 98312 | tf_op jit(solution)/shard_map/ppermute | solution.py:27
  137.5 0.5 collective-permute-start.30
  138.3 2.5 %collective-permute-start.37 = (bf16[4,32,128]{2,1,0:T(8,128)(2,1)S(1)}, bf16[4,32,128]{2,1,0:T(8,128)(2,1)S(1)}, u32[]{:S(2)}, u32[]{:S(2)}) collective-permute-start(bf16[4,32,128]{2,1,0:T(8,128)(2,1)S(1)} %constant_dynamic-update-slice_fusion.6.refs_0_), channel_id=1, source_target_pairs={{0,24},{8,16},{16,8},{24,0},{1,25},{9,17},{17,9},{25,1},{2,26},{10... | collective-permute-start | bytes 98312 | tf_op jit(solution)/shard_map/ppermute | solution.py:27
  140.8 0.5 collective-permute-start.36
  141.3 0.5 collective-permute-start.35
  141.9 2.2 %shard_map.130.refs_0_ = f32[1,1024,2048]{2,1,0:T(8,128)} custom-call(s32[1]{0:T(128)} %bitcast.place, bf16[1024,512]{1,0:T(8,128)(2,1)S(1)} %get-tuple-element.81.xt_ref, bf16[2,512,256]{2,1,0:T(8,128)(2,1)S(1)} %pad_maximum_fusion.1.e_ref, f32[8,1024,256]{2,1,0:T(8,128)S(1)} %get-tuple-element.82.m_ref, ...), custom_call_target="tpu_custom_call", output_to_operand_aliasing={{}: (6, {})} | custom-call | flops 536870912 | bytes 4194304 | tf_op jit(solution)/shard_map/pallas_call | solution.py:59
  144.3 3.8 %shard_map.131 = f32[1,1024,2048]{2,1,0:T(8,128)} custom-call(s32[1]{0:T(128)} %bitcast.place, bf16[1024,512]{1,0:T(8,128)(2,1)S(1)} %get-tuple-element.81.xt_ref, bf16[4,512,256]{2,1,0:T(8,128)(2,1)S(1)} %pad_maximum_fusion.e_ref, f32[8,1024,256]{2,1,0:T(8,128)S(1)} %get-tuple-element.82.m_ref, ...), custom_call_target="tpu_custom_call", output_to_operand_aliasing={{}: (6, {})} | custom-call | flops 1073741824 | bytes 8388608 | tf_op jit(solution)/shard_map/pallas_call | solution.py:59
  148.1 1.5 collective-permute-start.29
  149.6 1.5 shard_map.126.refs_4_
  151.0 1.5 shard_map.127.refs_4_
  152.6 2.7 %shard_map.128 = bf16[1024,2048]{1,0:T(8,128)(2,1)} custom-call(s32[1]{0:T(128)} %bitcast.place, bf16[2,1024,256]{2,1,0:T(8,128)(2,1)S(1)} %get-tuple-element.53.keep_ref, bf16[2,1024,256]{2,1,0:T(8,128)(2,1)S(1)} %get-tuple-element.54.send_ref, bf16[8,128,256]{2,1,0:T(8,128)(2,1)S(1)} %get-tuple-element.55.dec_ref, ...), custom_call_target="tpu_custom_call", output_to_operand_aliasing={{}: (8, {})} | custom-call | flops 536870912 | bytes 4194304 | tf_op jit(solution)/shard_map/pallas_call | solution.py:59
  (122 shorter events, 5.4 us)
Async XLA Ops:
  2.6 11.4 %collective-permute-start.2 = (bf16[1,512,256]{2,1,0:T(8,128)(2,1)S(1)}, bf16[1,512,256]{2,1,0:T(8,128)(2,1)S(1)}, u32[]{:S(2)}, u32[]{:S(2)}) collective-permute-start(bf16[1,512,256]{2,1,0:T(8,128)(2,1)S(1)} %first.11), channel_id=1, source_target_pairs={{0,1},{1,0},{2,3},{3,2},{4,5},{5,4},{6,7},{7,6},{8,9},{9,8},{10,11... | collective-permute-start | bytes 786440 | tf_op jit(solution)/shard_map/ppermute | solution.py:27
  5.2 13.2 %collective-permute-start.1 = (bf16[1,512,256]{2,1,0:T(8,128)(2,1)S(1)}, bf16[1,512,256]{2,1,0:T(8,128)(2,1)}, u32[]{:S(2)}, u32[]{:S(2)}) collective-permute-start(bf16[1,512,256]{2,1,0:T(8,128)(2,1)S(1)} %first.9), channel_id=1, source_target_pairs={{0,1},{1,0},{2,3},{3,2},{4,5},{5,4},{6,7},{7,6},{8,9},{9,8},{10,11... | collective-permute-start | bytes 786440 | tf_op jit(solution)/shard_map/ppermute | solution.py:27
  7.3 12.1 %collective-permute-start = (bf16[2,512,256]{2,1,0:T(8,128)(2,1)S(1)}, bf16[2,512,256]{2,1,0:T(8,128)(2,1)S(1)}, u32[]{:S(2)}, u32[]{:S(2)}) collective-permute-start(bf16[2,512,256]{2,1,0:T(8,128)(2,1)S(1)} %first.7), channel_id=1, source_target_pairs={{0,1},{1,0},{2,3},{3,2},{4,5},{5,4},{6,7},{7,6},{8,9},{9,8},{10,11... | collective-permute-start | bytes 1572872 | tf_op jit(solution)/shard_map/ppermute | solution.py:27
  14.0 6.3 %copy-start.6 = (s32[2,4,8,16,2]{3,4,2,1,0:T(2,128)S(1)}, s32[2,4,8,16,2]{3,4,2,1,0:T(2,128)}, u32[]{:S(2)}) copy-start(s32[2,4,8,16,2]{3,4,2,1,0:T(2,128)} %param.13) | copy-start | bytes 24580
  14.8 16.6 %collective-permute-start.3 = (bf16[512,256]{1,0:T(8,128)(2,1)}, bf16[512,256]{1,0:T(8,128)(2,1)S(1)}, u32[]{:S(2)}, u32[]{:S(2)}) collective-permute-start(bf16[512,256]{1,0:T(8,128)(2,1)} %fusion.2), channel_id=1, source_target_pairs={{0,4},{1,5},{2,6},{3,7},{4,0},{5,1},{6,2},{7,3},{8,12},{9,13},{10,... | collective-permute-start | bytes 786440 | tf_op jit(solution)/shard_map/ppermute | solution.py:27
  19.4 4.3 %copy-start.4 = (bf16[128,256]{1,0:T(8,128)(2,1)S(1)}, bf16[128,256]{1,0:T(8,128)(2,1)}, u32[]{:S(2)}) copy-start(bf16[128,256]{1,0:T(8,128)(2,1)} %constant.21.clone.cols_ref) | copy-start | bytes 196612
  20.5 7.3 %copy-start.1 = (bf16[2,512,1024]{2,1,0:T(8,128)(2,1)S(1)}, bf16[2,512,1024]{2,1,0:T(8,128)(2,1)}, u32[]{:S(2)}) copy-start(bf16[2,512,1024]{2,1,0:T(8,128)(2,1)} %x_ref.27) | copy-start | bytes 6291460
  21.9 18.7 %collective-permute-start.4 = (bf16[512,256]{1,0:T(8,128)(2,1)}, bf16[512,256]{1,0:T(8,128)(2,1)S(1)}, u32[]{:S(2)}, u32[]{:S(2)}) collective-permute-start(bf16[512,256]{1,0:T(8,128)(2,1)} %get-tuple-element.49), channel_id=1, source_target_pairs={{0,2},{1,3},{2,0},{3,1},{4,6},{5,7},{6,4},{7,5},{8,10},{9,11},{10,... | collective-permute-start | bytes 786440 | tf_op jit(solution)/shard_map/ppermute | solution.py:27
  23.4 17.1 %collective-permute-start.5 = (bf16[512,256]{1,0:T(8,128)(2,1)}, bf16[512,256]{1,0:T(8,128)(2,1)S(1)}, u32[]{:S(2)}, u32[]{:S(2)}) collective-permute-start(bf16[512,256]{1,0:T(8,128)(2,1)} %get-tuple-element.50), channel_id=1, source_target_pairs={{0,6},{1,7},{2,4},{3,5},{4,2},{5,3},{6,0},{7,1},{8,14},{9,15},{10,... | collective-permute-start | bytes 786440 | tf_op jit(solution)/shard_map/ppermute | solution.py:27
  23.7 0.8 copy-start.5
  27.8 12.7 %copy-start.3 = (bf16[2,512,256]{2,1,0:T(8,128)(2,1)S(1)}, bf16[2,512,256]{2,1,0:T(8,128)(2,1)}, u32[]{:S(2)}) copy-start(bf16[2,512,256]{2,1,0:T(8,128)(2,1)} %goal_ref.3) | copy-start | bytes 1572868
  40.7 22.8 %collective-permute-start.14 = (bf16[512,256]{1,0:T(8,128)(2,1)S(1)}, bf16[512,256]{1,0:T(8,128)(2,1)S(1)}, u32[]{:S(2)}, u32[]{:S(2)}) collective-permute-start(bf16[512,256]{1,0:T(8,128)(2,1)S(1)} %shard_map.107.refs_0_), channel_id=1, source_target_pairs={{0,4},{1,5},{2,6},{3,7},{4,0},{5,1},{6,2},{7,3},{8,12},{9,13},{10,... | collective-permute-start | bytes 786440 | tf_op jit(solution)/shard_map/ppermute | solution.py:27
  45.3 19.9 %collective-permute-start.13 = (bf16[512,256]{1,0:T(8,128)(2,1)S(1)}, bf16[512,256]{1,0:T(8,128)(2,1)S(1)}, u32[]{:S(2)}, u32[]{:S(2)}) collective-permute-start(bf16[512,256]{1,0:T(8,128)(2,1)S(1)} %shard_map.107.refs_0_), channel_id=1, source_target_pairs={{0,1},{1,0},{2,3},{3,2},{4,5},{5,4},{6,7},{7,6},{8,9},{9,8},{10,11... | collective-permute-start | bytes 786440 | tf_op jit(solution)/shard_map/ppermute | solution.py:27
  45.3 18.2 %collective-permute-start.8 = (bf16[512,256]{1,0:T(8,128)(2,1)S(1)}, bf16[512,256]{1,0:T(8,128)(2,1)S(1)}, u32[]{:S(2)}, u32[]{:S(2)}) collective-permute-start(bf16[512,256]{1,0:T(8,128)(2,1)S(1)} %shard_map.107.refs_0_), channel_id=1, source_target_pairs={{0,6},{1,7},{2,4},{3,5},{4,2},{5,3},{6,0},{7,1},{8,14},{9,15},{10,... | collective-permute-start | bytes 786440 | tf_op jit(solution)/shard_map/ppermute | solution.py:27
  45.9 19.3 %collective-permute-start.6 = (bf16[512,256]{1,0:T(8,128)(2,1)S(1)}, bf16[512,256]{1,0:T(8,128)(2,1)S(1)}, u32[]{:S(2)}, u32[]{:S(2)}) collective-permute-start(bf16[512,256]{1,0:T(8,128)(2,1)S(1)} %shard_map.107.refs_0_), channel_id=1, source_target_pairs={{0,2},{1,3},{2,0},{3,1},{4,6},{5,7},{6,4},{7,5},{8,10},{9,11},{10,... | collective-permute-start | bytes 786440 | tf_op jit(solution)/shard_map/ppermute | solution.py:27
  46.0 3.4 %copy-start.2 = (f32[1,1024,2048]{2,1,0:T(8,128)S(1)}, f32[1,1024,2048]{2,1,0:T(8,128)}, u32[]{:S(2)}) copy-start(f32[1,1024,2048]{2,1,0:T(8,128)} %m_ref.3) | copy-start | bytes 25165828
  63.5 2.0 %collective-permute-start.15 = (bf16[512,256]{1,0:T(8,128)(2,1)S(1)}, bf16[512,256]{1,0:T(8,128)(2,1)S(1)}, u32[]{:S(2)}, u32[]{:S(2)}) collective-permute-start(bf16[512,256]{1,0:T(8,128)(2,1)S(1)} %collective-permute-done.14.refs_0_), channel_id=1, source_target_pairs={{0,1},{1,0},{2,3},{3,2},{4,5},{5,4},{6,7},{7,6},{8,9},{9,8},{10,11... | collective-permute-start | bytes 786440 | tf_op jit(solution)/shard_map/ppermute | solution.py:27
  63.5 6.0 %collective-permute-start.9 = (bf16[512,256]{1,0:T(8,128)(2,1)S(1)}, bf16[512,256]{1,0:T(8,128)(2,1)S(1)}, u32[]{:S(2)}, u32[]{:S(2)}) collective-permute-start(bf16[512,256]{1,0:T(8,128)(2,1)S(1)} %collective-permute-done.8.refs_0_), channel_id=1, source_target_pairs={{0,1},{1,0},{2,3},{3,2},{4,5},{5,4},{6,7},{7,6},{8,9},{9,8},{10,11... | collective-permute-start | bytes 786440 | tf_op jit(solution)/shard_map/ppermute | solution.py:27
  65.2 4.1 %collective-permute-start.7 = (bf16[512,256]{1,0:T(8,128)(2,1)S(1)}, bf16[512,256]{1,0:T(8,128)(2,1)S(1)}, u32[]{:S(2)}, u32[]{:S(2)}) collective-permute-start(bf16[512,256]{1,0:T(8,128)(2,1)S(1)} %collective-permute-done.6.refs_0_), channel_id=1, source_target_pairs={{0,1},{1,0},{2,3},{3,2},{4,5},{5,4},{6,7},{7,6},{8,9},{9,8},{10,11... | collective-permute-start | bytes 786440 | tf_op jit(solution)/shard_map/ppermute | solution.py:27
  65.7 7.8 %copy-start = (bf16[1024,2048]{1,0:T(8,128)(2,1)S(1)}, bf16[1024,2048]{1,0:T(8,128)(2,1)}, u32[]{:S(2)}) copy-start(bf16[1024,2048]{1,0:T(8,128)(2,1)} %w_ref.23) | copy-start | bytes 12582916
  65.7 7.1 %collective-permute-start.18 = (bf16[4,32,128]{2,1,0:T(8,128)(2,1)S(1)}, bf16[4,32,128]{2,1,0:T(8,128)(2,1)S(1)}, u32[]{:S(2)}, u32[]{:S(2)}) collective-permute-start(bf16[4,32,128]{2,1,0:T(8,128)(2,1)S(1)} %constant_dynamic-update-slice_fusion.2.refs_0_), channel_id=1, source_target_pairs={{0,24},{8,16},{16,8},{24,0},{1,25},{9,17},{17,9},{25,1},{2,26},{10... | collective-permute-start | bytes 98312 | tf_op jit(solution)/shard_map/ppermute | solution.py:27
  68.2 5.2 %collective-permute-start.17 = (bf16[4,32,128]{2,1,0:T(8,128)(2,1)S(1)}, bf16[4,32,128]{2,1,0:T(8,128)(2,1)S(1)}, u32[]{:S(2)}, u32[]{:S(2)}) collective-permute-start(bf16[4,32,128]{2,1,0:T(8,128)(2,1)S(1)} %constant_dynamic-update-slice_fusion.2.refs_0_), channel_id=1, source_target_pairs={{0,16},{8,24},{16,0},{24,8},{1,17},{9,25},{17,1},{25,9},{2,18},{10... | collective-permute-start | bytes 98312 | tf_op jit(solution)/shard_map/ppermute | solution.py:27
  68.7 4.8 %collective-permute-start.16 = (bf16[4,32,128]{2,1,0:T(8,128)(2,1)S(1)}, bf16[4,32,128]{2,1,0:T(8,128)(2,1)S(1)}, u32[]{:S(2)}, u32[]{:S(2)}) collective-permute-start(bf16[4,32,128]{2,1,0:T(8,128)(2,1)S(1)} %constant_dynamic-update-slice_fusion.2.refs_0_), channel_id=1, source_target_pairs={{0,8},{8,0},{16,24},{24,16},{1,9},{9,1},{17,25},{25,17},{2,10},{10... | collective-permute-start | bytes 98312 | tf_op jit(solution)/shard_map/ppermute | solution.py:27
  69.7 5.0 %collective-permute-start.12 = (bf16[4,32,128]{2,1,0:T(8,128)(2,1)S(1)}, bf16[4,32,128]{2,1,0:T(8,128)(2,1)S(1)}, u32[]{:S(2)}, u32[]{:S(2)}) collective-permute-start(bf16[4,32,128]{2,1,0:T(8,128)(2,1)S(1)} %constant_dynamic-update-slice_fusion.refs_0_), channel_id=1, source_target_pairs={{0,24},{8,16},{16,8},{24,0},{1,25},{9,17},{17,9},{25,1},{2,26},{10... | collective-permute-start | bytes 98312 | tf_op jit(solution)/shard_map/ppermute | solution.py:27
  72.3 3.9 %collective-permute-start.11 = (bf16[4,32,128]{2,1,0:T(8,128)(2,1)S(1)}, bf16[4,32,128]{2,1,0:T(8,128)(2,1)S(1)}, u32[]{:S(2)}, u32[]{:S(2)}) collective-permute-start(bf16[4,32,128]{2,1,0:T(8,128)(2,1)S(1)} %constant_dynamic-update-slice_fusion.refs_0_), channel_id=1, source_target_pairs={{0,16},{8,24},{16,0},{24,8},{1,17},{9,25},{17,1},{25,9},{2,18},{10... | collective-permute-start | bytes 98312 | tf_op jit(solution)/shard_map/ppermute | solution.py:27
  72.9 4.0 %collective-permute-start.10 = (bf16[4,32,128]{2,1,0:T(8,128)(2,1)S(1)}, bf16[4,32,128]{2,1,0:T(8,128)(2,1)S(1)}, u32[]{:S(2)}, u32[]{:S(2)}) collective-permute-start(bf16[4,32,128]{2,1,0:T(8,128)(2,1)S(1)} %constant_dynamic-update-slice_fusion.refs_0_), channel_id=1, source_target_pairs={{0,8},{8,0},{16,24},{24,16},{1,9},{9,1},{17,25},{25,17},{2,10},{10... | collective-permute-start | bytes 98312 | tf_op jit(solution)/shard_map/ppermute | solution.py:27
  74.3 8.7 %collective-permute-start.20 = (bf16[1,512,256]{2,1,0:T(8,128)(2,1)S(1)}, bf16[1,512,256]{2,1,0:T(8,128)(2,1)S(1)}, u32[]{:S(2)}, u32[]{:S(2)}) collective-permute-start(bf16[1,512,256]{2,1,0:T(8,128)(2,1)S(1)} %get-tuple-element.70), channel_id=1, source_target_pairs={{0,1},{1,0},{2,3},{3,2},{4,5},{5,4},{6,7},{7,6},{8,9},{9,8},{10,11... | collective-permute-start | bytes 786440 | tf_op jit(solution)/shard_map/ppermute | solution.py:27
  78.8 8.2 %collective-permute-start.22 = (bf16[2,512,256]{2,1,0:T(8,128)(2,1)S(1)}, bf16[2,512,256]{2,1,0:T(8,128)(2,1)S(1)}, u32[]{:S(2)}, u32[]{:S(2)}) collective-permute-start(bf16[2,512,256]{2,1,0:T(8,128)(2,1)S(1)} %get-tuple-element.72), channel_id=1, source_target_pairs={{0,1},{1,0},{2,3},{3,2},{4,5},{5,4},{6,7},{7,6},{8,9},{9,8},{10,11... | collective-permute-start | bytes 1572872 | tf_op jit(solution)/shard_map/ppermute | solution.py:27
  79.7 11.6 %collective-permute-start.19 = (bf16[1,512,256]{2,1,0:T(8,128)(2,1)S(1)}, bf16[1,512,256]{2,1,0:T(8,128)(2,1)S(1)}, u32[]{:S(2)}, u32[]{:S(2)}) collective-permute-start(bf16[1,512,256]{2,1,0:T(8,128)(2,1)S(1)} %get-tuple-element.68), channel_id=1, source_target_pairs={{0,1},{1,0},{2,3},{3,2},{4,5},{5,4},{6,7},{7,6},{8,9},{9,8},{10,11... | collective-permute-start | bytes 786440 | tf_op jit(solution)/shard_map/ppermute | solution.py:27
  81.1 32.6 %slice-start = ((s8[8388608]{0:T(1024)(128)(4,1)}), s8[4194304]{0:T(1024)(128)(4,1)S(1)}, s32[]{:S(2)}) async-start(s8[8388608]{0:T(1024)(128)(4,1)} %bitcast.67), calls=%async_computation | async-start | bytes 8388608
  83.2 22.2 %collective-permute-start.21 = (bf16[512,256]{1,0:T(8,128)(2,1)S(1)}, bf16[512,256]{1,0:T(8,128)(2,1)S(1)}, u32[]{:S(2)}, u32[]{:S(2)}) collective-permute-start(bf16[512,256]{1,0:T(8,128)(2,1)S(1)} %fusion.3), channel_id=1, source_target_pairs={{0,4},{1,5},{2,6},{3,7},{4,0},{5,1},{6,2},{7,3},{8,12},{9,13},{10,... | collective-permute-start | bytes 786440 | tf_op jit(solution)/shard_map/ppermute | solution.py:27
  87.1 18.3 %collective-permute-start.24 = (bf16[512,256]{1,0:T(8,128)(2,1)S(1)}, bf16[512,256]{1,0:T(8,128)(2,1)S(1)}, u32[]{:S(2)}, u32[]{:S(2)}) collective-permute-start(bf16[512,256]{1,0:T(8,128)(2,1)S(1)} %get-tuple-element.88), channel_id=1, source_target_pairs={{0,6},{1,7},{2,4},{3,5},{4,2},{5,3},{6,0},{7,1},{8,14},{9,15},{10,... | collective-permute-start | bytes 786440 | tf_op jit(solution)/shard_map/ppermute | solution.py:27
  90.5 23.2 %slice-start.1 = ((s8[8388608]{0:T(1024)(128)(4,1)}), s8[4194304]{0:T(1024)(128)(4,1)S(1)}, s32[]{:S(2)}) async-start(s8[8388608]{0:T(1024)(128)(4,1)} %bitcast.67), calls=%async_computation.1 | async-start | bytes 8388608
  90.5 15.8 %collective-permute-start.23 = (bf16[512,256]{1,0:T(8,128)(2,1)S(1)}, bf16[512,256]{1,0:T(8,128)(2,1)S(1)}, u32[]{:S(2)}, u32[]{:S(2)}) collective-permute-start(bf16[512,256]{1,0:T(8,128)(2,1)S(1)} %get-tuple-element.89), channel_id=1, source_target_pairs={{0,2},{1,3},{2,0},{3,1},{4,6},{5,7},{6,4},{7,5},{8,10},{9,11},{10,... | collective-permute-start | bytes 786440 | tf_op jit(solution)/shard_map/ppermute | solution.py:27
  106.4 24.3 %collective-permute-start.33 = (bf16[512,256]{1,0:T(8,128)(2,1)S(1)}, bf16[512,256]{1,0:T(8,128)(2,1)S(1)}, u32[]{:S(2)}, u32[]{:S(2)}) collective-permute-start(bf16[512,256]{1,0:T(8,128)(2,1)S(1)} %shard_map.121.refs_0_), channel_id=1, source_target_pairs={{0,4},{1,5},{2,6},{3,7},{4,0},{5,1},{6,2},{7,3},{8,12},{9,13},{10,... | collective-permute-start | bytes 786440 | tf_op jit(solution)/shard_map/ppermute | solution.py:27
  113.0 20.0 %collective-permute-start.32 = (bf16[512,256]{1,0:T(8,128)(2,1)S(1)}, bf16[512,256]{1,0:T(8,128)(2,1)S(1)}, u32[]{:S(2)}, u32[]{:S(2)}) collective-permute-start(bf16[512,256]{1,0:T(8,128)(2,1)S(1)} %shard_map.121.refs_0_), channel_id=1, source_target_pairs={{0,1},{1,0},{2,3},{3,2},{4,5},{5,4},{6,7},{7,6},{8,9},{9,8},{10,11... | collective-permute-start | bytes 786440 | tf_op jit(solution)/shard_map/ppermute | solution.py:27
  113.0 17.8 %collective-permute-start.27 = (bf16[512,256]{1,0:T(8,128)(2,1)S(1)}, bf16[512,256]{1,0:T(8,128)(2,1)S(1)}, u32[]{:S(2)}, u32[]{:S(2)}) collective-permute-start(bf16[512,256]{1,0:T(8,128)(2,1)S(1)} %shard_map.121.refs_0_), channel_id=1, source_target_pairs={{0,6},{1,7},{2,4},{3,5},{4,2},{5,3},{6,0},{7,1},{8,14},{9,15},{10,... | collective-permute-start | bytes 786440 | tf_op jit(solution)/shard_map/ppermute | solution.py:27
  113.5 19.4 %collective-permute-start.25 = (bf16[512,256]{1,0:T(8,128)(2,1)S(1)}, bf16[512,256]{1,0:T(8,128)(2,1)S(1)}, u32[]{:S(2)}, u32[]{:S(2)}) collective-permute-start(bf16[512,256]{1,0:T(8,128)(2,1)S(1)} %shard_map.121.refs_0_), channel_id=1, source_target_pairs={{0,2},{1,3},{2,0},{3,1},{4,6},{5,7},{6,4},{7,5},{8,10},{9,11},{10,... | collective-permute-start | bytes 786440 | tf_op jit(solution)/shard_map/ppermute | solution.py:27
  130.7 7.3 %collective-permute-start.34 = (bf16[512,256]{1,0:T(8,128)(2,1)S(1)}, bf16[512,256]{1,0:T(8,128)(2,1)S(1)}, u32[]{:S(2)}, u32[]{:S(2)}) collective-permute-start(bf16[512,256]{1,0:T(8,128)(2,1)S(1)} %collective-permute-done.33.refs_0_), channel_id=1, source_target_pairs={{0,1},{1,0},{2,3},{3,2},{4,5},{5,4},{6,7},{7,6},{8,9},{9,8},{10,11... | collective-permute-start | bytes 786440 | tf_op jit(solution)/shard_map/ppermute | solution.py:27
  130.7 4.8 %collective-permute-start.28 = (bf16[512,256]{1,0:T(8,128)(2,1)S(1)}, bf16[512,256]{1,0:T(8,128)(2,1)S(1)}, u32[]{:S(2)}, u32[]{:S(2)}) collective-permute-start(bf16[512,256]{1,0:T(8,128)(2,1)S(1)} %collective-permute-done.27.refs_0_), channel_id=1, source_target_pairs={{0,1},{1,0},{2,3},{3,2},{4,5},{5,4},{6,7},{7,6},{8,9},{9,8},{10,11... | collective-permute-start | bytes 786440 | tf_op jit(solution)/shard_map/ppermute | solution.py:27
  132.9 2.8 %collective-permute-start.26 = (bf16[512,256]{1,0:T(8,128)(2,1)S(1)}, bf16[512,256]{1,0:T(8,128)(2,1)S(1)}, u32[]{:S(2)}, u32[]{:S(2)}) collective-permute-start(bf16[512,256]{1,0:T(8,128)(2,1)S(1)} %collective-permute-done.25.refs_0_), channel_id=1, source_target_pairs={{0,1},{1,0},{2,3},{3,2},{4,5},{5,4},{6,7},{7,6},{8,9},{9,8},{10,11... | collective-permute-start | bytes 786440 | tf_op jit(solution)/shard_map/ppermute | solution.py:27
  136.0 16.6 %collective-permute-start.31 = (bf16[4,32,128]{2,1,0:T(8,128)(2,1)S(1)}, bf16[4,32,128]{2,1,0:T(8,128)(2,1)S(1)}, u32[]{:S(2)}, u32[]{:S(2)}) collective-permute-start(bf16[4,32,128]{2,1,0:T(8,128)(2,1)S(1)} %constant_dynamic-update-slice_fusion.4.refs_0_), channel_id=1, source_target_pairs={{0,24},{8,16},{16,8},{24,0},{1,25},{9,17},{17,9},{25,1},{2,26},{10... | collective-permute-start | bytes 98312 | tf_op jit(solution)/shard_map/ppermute | solution.py:27
  137.5 15.0 %collective-permute-start.30 = (bf16[4,32,128]{2,1,0:T(8,128)(2,1)S(1)}, bf16[4,32,128]{2,1,0:T(8,128)(2,1)S(1)}, u32[]{:S(2)}, u32[]{:S(2)}) collective-permute-start(bf16[4,32,128]{2,1,0:T(8,128)(2,1)S(1)} %constant_dynamic-update-slice_fusion.4.refs_0_), channel_id=1, source_target_pairs={{0,16},{8,24},{16,0},{24,8},{1,17},{9,25},{17,1},{25,9},{2,18},{10... | collective-permute-start | bytes 98312 | tf_op jit(solution)/shard_map/ppermute | solution.py:27
  138.3 9.8 %collective-permute-start.37 = (bf16[4,32,128]{2,1,0:T(8,128)(2,1)S(1)}, bf16[4,32,128]{2,1,0:T(8,128)(2,1)S(1)}, u32[]{:S(2)}, u32[]{:S(2)}) collective-permute-start(bf16[4,32,128]{2,1,0:T(8,128)(2,1)S(1)} %constant_dynamic-update-slice_fusion.6.refs_0_), channel_id=1, source_target_pairs={{0,24},{8,16},{16,8},{24,0},{1,25},{9,17},{17,9},{25,1},{2,26},{10... | collective-permute-start | bytes 98312 | tf_op jit(solution)/shard_map/ppermute | solution.py:27
  140.8 8.8 %collective-permute-start.36 = (bf16[4,32,128]{2,1,0:T(8,128)(2,1)S(1)}, bf16[4,32,128]{2,1,0:T(8,128)(2,1)S(1)}, u32[]{:S(2)}, u32[]{:S(2)}) collective-permute-start(bf16[4,32,128]{2,1,0:T(8,128)(2,1)S(1)} %constant_dynamic-update-slice_fusion.6.refs_0_), channel_id=1, source_target_pairs={{0,16},{8,24},{16,0},{24,8},{1,17},{9,25},{17,1},{25,9},{2,18},{10... | collective-permute-start | bytes 98312 | tf_op jit(solution)/shard_map/ppermute | solution.py:27
  141.3 8.3 %collective-permute-start.35 = (bf16[4,32,128]{2,1,0:T(8,128)(2,1)S(1)}, bf16[4,32,128]{2,1,0:T(8,128)(2,1)S(1)}, u32[]{:S(2)}, u32[]{:S(2)}) collective-permute-start(bf16[4,32,128]{2,1,0:T(8,128)(2,1)S(1)} %constant_dynamic-update-slice_fusion.6.refs_0_), channel_id=1, source_target_pairs={{0,8},{8,0},{16,24},{24,16},{1,9},{9,1},{17,25},{25,17},{2,10},{10... | collective-permute-start | bytes 98312 | tf_op jit(solution)/shard_map/ppermute | solution.py:27
  148.1 4.5 %collective-permute-start.29 = (bf16[4,32,128]{2,1,0:T(8,128)(2,1)S(1)}, bf16[4,32,128]{2,1,0:T(8,128)(2,1)S(1)}, u32[]{:S(2)}, u32[]{:S(2)}) collective-permute-start(bf16[4,32,128]{2,1,0:T(8,128)(2,1)S(1)} %constant_dynamic-update-slice_fusion.4.refs_0_), channel_id=1, source_target_pairs={{0,8},{8,0},{16,24},{24,16},{1,9},{9,1},{17,25},{25,17},{2,10},{10... | collective-permute-start | bytes 98312 | tf_op jit(solution)/shard_map/ppermute | solution.py:27

commit v3 on v2

--- a/solution.py
+++ b/solution.py
@@ -72,7 +72,8 @@
 
 
 def row_mask(rows, lanes, per, count, wanted, axis):
-    return lax.broadcasted_iota(jnp.int32, (rows, lanes), axis) // per % count == wanted
+    at = lax.broadcasted_iota(jnp.int32, (rows, lanes), axis)
+    return lax.rem(lax.div(at, jnp.int32(per)), jnp.int32(count)) == wanted
 
 
 def spread_rows(kept, nbr, per):
@@ -336,20 +337,23 @@
     return (weight.astype(F32) - 0.1 * change).astype(BF)
 
 
-def first_kernel(chips, start, core, place, w_ref, x_ref, out_ref, w_buf, x_buf, sum_ref, sems):
-    count, rows, tile = w_buf.shape
+def first_kernel(chips, start, cores, place, w_ref, x_ref, *refs):
+    out_refs, (w_buf, x_buf, sum_ref, sems) = refs[: len(cores)], refs[len(cores) :]
+    total, rows, tile = w_buf.shape
+    count = total // len(cores)
     step = x_buf.shape[2]
+    tiles = [CORES * (start + at) + core for core in cores for at in range(count)]
     copies = []
     for k in range(rows // step):
         span = slice(k * step, (k + 1) * step)
         copies.append([])
-        for at in range(count):
-            column = natural(CORES * (start + at) + core, CORES * chips, place) * tile
+        for at, position in enumerate(tiles):
+            column = natural(position, CORES * chips, place) * tile
             source = w_ref.at[span, pl.ds(pl.multiple_of(column, tile), tile)]
             target = w_buf.at[at, span, :]
             copies[k].append(pltpu.make_async_copy(source, target, sems.at[k, at]))
         source = x_ref.at[0, :, span]
-        copies[k].append(pltpu.make_async_copy(source, x_buf.at[k], sems.at[k, count]))
+        copies[k].append(pltpu.make_async_copy(source, x_buf.at[k], sems.at[k, total]))
     for group in copies:
         for copy in group:
             copy.start()
@@ -357,38 +361,40 @@
         span = slice(k * step, (k + 1) * step)
         for copy in group:
             copy.wait()
-        for at in range(count):
+        for at in range(total):
             part = dot(x_buf[k], w_buf[at, span, :])
             if k > 0:
                 part = part + sum_ref[at]
             if k < len(copies) - 1:
                 sum_ref[at] = part
             else:
-                out_ref[at] = part.astype(BF)
-
-
-def first(place, weight, acts, tile, start, core, count):
+                out_refs[at // count][at % count] = part.astype(BF)
+
+
+def first(place, weight, acts, tile, start, cores, count):
     rows = weight.shape[0]
     tokens = acts.shape[1]
     step = 256
     hbm = pl.BlockSpec(memory_space=pltpu.HBM)
+    total = count * len(cores)
+    block = (count, tokens, tile)
     return pl.pallas_call(
-        functools.partial(first_kernel, weight.shape[1] // tile // CORES, start, core),
+        functools.partial(first_kernel, weight.shape[1] // tile // CORES, start, cores),
         grid_spec=pltpu.PrefetchScalarGridSpec(
             num_scalar_prefetch=1,
             grid=(1,),
             in_specs=[hbm, hbm],
-            out_specs=pl.BlockSpec((count, tokens, tile), lambda j, p: (0, 0, 0)),
+            out_specs=[pl.BlockSpec(block, lambda j, p: (0, 0, 0)) for _ in cores],
             scratch_shapes=[
-                pltpu.VMEM((count, rows, tile), BF),
+                pltpu.VMEM((total, rows, tile), BF),
                 pltpu.VMEM((rows // step, tokens, step), BF),
-                pltpu.VMEM((count, tokens, tile), F32),
-                pltpu.SemaphoreType.DMA((rows // step, count + 1)),
+                pltpu.VMEM((total, tokens, tile), F32),
+                pltpu.SemaphoreType.DMA((rows // step, total + 1)),
             ],
         ),
-        out_shape=shaped((count, tokens, tile), BF),
+        out_shape=[shaped(block, BF) for _ in cores],
         compiler_params=room(52),
-        cost_estimate=cost(2 * tokens * rows * tile * count, 2 * rows * (tile * count + tokens)),
+        cost_estimate=cost(2 * tokens * rows * tile * total, 2 * rows * (tile * total + tokens)),
         name="first",
     )(place, weight, acts)
 
@@ -518,10 +524,14 @@
         found_all = []
         for group, (start, size, chunk, skip) in enumerate(groups):
             found = [None, None]
+            if step == 0 and group != 1:
+                found[1], found[0] = first(place, weight, inputs, tile, start, (1, 0), size)
             for core in (1, 0):
-                if step == 0:
-                    found[core] = first(place, weight, inputs, tile, start, core, size)
-                else:
+                if step == 0 and group == 1:
+                    (found[core],) = first(
+                        place, weight, inputs, tile, start, (core,), size
+                    )
+                elif step > 0:
                     weights[group][core], found[core] = forward(
                         place,
                         weight,

time: 157 us -> 153 us (0.975)
  Pallas kernels: 49.6 us -> 45.5 us
    pallas_call x6 -> x4, Pallas kernels: 12.1 us -> 8.18 us  [first(): pl.pallas_call(functools.partial(first_kernel, weight.shape[1] // tile //...]
    unnamed x29 -> x27, local copies, waits for them, and re-layouts: 4.41 us -> 4.4 us
  transfers between devices with their start and end apart: 38 -> 38, of which waited for: 11 -> 11; matrix products, arithmetic and copies ran while one was open for 3% -> 4% of each run, Pallas kernels for 29% -> 27%
where the time goes in v3:
time: 153 us; the launch traced here: 151 us
  waiting for transfers between devices  53 us (35%)
  Pallas kernels  45.5 us (30%)
  starting transfers between devices  41.3 us (27%)
  local copies, waits for them, and re-layouts  6.32 us (4%)
  other arithmetic  3.83 us (3%)
    ppermute x38, waiting for transfers between devices, swap(): return lax.ppermute(value, axis, [(at, at ^ mask) for at in range(size)])  53 us
    ppermute x38, starting transfers between devices, swap(): return lax.ppermute(value, axis, [(at, at ^ mask) for at in range(size)])  41.3 us
    pallas_call x28, Pallas kernels, call(): pl.pallas_call(kernel, grid_spec=pltpu.PrefetchScalarGridSpec(num_scalar_...  37.3 us
    pallas_call x4, Pallas kernels, first(): pl.pallas_call(functools.partial(first_kernel, weight.shape[1] // tile //...  8.18 us
    unnamed x27, local copies, waits for them, and re-layouts  4.4 us
  transfers between devices with their start and end apart: 38, of which 11 were waited for; matrix products, arithmetic and copies ran while one was open for 4% of the time, Pallas kernels for 27%

profile of v3, /device:TPU:0, one launch (start us, length us, event | category | flops | bytes accessed | tf_op | source)
XLA Modules:
  0.0 151.2 jit_solution(16276894540203988195)
XLA Ops:
  0.6 2.0 %first.7 = (bf16[1,512,256]{2,1,0:T(8,128)(2,1)S(1)}, bf16[1,512,256]{2,1,0:T(8,128)(2,1)S(1)}) custom-call(s32[1]{0:T(128)} %bitcast.place, bf16[1024,2048]{1,0:T(8,128)(2,1)} %w_ref.19, bf16[2,512,1024]{2,1,0:T(8,128)(2,1)} %x_ref.23), custom_call_target="tpu_custom_call" | custom-call | flops 536870912 | bytes 2097152 | tf_op jit(solution)/shard_map/first/pallas_call | solution.py:381
  2.7 0.6 collective-permute-start.2
  3.2 2.0 %first.6 = (bf16[1,512,256]{2,1,0:T(8,128)(2,1)S(1)}, bf16[1,512,256]{2,1,0:T(8,128)(2,1)S(1)}) custom-call(s32[1]{0:T(128)} %bitcast.place, bf16[1024,2048]{1,0:T(8,128)(2,1)} %w_ref.19, bf16[2,512,1024]{2,1,0:T(8,128)(2,1)} %x_ref.23), custom_call_target="tpu_custom_call" | custom-call | flops 536870912 | bytes 2097152 | tf_op jit(solution)/shard_map/first/pallas_call | solution.py:381
  5.4 2.0 %first.5 = bf16[2,512,256]{2,1,0:T(8,128)(2,1)S(1)} custom-call(s32[1]{0:T(128)} %bitcast.place, bf16[1024,2048]{1,0:T(8,128)(2,1)} %w_ref.19, bf16[2,512,1024]{2,1,0:T(8,128)(2,1)} %x_ref.23), custom_call_target="tpu_custom_call" | custom-call | flops 536870912 | bytes 2097152 | tf_op jit(solution)/shard_map/first/pallas_call | solution.py:381
  7.4 0.6 collective-permute-start
  8.0 2.0 %first.4 = bf16[2,512,256]{2,1,0:T(8,128)(2,1)S(1)} custom-call(s32[1]{0:T(128)} %bitcast.place, bf16[1024,2048]{1,0:T(8,128)(2,1)} %w_ref.19, bf16[2,512,1024]{2,1,0:T(8,128)(2,1)} %x_ref.23), custom_call_target="tpu_custom_call" | custom-call | flops 536870912 | bytes 2097152 | tf_op jit(solution)/shard_map/first/pallas_call | solution.py:381
  10.1 0.8 fusion.2
  10.8 3.6 %collective-permute-start.3 = (bf16[512,256]{1,0:T(8,128)(2,1)}, bf16[512,256]{1,0:T(8,128)(2,1)S(1)}, u32[]{:S(2)}, u32[]{:S(2)}) collective-permute-start(bf16[512,256]{1,0:T(8,128)(2,1)} %fusion.2), channel_id=1, source_target_pairs={{0,4},{1,5},{2,6},{3,7},{4,0},{5,1},{6,2},{7,3},{8,12},{9,13},{10,... | collective-permute-start | bytes 786440 | tf_op jit(solution)/shard_map/ppermute | solution.py:27
  14.4 1.0 add_bitcast_fusion.1.total_ref
  15.5 0.9 fusion.1
  16.4 0.8 fusion.10
  18.7 1.6 %collective-permute-start.4 = (bf16[512,256]{1,0:T(8,128)(2,1)}, bf16[512,256]{1,0:T(8,128)(2,1)S(1)}, u32[]{:S(2)}, u32[]{:S(2)}) collective-permute-start(bf16[512,256]{1,0:T(8,128)(2,1)} %get-tuple-element.57), channel_id=1, source_target_pairs={{0,2},{1,3},{2,0},{3,1},{4,6},{5,7},{6,4},{7,5},{8,10},{9,11},{10,... | collective-permute-start | bytes 786440 | tf_op jit(solution)/shard_map/ppermute | solution.py:27
  20.5 0.8 copy-done.5
  21.4 1.6 %shard_map.112 = (bf16[8,128,256]{2,1,0:T(8,128)(2,1)S(1)}, bf16[8,128,96]{2,1,0:T(8,128)(2,1)S(1)}, bf16[8,64,128]{2,1,0:T(8,128)(2,1)S(1)}) custom-call(s32[1]{0:T(128)} %bitcast.place, s32[8,1,256]{2,1,0:T(1,128)S(1)} %reshape.67.all_ref, s32[8,1,96]{2,1,0:T(1,128)S(1)} %bitcast.77, bf16[128,256]{1,0:T(8,128)(2,1)S(1)} %copy-done.4, ...), custom_call_target="tpu_custom_call" | custom-call | flops 234881024 | bytes 2097152 | tf_op jit(solution)/shard_map/pallas_call | solution.py:59
  23.0 1.6 %shard_map.104 = (bf16[8,128,256]{2,1,0:T(8,128)(2,1)S(1)}, bf16[8,128,96]{2,1,0:T(8,128)(2,1)S(1)}, bf16[8,64,128]{2,1,0:T(8,128)(2,1)S(1)}) custom-call(s32[1]{0:T(128)} %bitcast.place, s32[8,1,256]{2,1,0:T(1,128)S(1)} %reshape.66.all_ref, s32[8,1,96]{2,1,0:T(1,128)S(1)} %bitcast.78, bf16[128,256]{1,0:T(8,128)(2,1)S(1)} %copy-done.4, ...), custom_call_target="tpu_custom_call" | custom-call | flops 234881024 | bytes 2097152 | tf_op jit(solution)/shard_map/pallas_call | solution.py:59
  24.7 0.8 shard_map.105
  25.5 0.8 shard_map.113
  26.3 1.1 collective-permute-done.3.refs_0_
  27.5 9.9 %collective-permute-done.4.refs_1_ = bf16[512,256]{1,0:T(8,128)(2,1)S(1)} collective-permute-done((bf16[512,256]{1,0:T(8,128)(2,1)}, bf16[512,256]{1,0:T(8,128)(2,1)S(1)}, u32[]{:S(2)}, u32[]{:S(2)}) %collective-permute-start.4) | collective-permute-done | bytes 262176 | tf_op jit(solution)/shard_map/ppermute | solution.py:27
  37.5 3.8 %collective-permute-start.14 = (bf16[512,256]{1,0:T(8,128)(2,1)S(1)}, bf16[512,256]{1,0:T(8,128)(2,1)S(1)}, u32[]{:S(2)}, u32[]{:S(2)}) collective-permute-start(bf16[512,256]{1,0:T(8,128)(2,1)S(1)} %shard_map.107.refs_0_), channel_id=1, source_target_pairs={{0,4},{1,5},{2,6},{3,7},{4,0},{5,1},{6,2},{7,3},{8,12},{9,13},{10,... | collective-permute-start | bytes 786440 | tf_op jit(solution)/shard_map/ppermute | solution.py:27
  41.4 0.5 collective-permute-start.8
  42.1 3.4 %copy-done.2 = f32[1,1024,2048]{2,1,0:T(8,128)S(1)} copy-done((f32[1,1024,2048]{2,1,0:T(8,128)S(1)}, f32[1,1024,2048]{2,1,0:T(8,128)}, u32[]{:S(2)}) %copy-start.2) | copy-done | bytes 8388632
  45.5 2.4 %shard_map.106.old_ref = f32[8,32,128]{2,1,0:T(8,128)S(1)} custom-call(s32[1]{0:T(128)} %bitcast.place, bf16[8,64,128]{2,1,0:T(8,128)(2,1)S(1)} %get-tuple-element.51.kept_ref, f32[1,1024,2048]{2,1,0:T(8,128)S(1)} %copy-done.2), custom_call_target="tpu_custom_call" | custom-call | flops 268435456 | bytes 8388608 | tf_op jit(solution)/shard_map/pallas_call | solution.py:59
  47.9 11.6 %collective-permute-done.14.refs_0_ = bf16[512,256]{1,0:T(8,128)(2,1)S(1)} collective-permute-done((bf16[512,256]{1,0:T(8,128)(2,1)S(1)}, bf16[512,256]{1,0:T(8,128)(2,1)S(1)}, u32[]{:S(2)}, u32[]{:S(2)}) %collective-permute-start.14) | collective-permute-done | bytes 262176 | tf_op jit(solution)/shard_map/ppermute | solution.py:27
  59.5 0.5 collective-permute-start.9
  60.1 1.2 collective-permute-done.6.refs_0_
  61.8 2.5 %collective-permute-start.18 = (bf16[4,32,128]{2,1,0:T(8,128)(2,1)S(1)}, bf16[4,32,128]{2,1,0:T(8,128)(2,1)S(1)}, u32[]{:S(2)}, u32[]{:S(2)}) collective-permute-start(bf16[4,32,128]{2,1,0:T(8,128)(2,1)S(1)} %constant_dynamic-update-slice_fusion.2.refs_0_), channel_id=1, source_target_pairs={{0,24},{8,16},{16,8},{24,0},{1,25},{9,17},{17,9},{25,1},{2,26},{10... | collective-permute-start | bytes 98312 | tf_op jit(solution)/shard_map/ppermute | solution.py:27
  64.3 0.5 collective-permute-start.17
  64.8 0.5 collective-permute-start.16
  65.8 2.5 %collective-permute-start.12 = (bf16[4,32,128]{2,1,0:T(8,128)(2,1)S(1)}, bf16[4,32,128]{2,1,0:T(8,128)(2,1)S(1)}, u32[]{:S(2)}, u32[]{:S(2)}) collective-permute-start(bf16[4,32,128]{2,1,0:T(8,128)(2,1)S(1)} %constant_dynamic-update-slice_fusion.refs_0_), channel_id=1, source_target_pairs={{0,24},{8,16},{16,8},{24,0},{1,25},{9,17},{17,9},{25,1},{2,26},{10... | collective-permute-start | bytes 98312 | tf_op jit(solution)/shard_map/ppermute | solution.py:27
  68.3 0.5 collective-permute-start.11
  68.9 0.6 collective-permute-start.10
  69.6 0.8 shard_map.120
  70.5 0.3 collective-permute-done.12.refs_3_
  70.8 1.5 collective-permute-done.11.refs_2_
  72.2 0.6 collective-permute-done.10.refs_1_
  72.9 1.9 %shard_map.111 = (bf16[2,1024,256]{2,1,0:T(8,128)(2,1)S(1)}, bf16[2,512,256]{2,1,0:T(8,128)(2,1)S(1)}) custom-call(s32[1]{0:T(128)} %bitcast.place, bf16[1024,2048]{1,0:T(8,128)(2,1)S(1)} %copy-done, bf16[2,512,1024]{2,1,0:T(8,128)(2,1)S(1)} %copy-done.1, bf16[8,128,256]{2,1,0:T(8,128)(2,1)S(1)} %get-tuple-element.50.dec_ref, ...), custom_call_target="tpu_custom_call" | custom-call | flops 536870912 | bytes 2097152 | tf_op jit(solution)/shard_map/pallas_call | solution.py:59
  74.9 0.8 shard_map.118
  75.7 0.6 collective-permute-start.19
  76.3 0.8 shard_map.119
  77.1 1.9 %shard_map.110 = (bf16[2,1024,256]{2,1,0:T(8,128)(2,1)S(1)}, bf16[2,512,256]{2,1,0:T(8,128)(2,1)S(1)}) custom-call(s32[1]{0:T(128)} %bitcast.place, bf16[1024,2048]{1,0:T(8,128)(2,1)S(1)} %copy-done, bf16[2,512,1024]{2,1,0:T(8,128)(2,1)S(1)} %copy-done.1, bf16[8,128,256]{2,1,0:T(8,128)(2,1)S(1)} %get-tuple-element.50.dec_ref, ...), custom_call_target="tpu_custom_call" | custom-call | flops 536870912 | bytes 2097152 | tf_op jit(solution)/shard_map/pallas_call | solution.py:59
  79.1 3.9 %collective-permute-start.21 = (bf16[512,256]{1,0:T(8,128)(2,1)S(1)}, bf16[512,256]{1,0:T(8,128)(2,1)S(1)}, u32[]{:S(2)}, u32[]{:S(2)}) collective-permute-start(bf16[512,256]{1,0:T(8,128)(2,1)S(1)} %fusion.3), channel_id=1, source_target_pairs={{0,4},{1,5},{2,6},{3,7},{4,0},{5,1},{6,2},{7,3},{8,12},{9,13},{10,... | collective-permute-start | bytes 786440 | tf_op jit(solution)/shard_map/ppermute | solution.py:27
  83.1 3.3 %collective-permute-start.24 = (bf16[512,256]{1,0:T(8,128)(2,1)S(1)}, bf16[512,256]{1,0:T(8,128)(2,1)S(1)}, u32[]{:S(2)}, u32[]{:S(2)}) collective-permute-start(bf16[512,256]{1,0:T(8,128)(2,1)S(1)} %get-tuple-element.96), channel_id=1, source_target_pairs={{0,6},{1,7},{2,4},{3,5},{4,2},{5,3},{6,0},{7,1},{8,14},{9,15},{10,... | collective-permute-start | bytes 786440 | tf_op jit(solution)/shard_map/ppermute | solution.py:27
  86.4 0.8 shard_map.117
  87.3 14.1 %collective-permute-done.21.refs_0_ = bf16[512,256]{1,0:T(8,128)(2,1)S(1)} collective-permute-done((bf16[512,256]{1,0:T(8,128)(2,1)S(1)}, bf16[512,256]{1,0:T(8,128)(2,1)S(1)}, u32[]{:S(2)}, u32[]{:S(2)}) %collective-permute-start.21) | collective-permute-done | bytes 262176 | tf_op jit(solution)/shard_map/ppermute | solution.py:27
  101.4 0.9 collective-permute-done.23.refs_1_
  102.4 6.5 %collective-permute-start.33 = (bf16[512,256]{1,0:T(8,128)(2,1)S(1)}, bf16[512,256]{1,0:T(8,128)(2,1)S(1)}, u32[]{:S(2)}, u32[]{:S(2)}) collective-permute-start(bf16[512,256]{1,0:T(8,128)(2,1)S(1)} %shard_map.121.refs_0_), channel_id=1, source_target_pairs={{0,4},{1,5},{2,6},{3,7},{4,0},{5,1},{6,2},{7,3},{8,12},{9,13},{10,... | collective-permute-start | bytes 786440 | tf_op jit(solution)/shard_map/ppermute | solution.py:27
  108.9 0.6 collective-permute-start.27
  109.7 7.0 %shard_map.116 = (f32[8,1024,256]{2,1,0:T(8,128)S(1)}, f32[8,32,128]{2,1,0:T(8,128)S(1)}) custom-call(s32[1]{0:T(128)} %bitcast.place, bf16[1024,512]{1,0:T(8,128)(2,1)S(1)} %get-tuple-element.66.xt_ref, bf16[8,512,256]{2,1,0:T(8,128)(2,1)S(1)} %bitcast_dynamic-update-slice_fusion.e_ref, f32[1,1024,2048]{2,1,0:T(8,128)S(1)} %bitcast.68, ...), custom_call_target="tpu_custom_call" | custom-call | flops 2147483648 | bytes 16777216 | tf_op jit(solution)/shard_map/pallas_call | solution.py:59
  116.7 9.9 %collective-permute-done.33.refs_0_ = bf16[512,256]{1,0:T(8,128)(2,1)S(1)} collective-permute-done((bf16[512,256]{1,0:T(8,128)(2,1)S(1)}, bf16[512,256]{1,0:T(8,128)(2,1)S(1)}, u32[]{:S(2)}, u32[]{:S(2)}) %collective-permute-start.33) | collective-permute-done | bytes 262176 | tf_op jit(solution)/shard_map/ppermute | solution.py:27
  126.6 0.5 collective-permute-start.28
  127.1 1.8 %collective-permute-done.25.refs_0_ = bf16[512,256]{1,0:T(8,128)(2,1)S(1)} collective-permute-done((bf16[512,256]{1,0:T(8,128)(2,1)S(1)}, bf16[512,256]{1,0:T(8,128)(2,1)S(1)}, u32[]{:S(2)}, u32[]{:S(2)}) %collective-permute-start.25) | collective-permute-done | bytes 262176 | tf_op jit(solution)/shard_map/ppermute | solution.py:27
  129.2 2.2 %shard_map.129.refs_0_ = f32[1,1024,2048]{2,1,0:T(8,128)} custom-call(s32[1]{0:T(128)} %bitcast.place, bf16[1024,512]{1,0:T(8,128)(2,1)S(1)} %get-tuple-element.89.xt_ref, bf16[2,512,256]{2,1,0:T(8,128)(2,1)S(1)} %pad_maximum_fusion.2.e_ref, f32[8,1024,256]{2,1,0:T(8,128)S(1)} %get-tuple-element.90.m_ref, bf16[8,128,96]{2,1,0:T(8,128)(2,1)S(1)} %get-tuple-element.91.dec_ref, ...), custom_call_target="tpu_custom_call" | custom-call | flops 536870912 | bytes 4194304 | tf_op jit(solution)/shard_map/pallas_call | solution.py:59
  131.9 1.6 %collective-permute-start.31 = (bf16[4,32,128]{2,1,0:T(8,128)(2,1)S(1)}, bf16[4,32,128]{2,1,0:T(8,128)(2,1)S(1)}, u32[]{:S(2)}, u32[]{:S(2)}) collective-permute-start(bf16[4,32,128]{2,1,0:T(8,128)(2,1)S(1)} %constant_dynamic-update-slice_fusion.4.refs_0_), channel_id=1, source_target_pairs={{0,24},{8,16},{16,8},{24,0},{1,25},{9,17},{17,9},{25,1},{2,26},{10... | collective-permute-start | bytes 98312 | tf_op jit(solution)/shard_map/ppermute | solution.py:27
  133.5 0.5 collective-permute-start.30
  134.2 2.5 %collective-permute-start.37 = (bf16[4,32,128]{2,1,0:T(8,128)(2,1)S(1)}, bf16[4,32,128]{2,1,0:T(8,128)(2,1)S(1)}, u32[]{:S(2)}, u32[]{:S(2)}) collective-permute-start(bf16[4,32,128]{2,1,0:T(8,128)(2,1)S(1)} %constant_dynamic-update-slice_fusion.6.refs_0_), channel_id=1, source_target_pairs={{0,24},{8,16},{16,8},{24,0},{1,25},{9,17},{17,9},{25,1},{2,26},{10... | collective-permute-start | bytes 98312 | tf_op jit(solution)/shard_map/ppermute | solution.py:27
  136.8 0.5 collective-permute-start.36
  137.3 0.5 collective-permute-start.35
  137.9 2.2 %shard_map.130.refs_0_ = f32[1,1024,2048]{2,1,0:T(8,128)} custom-call(s32[1]{0:T(128)} %bitcast.place, bf16[1024,512]{1,0:T(8,128)(2,1)S(1)} %get-tuple-element.89.xt_ref, bf16[2,512,256]{2,1,0:T(8,128)(2,1)S(1)} %pad_maximum_fusion.1.e_ref, f32[8,1024,256]{2,1,0:T(8,128)S(1)} %get-tuple-element.90.m_ref, ...), custom_call_target="tpu_custom_call", output_to_operand_aliasing={{}: (6, {})} | custom-call | flops 536870912 | bytes 4194304 | tf_op jit(solution)/shard_map/pallas_call | solution.py:59
  140.3 3.8 %shard_map.131 = f32[1,1024,2048]{2,1,0:T(8,128)} custom-call(s32[1]{0:T(128)} %bitcast.place, bf16[1024,512]{1,0:T(8,128)(2,1)S(1)} %get-tuple-element.89.xt_ref, bf16[4,512,256]{2,1,0:T(8,128)(2,1)S(1)} %pad_maximum_fusion.e_ref, f32[8,1024,256]{2,1,0:T(8,128)S(1)} %get-tuple-element.90.m_ref, ...), custom_call_target="tpu_custom_call", output_to_operand_aliasing={{}: (6, {})} | custom-call | flops 1073741824 | bytes 8388608 | tf_op jit(solution)/shard_map/pallas_call | solution.py:59
  144.0 1.5 collective-permute-start.29
  145.5 1.5 shard_map.126.refs_4_
  147.0 1.5 shard_map.127.refs_4_
  148.5 2.7 %shard_map.128 = bf16[1024,2048]{1,0:T(8,128)(2,1)} custom-call(s32[1]{0:T(128)} %bitcast.place, bf16[2,1024,256]{2,1,0:T(8,128)(2,1)S(1)} %get-tuple-element.61.keep_ref, bf16[2,1024,256]{2,1,0:T(8,128)(2,1)S(1)} %get-tuple-element.62.send_ref, bf16[8,128,256]{2,1,0:T(8,128)(2,1)S(1)} %get-tuple-element.63.dec_ref, ...), custom_call_target="tpu_custom_call", output_to_operand_aliasing={{}: (8, {})} | custom-call | flops 536870912 | bytes 4194304 | tf_op jit(solution)/shard_map/pallas_call | solution.py:59
  (118 shorter events, 5.1 us)
Async XLA Ops:
  2.7 7.4 %collective-permute-start.2 = (bf16[1,512,256]{2,1,0:T(8,128)(2,1)S(1)}, bf16[1,512,256]{2,1,0:T(8,128)(2,1)S(1)}, u32[]{:S(2)}, u32[]{:S(2)}) collective-permute-start(bf16[1,512,256]{2,1,0:T(8,128)(2,1)S(1)} %get-tuple-element.56), channel_id=1, source_target_pairs={{0,1},{1,0},{2,3},{3,2},{4,5},{5,4},{6,7},{7,6},{8,9},{9,8},{10,11... | collective-permute-start | bytes 786440 | tf_op jit(solution)/shard_map/ppermute | solution.py:27
  5.3 9.1 %collective-permute-start.1 = (bf16[1,512,256]{2,1,0:T(8,128)(2,1)S(1)}, bf16[1,512,256]{2,1,0:T(8,128)(2,1)}, u32[]{:S(2)}, u32[]{:S(2)}) collective-permute-start(bf16[1,512,256]{2,1,0:T(8,128)(2,1)S(1)} %get-tuple-element.54), channel_id=1, source_target_pairs={{0,1},{1,0},{2,3},{3,2},{4,5},{5,4},{6,7},{7,6},{8,9},{9,8},{10,11... | collective-permute-start | bytes 786440 | tf_op jit(solution)/shard_map/ppermute | solution.py:27
  7.4 8.0 %collective-permute-start = (bf16[2,512,256]{2,1,0:T(8,128)(2,1)S(1)}, bf16[2,512,256]{2,1,0:T(8,128)(2,1)S(1)}, u32[]{:S(2)}, u32[]{:S(2)}) collective-permute-start(bf16[2,512,256]{2,1,0:T(8,128)(2,1)S(1)} %first.5), channel_id=1, source_target_pairs={{0,1},{1,0},{2,3},{3,2},{4,5},{5,4},{6,7},{7,6},{8,9},{9,8},{10,11... | collective-permute-start | bytes 1572872 | tf_op jit(solution)/shard_map/ppermute | solution.py:27
  10.8 16.6 %collective-permute-start.3 = (bf16[512,256]{1,0:T(8,128)(2,1)}, bf16[512,256]{1,0:T(8,128)(2,1)S(1)}, u32[]{:S(2)}, u32[]{:S(2)}) collective-permute-start(bf16[512,256]{1,0:T(8,128)(2,1)} %fusion.2), channel_id=1, source_target_pairs={{0,4},{1,5},{2,6},{3,7},{4,0},{5,1},{6,2},{7,3},{8,12},{9,13},{10,... | collective-permute-start | bytes 786440 | tf_op jit(solution)/shard_map/ppermute | solution.py:27
  15.4 5.1 %copy-start.4 = (bf16[128,256]{1,0:T(8,128)(2,1)S(1)}, bf16[128,256]{1,0:T(8,128)(2,1)}, u32[]{:S(2)}) copy-start(bf16[128,256]{1,0:T(8,128)(2,1)} %constant.21.clone.cols_ref) | copy-start | bytes 196612
  17.4 7.3 %copy-start.1 = (bf16[2,512,1024]{2,1,0:T(8,128)(2,1)S(1)}, bf16[2,512,1024]{2,1,0:T(8,128)(2,1)}, u32[]{:S(2)}) copy-start(bf16[2,512,1024]{2,1,0:T(8,128)(2,1)} %x_ref.23) | copy-start | bytes 6291460
  18.7 18.7 %collective-permute-start.4 = (bf16[512,256]{1,0:T(8,128)(2,1)}, bf16[512,256]{1,0:T(8,128)(2,1)S(1)}, u32[]{:S(2)}, u32[]{:S(2)}) collective-permute-start(bf16[512,256]{1,0:T(8,128)(2,1)} %get-tuple-element.57), channel_id=1, source_target_pairs={{0,2},{1,3},{2,0},{3,1},{4,6},{5,7},{6,4},{7,5},{8,10},{9,11},{10,... | collective-permute-start | bytes 786440 | tf_op jit(solution)/shard_map/ppermute | solution.py:27
  20.3 17.1 %collective-permute-start.5 = (bf16[512,256]{1,0:T(8,128)(2,1)}, bf16[512,256]{1,0:T(8,128)(2,1)S(1)}, u32[]{:S(2)}, u32[]{:S(2)}) collective-permute-start(bf16[512,256]{1,0:T(8,128)(2,1)} %get-tuple-element.58), channel_id=1, source_target_pairs={{0,6},{1,7},{2,4},{3,5},{4,2},{5,3},{6,0},{7,1},{8,14},{9,15},{10,... | collective-permute-start | bytes 786440 | tf_op jit(solution)/shard_map/ppermute | solution.py:27
  20.5 0.8 copy-start.5
  24.7 12.7 %copy-start.3 = (bf16[2,512,256]{2,1,0:T(8,128)(2,1)S(1)}, bf16[2,512,256]{2,1,0:T(8,128)(2,1)}, u32[]{:S(2)}) copy-start(bf16[2,512,256]{2,1,0:T(8,128)(2,1)} %goal_ref.3) | copy-start | bytes 1572868
  37.5 22.0 %collective-permute-start.14 = (bf16[512,256]{1,0:T(8,128)(2,1)S(1)}, bf16[512,256]{1,0:T(8,128)(2,1)S(1)}, u32[]{:S(2)}, u32[]{:S(2)}) collective-permute-start(bf16[512,256]{1,0:T(8,128)(2,1)S(1)} %shard_map.107.refs_0_), channel_id=1, source_target_pairs={{0,4},{1,5},{2,6},{3,7},{4,0},{5,1},{6,2},{7,3},{8,12},{9,13},{10,... | collective-permute-start | bytes 786440 | tf_op jit(solution)/shard_map/ppermute | solution.py:27
  41.4 19.9 %collective-permute-start.13 = (bf16[512,256]{1,0:T(8,128)(2,1)S(1)}, bf16[512,256]{1,0:T(8,128)(2,1)S(1)}, u32[]{:S(2)}, u32[]{:S(2)}) collective-permute-start(bf16[512,256]{1,0:T(8,128)(2,1)S(1)} %shard_map.107.refs_0_), channel_id=1, source_target_pairs={{0,1},{1,0},{2,3},{3,2},{4,5},{5,4},{6,7},{7,6},{8,9},{9,8},{10,11... | collective-permute-start | bytes 786440 | tf_op jit(solution)/shard_map/ppermute | solution.py:27
  41.4 18.2 %collective-permute-start.8 = (bf16[512,256]{1,0:T(8,128)(2,1)S(1)}, bf16[512,256]{1,0:T(8,128)(2,1)S(1)}, u32[]{:S(2)}, u32[]{:S(2)}) collective-permute-start(bf16[512,256]{1,0:T(8,128)(2,1)S(1)} %shard_map.107.refs_0_), channel_id=1, source_target_pairs={{0,6},{1,7},{2,4},{3,5},{4,2},{5,3},{6,0},{7,1},{8,14},{9,15},{10,... | collective-permute-start | bytes 786440 | tf_op jit(solution)/shard_map/ppermute | solution.py:27
  41.9 19.3 %collective-permute-start.6 = (bf16[512,256]{1,0:T(8,128)(2,1)S(1)}, bf16[512,256]{1,0:T(8,128)(2,1)S(1)}, u32[]{:S(2)}, u32[]{:S(2)}) collective-permute-start(bf16[512,256]{1,0:T(8,128)(2,1)S(1)} %shard_map.107.refs_0_), channel_id=1, source_target_pairs={{0,2},{1,3},{2,0},{3,1},{4,6},{5,7},{6,4},{7,5},{8,10},{9,11},{10,... | collective-permute-start | bytes 786440 | tf_op jit(solution)/shard_map/ppermute | solution.py:27
  42.1 3.4 %copy-start.2 = (f32[1,1024,2048]{2,1,0:T(8,128)S(1)}, f32[1,1024,2048]{2,1,0:T(8,128)}, u32[]{:S(2)}) copy-start(f32[1,1024,2048]{2,1,0:T(8,128)} %m_ref.3) | copy-start | bytes 25165828
  59.5 2.0 %collective-permute-start.15 = (bf16[512,256]{1,0:T(8,128)(2,1)S(1)}, bf16[512,256]{1,0:T(8,128)(2,1)S(1)}, u32[]{:S(2)}, u32[]{:S(2)}) collective-permute-start(bf16[512,256]{1,0:T(8,128)(2,1)S(1)} %collective-permute-done.14.refs_0_), channel_id=1, source_target_pairs={{0,1},{1,0},{2,3},{3,2},{4,5},{5,4},{6,7},{7,6},{8,9},{9,8},{10,11... | collective-permute-start | bytes 786440 | tf_op jit(solution)/shard_map/ppermute | solution.py:27
  59.5 6.0 %collective-permute-start.9 = (bf16[512,256]{1,0:T(8,128)(2,1)S(1)}, bf16[512,256]{1,0:T(8,128)(2,1)S(1)}, u32[]{:S(2)}, u32[]{:S(2)}) collective-permute-start(bf16[512,256]{1,0:T(8,128)(2,1)S(1)} %collective-permute-done.8.refs_0_), channel_id=1, source_target_pairs={{0,1},{1,0},{2,3},{3,2},{4,5},{5,4},{6,7},{7,6},{8,9},{9,8},{10,11... | collective-permute-start | bytes 786440 | tf_op jit(solution)/shard_map/ppermute | solution.py:27
  61.2 4.1 %collective-permute-start.7 = (bf16[512,256]{1,0:T(8,128)(2,1)S(1)}, bf16[512,256]{1,0:T(8,128)(2,1)S(1)}, u32[]{:S(2)}, u32[]{:S(2)}) collective-permute-start(bf16[512,256]{1,0:T(8,128)(2,1)S(1)} %collective-permute-done.6.refs_0_), channel_id=1, source_target_pairs={{0,1},{1,0},{2,3},{3,2},{4,5},{5,4},{6,7},{7,6},{8,9},{9,8},{10,11... | collective-permute-start | bytes 786440 | tf_op jit(solution)/shard_map/ppermute | solution.py:27
  61.8 7.8 %copy-start = (bf16[1024,2048]{1,0:T(8,128)(2,1)S(1)}, bf16[1024,2048]{1,0:T(8,128)(2,1)}, u32[]{:S(2)}) copy-start(bf16[1024,2048]{1,0:T(8,128)(2,1)} %w_ref.19) | copy-start | bytes 12582916
  61.8 7.1 %collective-permute-start.18 = (bf16[4,32,128]{2,1,0:T(8,128)(2,1)S(1)}, bf16[4,32,128]{2,1,0:T(8,128)(2,1)S(1)}, u32[]{:S(2)}, u32[]{:S(2)}) collective-permute-start(bf16[4,32,128]{2,1,0:T(8,128)(2,1)S(1)} %constant_dynamic-update-slice_fusion.2.refs_0_), channel_id=1, source_target_pairs={{0,24},{8,16},{16,8},{24,0},{1,25},{9,17},{17,9},{25,1},{2,26},{10... | collective-permute-start | bytes 98312 | tf_op jit(solution)/shard_map/ppermute | solution.py:27
  64.3 5.2 %collective-permute-start.17 = (bf16[4,32,128]{2,1,0:T(8,128)(2,1)S(1)}, bf16[4,32,128]{2,1,0:T(8,128)(2,1)S(1)}, u32[]{:S(2)}, u32[]{:S(2)}) collective-permute-start(bf16[4,32,128]{2,1,0:T(8,128)(2,1)S(1)} %constant_dynamic-update-slice_fusion.2.refs_0_), channel_id=1, source_target_pairs={{0,16},{8,24},{16,0},{24,8},{1,17},{9,25},{17,1},{25,9},{2,18},{10... | collective-permute-start | bytes 98312 | tf_op jit(solution)/shard_map/ppermute | solution.py:27
  64.8 4.8 %collective-permute-start.16 = (bf16[4,32,128]{2,1,0:T(8,128)(2,1)S(1)}, bf16[4,32,128]{2,1,0:T(8,128)(2,1)S(1)}, u32[]{:S(2)}, u32[]{:S(2)}) collective-permute-start(bf16[4,32,128]{2,1,0:T(8,128)(2,1)S(1)} %constant_dynamic-update-slice_fusion.2.refs_0_), channel_id=1, source_target_pairs={{0,8},{8,0},{16,24},{24,16},{1,9},{9,1},{17,25},{25,17},{2,10},{10... | collective-permute-start | bytes 98312 | tf_op jit(solution)/shard_map/ppermute | solution.py:27
  65.8 5.0 %collective-permute-start.12 = (bf16[4,32,128]{2,1,0:T(8,128)(2,1)S(1)}, bf16[4,32,128]{2,1,0:T(8,128)(2,1)S(1)}, u32[]{:S(2)}, u32[]{:S(2)}) collective-permute-start(bf16[4,32,128]{2,1,0:T(8,128)(2,1)S(1)} %constant_dynamic-update-slice_fusion.refs_0_), channel_id=1, source_target_pairs={{0,24},{8,16},{16,8},{24,0},{1,25},{9,17},{17,9},{25,1},{2,26},{10... | collective-permute-start | bytes 98312 | tf_op jit(solution)/shard_map/ppermute | solution.py:27
  68.3 3.9 %collective-permute-start.11 = (bf16[4,32,128]{2,1,0:T(8,128)(2,1)S(1)}, bf16[4,32,128]{2,1,0:T(8,128)(2,1)S(1)}, u32[]{:S(2)}, u32[]{:S(2)}) collective-permute-start(bf16[4,32,128]{2,1,0:T(8,128)(2,1)S(1)} %constant_dynamic-update-slice_fusion.refs_0_), channel_id=1, source_target_pairs={{0,16},{8,24},{16,0},{24,8},{1,17},{9,25},{17,1},{25,9},{2,18},{10... | collective-permute-start | bytes 98312 | tf_op jit(solution)/shard_map/ppermute | solution.py:27
  68.9 4.0 %collective-permute-start.10 = (bf16[4,32,128]{2,1,0:T(8,128)(2,1)S(1)}, bf16[4,32,128]{2,1,0:T(8,128)(2,1)S(1)}, u32[]{:S(2)}, u32[]{:S(2)}) collective-permute-start(bf16[4,32,128]{2,1,0:T(8,128)(2,1)S(1)} %constant_dynamic-update-slice_fusion.refs_0_), channel_id=1, source_target_pairs={{0,8},{8,0},{16,24},{24,16},{1,9},{9,1},{17,25},{25,17},{2,10},{10... | collective-permute-start | bytes 98312 | tf_op jit(solution)/shard_map/ppermute | solution.py:27
  70.4 8.7 %collective-permute-start.20 = (bf16[1,512,256]{2,1,0:T(8,128)(2,1)S(1)}, bf16[1,512,256]{2,1,0:T(8,128)(2,1)S(1)}, u32[]{:S(2)}, u32[]{:S(2)}) collective-permute-start(bf16[1,512,256]{2,1,0:T(8,128)(2,1)S(1)} %get-tuple-element.78), channel_id=1, source_target_pairs={{0,1},{1,0},{2,3},{3,2},{4,5},{5,4},{6,7},{7,6},{8,9},{9,8},{10,11... | collective-permute-start | bytes 786440 | tf_op jit(solution)/shard_map/ppermute | solution.py:27
  74.8 8.2 %collective-permute-start.22 = (bf16[2,512,256]{2,1,0:T(8,128)(2,1)S(1)}, bf16[2,512,256]{2,1,0:T(8,128)(2,1)S(1)}, u32[]{:S(2)}, u32[]{:S(2)}) collective-permute-start(bf16[2,512,256]{2,1,0:T(8,128)(2,1)S(1)} %get-tuple-element.80), channel_id=1, source_target_pairs={{0,1},{1,0},{2,3},{3,2},{4,5},{5,4},{6,7},{7,6},{8,9},{9,8},{10,11... | collective-permute-start | bytes 1572872 | tf_op jit(solution)/shard_map/ppermute | solution.py:27
  75.7 11.5 %collective-permute-start.19 = (bf16[1,512,256]{2,1,0:T(8,128)(2,1)S(1)}, bf16[1,512,256]{2,1,0:T(8,128)(2,1)S(1)}, u32[]{:S(2)}, u32[]{:S(2)}) collective-permute-start(bf16[1,512,256]{2,1,0:T(8,128)(2,1)S(1)} %get-tuple-element.76), channel_id=1, source_target_pairs={{0,1},{1,0},{2,3},{3,2},{4,5},{5,4},{6,7},{7,6},{8,9},{9,8},{10,11... | collective-permute-start | bytes 786440 | tf_op jit(solution)/shard_map/ppermute | solution.py:27
  77.1 32.6 %slice-start = ((s8[8388608]{0:T(1024)(128)(4,1)}), s8[4194304]{0:T(1024)(128)(4,1)S(1)}, s32[]{:S(2)}) async-start(s8[8388608]{0:T(1024)(128)(4,1)} %bitcast.67), calls=%async_computation | async-start | bytes 8388608
  79.1 22.3 %collective-permute-start.21 = (bf16[512,256]{1,0:T(8,128)(2,1)S(1)}, bf16[512,256]{1,0:T(8,128)(2,1)S(1)}, u32[]{:S(2)}, u32[]{:S(2)}) collective-permute-start(bf16[512,256]{1,0:T(8,128)(2,1)S(1)} %fusion.3), channel_id=1, source_target_pairs={{0,4},{1,5},{2,6},{3,7},{4,0},{5,1},{6,2},{7,3},{8,12},{9,13},{10,... | collective-permute-start | bytes 786440 | tf_op jit(solution)/shard_map/ppermute | solution.py:27
  83.1 18.3 %collective-permute-start.24 = (bf16[512,256]{1,0:T(8,128)(2,1)S(1)}, bf16[512,256]{1,0:T(8,128)(2,1)S(1)}, u32[]{:S(2)}, u32[]{:S(2)}) collective-permute-start(bf16[512,256]{1,0:T(8,128)(2,1)S(1)} %get-tuple-element.96), channel_id=1, source_target_pairs={{0,6},{1,7},{2,4},{3,5},{4,2},{5,3},{6,0},{7,1},{8,14},{9,15},{10,... | collective-permute-start | bytes 786440 | tf_op jit(solution)/shard_map/ppermute | solution.py:27
  86.4 23.2 %slice-start.1 = ((s8[8388608]{0:T(1024)(128)(4,1)}), s8[4194304]{0:T(1024)(128)(4,1)S(1)}, s32[]{:S(2)}) async-start(s8[8388608]{0:T(1024)(128)(4,1)} %bitcast.67), calls=%async_computation.1 | async-start | bytes 8388608
  86.4 15.9 %collective-permute-start.23 = (bf16[512,256]{1,0:T(8,128)(2,1)S(1)}, bf16[512,256]{1,0:T(8,128)(2,1)S(1)}, u32[]{:S(2)}, u32[]{:S(2)}) collective-permute-start(bf16[512,256]{1,0:T(8,128)(2,1)S(1)} %get-tuple-element.97), channel_id=1, source_target_pairs={{0,2},{1,3},{2,0},{3,1},{4,6},{5,7},{6,4},{7,5},{8,10},{9,11},{10,... | collective-permute-start | bytes 786440 | tf_op jit(solution)/shard_map/ppermute | solution.py:27
  102.4 24.2 %collective-permute-start.33 = (bf16[512,256]{1,0:T(8,128)(2,1)S(1)}, bf16[512,256]{1,0:T(8,128)(2,1)S(1)}, u32[]{:S(2)}, u32[]{:S(2)}) collective-permute-start(bf16[512,256]{1,0:T(8,128)(2,1)S(1)} %shard_map.121.refs_0_), channel_id=1, source_target_pairs={{0,4},{1,5},{2,6},{3,7},{4,0},{5,1},{6,2},{7,3},{8,12},{9,13},{10,... | collective-permute-start | bytes 786440 | tf_op jit(solution)/shard_map/ppermute | solution.py:27
  108.9 20.0 %collective-permute-start.32 = (bf16[512,256]{1,0:T(8,128)(2,1)S(1)}, bf16[512,256]{1,0:T(8,128)(2,1)S(1)}, u32[]{:S(2)}, u32[]{:S(2)}) collective-permute-start(bf16[512,256]{1,0:T(8,128)(2,1)S(1)} %shard_map.121.refs_0_), channel_id=1, source_target_pairs={{0,1},{1,0},{2,3},{3,2},{4,5},{5,4},{6,7},{7,6},{8,9},{9,8},{10,11... | collective-permute-start | bytes 786440 | tf_op jit(solution)/shard_map/ppermute | solution.py:27
  108.9 17.7 %collective-permute-start.27 = (bf16[512,256]{1,0:T(8,128)(2,1)S(1)}, bf16[512,256]{1,0:T(8,128)(2,1)S(1)}, u32[]{:S(2)}, u32[]{:S(2)}) collective-permute-start(bf16[512,256]{1,0:T(8,128)(2,1)S(1)} %shard_map.121.refs_0_), channel_id=1, source_target_pairs={{0,6},{1,7},{2,4},{3,5},{4,2},{5,3},{6,0},{7,1},{8,14},{9,15},{10,... | collective-permute-start | bytes 786440 | tf_op jit(solution)/shard_map/ppermute | solution.py:27
  109.5 19.4 %collective-permute-start.25 = (bf16[512,256]{1,0:T(8,128)(2,1)S(1)}, bf16[512,256]{1,0:T(8,128)(2,1)S(1)}, u32[]{:S(2)}, u32[]{:S(2)}) collective-permute-start(bf16[512,256]{1,0:T(8,128)(2,1)S(1)} %shard_map.121.refs_0_), channel_id=1, source_target_pairs={{0,2},{1,3},{2,0},{3,1},{4,6},{5,7},{6,4},{7,5},{8,10},{9,11},{10,... | collective-permute-start | bytes 786440 | tf_op jit(solution)/shard_map/ppermute | solution.py:27
  126.6 7.4 %collective-permute-start.34 = (bf16[512,256]{1,0:T(8,128)(2,1)S(1)}, bf16[512,256]{1,0:T(8,128)(2,1)S(1)}, u32[]{:S(2)}, u32[]{:S(2)}) collective-permute-start(bf16[512,256]{1,0:T(8,128)(2,1)S(1)} %collective-permute-done.33.refs_0_), channel_id=1, source_target_pairs={{0,1},{1,0},{2,3},{3,2},{4,5},{5,4},{6,7},{7,6},{8,9},{9,8},{10,11... | collective-permute-start | bytes 786440 | tf_op jit(solution)/shard_map/ppermute | solution.py:27
  126.6 4.8 %collective-permute-start.28 = (bf16[512,256]{1,0:T(8,128)(2,1)S(1)}, bf16[512,256]{1,0:T(8,128)(2,1)S(1)}, u32[]{:S(2)}, u32[]{:S(2)}) collective-permute-start(bf16[512,256]{1,0:T(8,128)(2,1)S(1)} %collective-permute-done.27.refs_0_), channel_id=1, source_target_pairs={{0,1},{1,0},{2,3},{3,2},{4,5},{5,4},{6,7},{7,6},{8,9},{9,8},{10,11... | collective-permute-start | bytes 786440 | tf_op jit(solution)/shard_map/ppermute | solution.py:27
  128.9 2.8 %collective-permute-start.26 = (bf16[512,256]{1,0:T(8,128)(2,1)S(1)}, bf16[512,256]{1,0:T(8,128)(2,1)S(1)}, u32[]{:S(2)}, u32[]{:S(2)}) collective-permute-start(bf16[512,256]{1,0:T(8,128)(2,1)S(1)} %collective-permute-done.25.refs_0_), channel_id=1, source_target_pairs={{0,1},{1,0},{2,3},{3,2},{4,5},{5,4},{6,7},{7,6},{8,9},{9,8},{10,11... | collective-permute-start | bytes 786440 | tf_op jit(solution)/shard_map/ppermute | solution.py:27
  131.9 16.6 %collective-permute-start.31 = (bf16[4,32,128]{2,1,0:T(8,128)(2,1)S(1)}, bf16[4,32,128]{2,1,0:T(8,128)(2,1)S(1)}, u32[]{:S(2)}, u32[]{:S(2)}) collective-permute-start(bf16[4,32,128]{2,1,0:T(8,128)(2,1)S(1)} %constant_dynamic-update-slice_fusion.4.refs_0_), channel_id=1, source_target_pairs={{0,24},{8,16},{16,8},{24,0},{1,25},{9,17},{17,9},{25,1},{2,26},{10... | collective-permute-start | bytes 98312 | tf_op jit(solution)/shard_map/ppermute | solution.py:27
  133.5 15.0 %collective-permute-start.30 = (bf16[4,32,128]{2,1,0:T(8,128)(2,1)S(1)}, bf16[4,32,128]{2,1,0:T(8,128)(2,1)S(1)}, u32[]{:S(2)}, u32[]{:S(2)}) collective-permute-start(bf16[4,32,128]{2,1,0:T(8,128)(2,1)S(1)} %constant_dynamic-update-slice_fusion.4.refs_0_), channel_id=1, source_target_pairs={{0,16},{8,24},{16,0},{24,8},{1,17},{9,25},{17,1},{25,9},{2,18},{10... | collective-permute-start | bytes 98312 | tf_op jit(solution)/shard_map/ppermute | solution.py:27
  134.2 9.8 %collective-permute-start.37 = (bf16[4,32,128]{2,1,0:T(8,128)(2,1)S(1)}, bf16[4,32,128]{2,1,0:T(8,128)(2,1)S(1)}, u32[]{:S(2)}, u32[]{:S(2)}) collective-permute-start(bf16[4,32,128]{2,1,0:T(8,128)(2,1)S(1)} %constant_dynamic-update-slice_fusion.6.refs_0_), channel_id=1, source_target_pairs={{0,24},{8,16},{16,8},{24,0},{1,25},{9,17},{17,9},{25,1},{2,26},{10... | collective-permute-start | bytes 98312 | tf_op jit(solution)/shard_map/ppermute | solution.py:27
  136.8 8.8 %collective-permute-start.36 = (bf16[4,32,128]{2,1,0:T(8,128)(2,1)S(1)}, bf16[4,32,128]{2,1,0:T(8,128)(2,1)S(1)}, u32[]{:S(2)}, u32[]{:S(2)}) collective-permute-start(bf16[4,32,128]{2,1,0:T(8,128)(2,1)S(1)} %constant_dynamic-update-slice_fusion.6.refs_0_), channel_id=1, source_target_pairs={{0,16},{8,24},{16,0},{24,8},{1,17},{9,25},{17,1},{25,9},{2,18},{10... | collective-permute-start | bytes 98312 | tf_op jit(solution)/shard_map/ppermute | solution.py:27
  137.3 8.3 %collective-permute-start.35 = (bf16[4,32,128]{2,1,0:T(8,128)(2,1)S(1)}, bf16[4,32,128]{2,1,0:T(8,128)(2,1)S(1)}, u32[]{:S(2)}, u32[]{:S(2)}) collective-permute-start(bf16[4,32,128]{2,1,0:T(8,128)(2,1)S(1)} %constant_dynamic-update-slice_fusion.6.refs_0_), channel_id=1, source_target_pairs={{0,8},{8,0},{16,24},{24,16},{1,9},{9,1},{17,25},{25,17},{2,10},{10... | collective-permute-start | bytes 98312 | tf_op jit(solution)/shard_map/ppermute | solution.py:27
  144.0 4.5 %collective-permute-start.29 = (bf16[4,32,128]{2,1,0:T(8,128)(2,1)S(1)}, bf16[4,32,128]{2,1,0:T(8,128)(2,1)S(1)}, u32[]{:S(2)}, u32[]{:S(2)}) collective-permute-start(bf16[4,32,128]{2,1,0:T(8,128)(2,1)S(1)} %constant_dynamic-update-slice_fusion.4.refs_0_), channel_id=1, source_target_pairs={{0,8},{8,0},{16,24},{24,16},{1,9},{9,1},{17,25},{25,17},{2,10},{10... | collective-permute-start | bytes 98312 | tf_op jit(solution)/shard_map/ppermute | solution.py:27
